TPU v7x, 128 devices: a whole 4x4x4 slice. The times are simulated.
128 devices in a mesh: tok: 16 (over z, x_hi, core), req: 8 (over x_lo, y).
Axes of the slice: x: 4 (x_hi: 2, x_lo: 2; x = x_hi * 2 + x_lo), y: 4, z: 4, core: 2. Of those that a mesh axis runs over, the one named last changes fastest.
Arguments:
- query_rows: bfloat16 [8, 4096, 7168], P('req', 'tok'), may hold values from -16 to 16
- key_rows: bfloat16 [8, 4096, 7168], P('req', 'tok'), may hold values from -16 to 16
- value_rows: bfloat16 [8, 4096, 7168], P('req', 'tok'), may hold values from -6 to 6
- lengths: int32 [8, 6], P('req'), may hold values from 1 to 2048, 4096 in all within a row
- cache_blocks: bfloat16 [8, 128, 2, 32, 3584], P('req', 'tok'), may hold values from -6 to 6
- destinations: int32 [8, 128, 1], P('req', 'tok'), may hold values from 0 to 7; in each aligned block of 8 rows (0 to 7, 8 to 15, ..., all dimensions but the last counted through in order) at most 2 rows name the same one
Outputs:
- attended: bfloat16 [8, 4096, 7168], P('req', 'tok')
- moved_cache: bfloat16 [8, 8, 2, 2, 16, 32, 3584], P('req', None, None, None, None, 'tok')
Inputs may be any that keep to these rules, and one draw needn't show every extreme that they name: The 6 lengths of each span sum to 4096, and the longest of every span is exactly 2048. `destinations`: of the 8 rows of one device (aligned blocks of 8 rows), at most 2 name the same group, and in every draw some device names one group exactly 2 times.
All inputs are finite; a program needn't handle non-finite values.
Results may differ from a plain program's by a relative error of at most 0.0037.
Values may be sent and summed in bfloat16 or wider, within the bound.
A program may use at most 192 MiB of HBM per device.

v0:
```python
import jax
import jax.numpy as jnp
from jax import lax
from jax.sharding import PartitionSpec as P

HD = 224
CAP = 2


def segment_ids(lengths_row, span_length):
    ends = jnp.cumsum(lengths_row)
    positions = jnp.arange(span_length, dtype=jnp.int32)
    return jnp.sum((positions[:, None] >= ends[None, :]).astype(jnp.int32), axis=1)


def attend_item(query_all, key_all, value_all, segments):
    length = query_all.shape[0]
    heads_here = query_all.shape[1] // HD
    positions = jnp.arange(length, dtype=jnp.int32)
    block_rows = min(512, length)
    results = []
    for block_start in range(0, length, block_rows):
        block_end = block_start + block_rows
        visible = (segments[block_start:block_end, None] == segments[None, :block_end]) & (
            positions[block_start:block_end, None] >= positions[None, :block_end]
        )
        head_results = []
        for head in range(heads_here):
            low = head * HD
            high = low + HD
            query_block = query_all[block_start:block_end, low:high]
            key_block = key_all[:block_end, low:high]
            value_block = value_all[:block_end, low:high]
            scores = lax.dot_general(
                query_block, key_block, (((1,), (1,)), ((), ())), preferred_element_type=jnp.float32
            ) * HD ** (-0.5)
            scores = jnp.where(visible, scores, -1e30)
            row_max = jnp.max(scores, axis=1, keepdims=True)
            weights = jnp.where(visible, jnp.exp(scores - row_max), 0.0)
            row_total = jnp.sum(weights, axis=1, keepdims=True)
            summed = jnp.dot(
                weights.astype(jnp.bfloat16), value_block, preferred_element_type=jnp.float32
            )
            head_results.append((summed / row_total).astype(jnp.bfloat16))
        results.append(jnp.concatenate(head_results, axis=1))
    return jnp.concatenate(results, axis=0)


def attend_heads(parts, segments):
    query_part, key_part, value_part = parts
    length = query_part.shape[0]
    item_count = query_part.shape[2]
    outputs = [attend_item(query_part[:, 0, 0], key_part[:, 0, 0], value_part[:, 0, 0], segments)]
    return jnp.stack(outputs, axis=1).reshape(length, 1, item_count, query_part.shape[3])


def regroup_attend(query_rows, key_rows, value_rows, segments):
    tok_count = lax.axis_size("tok")
    token_rows = query_rows.shape[1]
    feature_width = query_rows.shape[2]
    group_width = feature_width // tok_count

    def by_group(rows_in):
        return rows_in[0].reshape(token_rows, tok_count, 1, group_width)

    mixed = attend_heads(
        (
            lax.all_to_all(by_group(query_rows), "tok", split_axis=1, concat_axis=0, tiled=True),
            lax.all_to_all(by_group(key_rows), "tok", split_axis=1, concat_axis=0, tiled=True),
            lax.all_to_all(by_group(value_rows), "tok", split_axis=1, concat_axis=0, tiled=True),
        ),
        segments=segments,
    )
    returned = lax.all_to_all(mixed, "tok", split_axis=0, concat_axis=1, tiled=True)
    return returned.reshape(1, token_rows, feature_width)


def relocate(cache_blocks, destinations):
    groups = lax.axis_size("req")
    tok_count = lax.axis_size("tok")
    targets = destinations[0, :, 0]
    block_count = targets.shape[0]
    positions = jnp.arange(block_count, dtype=jnp.int32)
    earlier = (targets[:, None] == targets[None, :]) & (positions[None, :] < positions[:, None])
    slot_rank = jnp.sum(earlier.astype(jnp.int32), axis=1)
    group_ids = jnp.arange(groups, dtype=jnp.int32)
    slot_ids = jnp.arange(CAP, dtype=jnp.int32)
    placing = (
        (targets[:, None, None] == group_ids[None, :, None])
        & (slot_rank[:, None, None] == slot_ids[None, None, :])
    ).astype(cache_blocks.dtype)
    local_blocks = cache_blocks[0]
    heads_all = local_blocks.shape[2]
    local_blocks = local_blocks.reshape(
        block_count, 2, tok_count, heads_all // tok_count, local_blocks.shape[3]
    )
    outgoing = jnp.einsum(
        "bdc,bjthy->dcjthy", placing, local_blocks, preferred_element_type=jnp.float32
    ).astype(jnp.bfloat16)
    arrived = lax.all_to_all(
        lax.all_to_all(outgoing, "tok", split_axis=3, concat_axis=3, tiled=True),
        "req",
        split_axis=0,
        concat_axis=0,
        tiled=True,
    )
    return arrived[None]


def on_device(query_rows, key_rows, value_rows, lengths, cache_blocks, destinations):
    span_length = query_rows.shape[1] * lax.axis_size("tok")
    segments = segment_ids(lengths[0], span_length)
    attended = regroup_attend(query_rows, key_rows, value_rows, segments)
    moved_cache = relocate(cache_blocks, destinations)
    return (attended, moved_cache)


def solution(mesh):
    return jax.shard_map(
        on_device,
        mesh=mesh,
        in_specs=(
            P("req", "tok", None),
            P("req", "tok", None),
            P("req", "tok", None),
            P("req", None),
            P("req", "tok", None, None, None),
            P("req", "tok", None),
        ),
        out_specs=(P("req", "tok", None), P("req", None, None, None, None, "tok", None)),
        check_vma=False,
    )
```

profile of v0, /device:TPU:1, one launch (start us, length us, event | category | flops | bytes accessed | tf_op | source)
XLA Modules:
  0.0 419.9 jit_solution(5922651007471697967)
XLA Ops:
  0.6 5.9 %copy.54 = bf16[1,256,7168]{1,2,0:T(8,128)(2,1)} copy(bf16[1,256,7168]{2,1,0:T(8,128)(2,1)} %param.7) | data formatting | bytes 7340032 | tf_op args[1]
  6.5 9.3 %all-to-all-start.1 = ((bf16[256,16,1,448]{0,3,2,1:T(8,128)(2,1)}), bf16[256,16,1,448]{0,3,2,1:T(8,128)(2,1)}, u32[]{:S(2)}, u32[]{:S(2)}) async-start(bf16[256,16,1,448]{0,3,2,1:T(8,128)(2,1)} %bitcast.60), calls=%async_computation.1 | async-start | bytes 7340032 | tf_op jit(solution)/shard_map/all_to_all | solution.py:69
  15.8 5.9 %copy.51 = bf16[1,256,7168]{1,2,0:T(8,128)(2,1)} copy(bf16[1,256,7168]{2,1,0:T(8,128)(2,1)} %param.6) | data formatting | bytes 7340032 | tf_op args[0]
  21.7 39.6 %all-to-all-done.1 = bf16[256,16,1,448]{0,3,2,1:T(8,128)(2,1)} async-done(((bf16[256,16,1,448]{0,3,2,1:T(8,128)(2,1)}), bf16[256,16,1,448]{0,3,2,1:T(8,128)(2,1)}, u32[]{:S(2)}, u32[]{:S(2)}) %all-to-all-start.1) | async-done | bytes 3670048 | tf_op jit(solution)/shard_map/all_to_all | solution.py:69
  61.3 5.2 %all-to-all-start = ((bf16[256,16,1,448]{0,3,2,1:T(8,128)(2,1)}), bf16[256,16,1,448]{0,3,2,1:T(8,128)(2,1)}, u32[]{:S(2)}, u32[]{:S(2)}) async-start(bf16[256,16,1,448]{0,3,2,1:T(8,128)(2,1)} %bitcast.59), calls=%async_computation | async-start | bytes 7340032 | tf_op jit(solution)/shard_map/all_to_all | solution.py:68
  66.5 5.9 %copy.57 = bf16[1,256,7168]{1,2,0:T(8,128)(2,1)} copy(bf16[1,256,7168]{2,1,0:T(8,128)(2,1)} %param.8) | data formatting | bytes 7340032 | tf_op args[2]
  72.4 5.9 %copy.69 = bf16[1,8,2,32,3584]{4,1,3,2,0:T(8,128)(2,1)} copy(bf16[1,8,2,32,3584]{4,3,2,1,0:T(8,128)(2,1)} %param.10) | data formatting | bytes 7340032 | tf_op jit(solution)/shard_map/reshape;squeeze | solution.py:94
  78.8 7.1 %convolution_convert_fusion = bf16[8,2,2,16,2,3584]{5,0,4,3,2,1:T(8,128)(2,1)} fusion(bf16[8,2,16,2,3584,1]{4,0,3,2,1,5:T(8,128)(2,1)} %bitcast.62, pred[8,2]{0,1:T(4,128)(4,1)S(1)} %iota_compare_fusion.4, pred[8,8]{0,1:T(8,128)(4,1)S(1)} %iota_compare_fusion.3), kind=kOutput, calls=%fused_computation.6 | convolution fusion | flops 62390400 | bytes 11010128 | tf_op jit(solution)/shard_map/bdc,bjthy->dcjthy/dot_general | solution.py:97
  86.0 26.1 %all-to-all-done = bf16[256,16,1,448]{0,3,2,1:T(8,128)(2,1)} async-done(((bf16[256,16,1,448]{0,3,2,1:T(8,128)(2,1)}), bf16[256,16,1,448]{0,3,2,1:T(8,128)(2,1)}, u32[]{:S(2)}, u32[]{:S(2)}) %all-to-all-start) | async-done | bytes 3670048 | tf_op jit(solution)/shard_map/all_to_all | solution.py:68
  112.0 5.8 %all-to-all-start.2 = ((bf16[256,16,1,448]{0,3,2,1:T(8,128)(2,1)}), bf16[256,16,1,448]{0,3,2,1:T(8,128)(2,1)}, u32[]{:S(2)}, u32[]{:S(2)}) async-start(bf16[256,16,1,448]{0,3,2,1:T(8,128)(2,1)} %bitcast.58), calls=%async_computation.2 | async-start | bytes 7340032 | tf_op jit(solution)/shard_map/all_to_all | solution.py:70
  118.0 6.7 %copy.64 = bf16[8,2,2,16,2,3584]{5,0,4,2,1,3:T(8,128)(2,1)} copy(bf16[8,2,2,16,2,3584]{5,0,4,3,2,1:T(8,128)(2,1)} %convolution_convert_fusion) | data formatting | bytes 14680064 | tf_op jit(solution)/shard_map/convert_element_type | solution.py:99
  124.7 2.5 copy.73
  127.2 3.8 copy.72
  131.0 1.7 fusion.301
  132.8 1.4 fusion.302
  134.1 2.6 fusion.303
  136.8 1.1 fusion.304
  137.9 3.5 fusion.305
  141.4 3.4 fusion.306
  144.8 4.5 %fusion.307 = (f32[512]{0:T(512)S(1)}, f32[512,3584]{1,0:T(8,128)}) fusion(bf16[4096,448]{0,1:T(8,128)(2,1)S(1)} %bitcast.78, bf16[4096,448]{0,1:T(8,128)(2,1)S(1)} %bitcast.94, s32[3584]{0:T(1024)S(1)} %iota_add_fusion, s32[512]{0:T(512)S(1)} %iota_add_fusion.7, s32[3584]{0:T(1024)S(1)} %bitcast.120, s32[512]{0:T(512)S(1)} %get-tuple-element.29), kind=kOutput, calls=%fused_computation.282 | convolution fusion | flops 833093120 | bytes 9213952 | tf_op jit(solution)/shard_map/dot_general | solution.py:34
  149.3 4.5 %fusion.308 = (f32[512]{0:T(512)S(1)}, f32[512,3584]{1,0:T(8,128)}) fusion(bf16[4096,448]{0,1:T(8,128)(2,1)S(1)} %bitcast.79, bf16[4096,448]{0,1:T(8,128)(2,1)S(1)} %bitcast.95, s32[3584]{0:T(1024)S(1)} %iota_add_fusion, s32[512]{0:T(512)S(1)} %iota_add_fusion.7, s32[3584]{0:T(1024)S(1)} %bitcast.121, s32[512]{0:T(512)S(1)} %get-tuple-element.29), kind=kOutput, calls=%fused_computation.283 | convolution fusion | flops 833093120 | bytes 9213952 | tf_op jit(solution)/shard_map/dot_general | solution.py:34
  153.8 9.5 %all-to-all-done.2 = bf16[256,16,1,448]{0,3,2,1:T(8,128)(2,1)} async-done(((bf16[256,16,1,448]{0,3,2,1:T(8,128)(2,1)}), bf16[256,16,1,448]{0,3,2,1:T(8,128)(2,1)}, u32[]{:S(2)}, u32[]{:S(2)}) %all-to-all-start.2) | async-done | bytes 3670048 | tf_op jit(solution)/shard_map/all_to_all | solution.py:70
  163.3 5.6 %all-to-all-start.4 = ((bf16[8,2,2,16,2,3584]{5,0,4,2,1,3:T(8,128)(2,1)}), bf16[8,2,2,16,2,3584]{5,0,4,2,1,3:T(8,128)(2,1)}, u32[]{:S(2)}, u32[]{:S(2)}) async-start(bf16[8,2,2,16,2,3584]{5,0,4,2,1,3:T(8,128)(2,1)} %copy.64), calls=%async_computation.4 | async-start | bytes 14680064 | tf_op jit(solution)/shard_map/all_to_all | solution.py:101
  169.0 2.7 copy.71
  173.0 1.1 copy-done.1
  174.1 1.1 copy-done.3
  176.0 1.4 fusion.89
  181.1 2.2 fusion.53
  183.4 1.1 fusion.180
  185.6 1.5 fusion.17
  187.0 2.4 fusion.49
  189.5 1.7 fusion.51
  191.2 1.6 fusion.212
  192.8 1.6 fusion.206
  195.4 3.6 fusion.27
  198.9 1.7 fusion.198
  200.6 1.6 fusion.188
  202.2 2.1 fusion.3
  204.3 3.4 fusion.31
  207.7 2.3 fusion.33
  210.1 2.0 fusion.126
  212.2 2.2 fusion.116
  218.3 4.5 %fusion.5 = (f32[512]{0:T(512)S(1)}, f32[512]{0:T(512)S(1)}) fusion(f32[512,3584]{1,0:T(8,128)S(1)} %bitcast.65, f32[512]{0:T(512)S(1)} %get-tuple-element.59, s32[3584]{0:T(1024)S(1)} %iota_add_fusion, s32[512]{0:T(512)S(1)} %iota_add_fusion.7, s32[3584]{0:T(1024)S(1)} %bitcast.122, s32[512]{0:T(512)S(1)} %get-tuple-element.29, ...), kind=kLoop, calls=%fused_computation.26 | loop fusion | flops 16514048 | bytes 14721024 | tf_op jit(solution)/shard_map/reduce_sum | solution.py:40
  223.6 2.2 fusion.146
  225.8 2.2 fusion.136
  228.8 2.8 fusion.1
  231.6 4.6 %fusion.9 = (f32[512]{0:T(512)S(1)}, f32[512]{0:T(512)S(1)}, f32[512,4096]{1,0:T(8,128)S(1)}) fusion(f32[512,4096]{1,0:T(8,128)S(1)} %get-tuple-element.62, f32[512]{0:T(512)S(1)} %get-tuple-element.61, s32[512]{0:T(512)S(1)} %iota_add_fusion.6, s32[4096]{0:T(1024)S(1)} %convert_reduce_fusion, s32[512]{0:T(512)S(1)} %get-tuple-element.28, ...), kind=kOutput, calls=%fused_computation.30 | convolution fusion | flops 962591744 | bytes 18868224 | tf_op jit(solution)/shard_map/dot_general | solution.py:34
  236.2 3.4 fusion.11
  239.7 3.0 fusion.166
  242.7 3.0 fusion.156
  246.9 6.2 %reduce = bf16[4096,448]{0,1:T(8,128)(2,1)} reduce(bf16[4096,1,1,448]{0,3,2,1:T(8,128)(2,1)} %bitcast.14, bf16[]{:T(256)} %broadcast.221), dimensions={1,2}, to_apply=%copy.60.reduce_sub_computation | reduce | bytes 7340034 | tf_op jit(solution)/shard_map/reshape;stack | solution.py:54
  253.1 6.3 %copy.77 = bf16[4096,448]{1,0:T(8,128)(2,1)} copy(bf16[4096,448]{0,1:T(8,128)(2,1)} %reduce) | data formatting | bytes 7340032
  259.4 12.3 %reshape.155 = bf16[16,2,57344]{2,1,0:T(2,128)(2,1)} reshape(bf16[4096,448]{1,0:T(8,128)(2,1)} %copy.77) | data formatting | bytes 7340032
  271.8 7.3 %all-to-all-start.3 = ((bf16[16,2,57344]{2,1,0:T(2,128)(2,1)}), bf16[16,2,57344]{2,1,0:T(2,128)(2,1)}, u32[]{:S(2)}, u32[]{:S(2)}) async-start(bf16[16,2,57344]{2,1,0:T(2,128)(2,1)} %reshape.155), calls=%async_computation.3 | async-start | bytes 7340032 | tf_op jit(solution)/shard_map/all_to_all | solution.py:74
  279.0 11.8 %copy.65 = bf16[8,2,2,16,2,3584]{5,4,3,2,1,0:T(2,128)(2,1)} copy(bf16[8,2,2,16,2,3584]{5,0,4,2,1,3:T(8,128)(2,1)} %all-to-all-done.4) | data formatting | bytes 14680064 | tf_op jit(solution)/shard_map/all_to_all | solution.py:101
  290.9 33.7 %all-to-all-done.3 = bf16[16,2,57344]{2,1,0:T(2,128)(2,1)} async-done(((bf16[16,2,57344]{2,1,0:T(2,128)(2,1)}), bf16[16,2,57344]{2,1,0:T(2,128)(2,1)}, u32[]{:S(2)}, u32[]{:S(2)}) %all-to-all-start.3) | async-done | bytes 3670048 | tf_op jit(solution)/shard_map/all_to_all | solution.py:74
  324.5 5.2 %all-to-all-start.5 = ((bf16[8,2,2,16,2,3584]{5,4,3,2,1,0:T(2,128)(2,1)}), bf16[8,2,2,16,2,3584]{5,4,3,2,1,0:T(2,128)(2,1)}, u32[]{:S(2)}, u32[]{:S(2)}) async-start(bf16[8,2,2,16,2,3584]{5,4,3,2,1,0:T(2,128)(2,1)} %copy.65), calls=%async_computation.5 | async-start | bytes 14680064 | tf_op jit(solution)/shard_map/all_to_all | solution.py:100
  329.7 13.2 %reshape.156 = bf16[4096,1,1,448]{3,2,1,0:T(2,128)(2,1)} reshape(bf16[16,2,57344]{2,1,0:T(2,128)(2,1)} %all-to-all-done.3) | data formatting | bytes 7340032
  342.9 6.6 %copy.70 = bf16[4096,1,1,448]{3,0,1,2:T(8,128)(2,1)} copy(bf16[4096,1,1,448]{3,2,1,0:T(2,128)(2,1)} %reshape.156) | data formatting | bytes 7340032
  349.5 7.7 %copy.68 = bf16[16,256,1,1,448]{1,0,4,3,2:T(8,128)(2,1)} copy(bf16[16,256,1,1,448]{4,1,0,3,2:T(8,128)(2,1)} %bitcast.57) | data formatting | bytes 7340032 | tf_op jit(solution)/shard_map/all_to_all | solution.py:74
  357.2 5.1 %copy.62 = bf16[256,16,1,1,448]{0,4,1,3,2:T(8,128)(2,1)} copy(bf16[256,16,1,1,448]{0,1,4,3,2:T(8,128)(2,1)} %bitcast.63) | data formatting | bytes 7340032 | tf_op jit(solution)/shard_map/all_to_all | solution.py:74
  362.3 5.9 %copy.66 = bf16[1,256,7168]{2,1,0:T(8,128)(2,1)} copy(bf16[1,256,7168]{1,2,0:T(8,128)(2,1)} %bitcast.61) | data formatting | bytes 7340032
  368.2 43.8 %all-to-all-done.5 = bf16[8,2,2,16,2,3584]{5,4,3,2,1,0:T(2,128)(2,1)} async-done(((bf16[8,2,2,16,2,3584]{5,4,3,2,1,0:T(2,128)(2,1)}), bf16[8,2,2,16,2,3584]{5,4,3,2,1,0:T(2,128)(2,1)}, u32[]{:S(2)}, u32[]{:S(2)}) %all-to-all-start.5) | async-done | bytes 7340064 | tf_op jit(solution)/shard_map/all_to_all | solution.py:100
  412.1 7.6 %copy.86 = bf16[1,8,2,2,16,2,3584]{6,5,4,3,2,1,0:T(2,128)(2,1)} copy(bf16[1,8,2,2,16,2,3584]{6,5,4,3,2,1,0:T(2,128)(2,1)} %bitcast.22) | data formatting | bytes 14680064
  (79 shorter events, 15.3 us)
Async XLA Ops:
  6.5 54.8 %all-to-all-start.1 = ((bf16[256,16,1,448]{0,3,2,1:T(8,128)(2,1)}), bf16[256,16,1,448]{0,3,2,1:T(8,128)(2,1)}, u32[]{:S(2)}, u32[]{:S(2)}) async-start(bf16[256,16,1,448]{0,3,2,1:T(8,128)(2,1)} %bitcast.60), calls=%async_computation.1 | async-start | bytes 7340032 | tf_op jit(solution)/shard_map/all_to_all | solution.py:69
  61.3 50.7 %all-to-all-start = ((bf16[256,16,1,448]{0,3,2,1:T(8,128)(2,1)}), bf16[256,16,1,448]{0,3,2,1:T(8,128)(2,1)}, u32[]{:S(2)}, u32[]{:S(2)}) async-start(bf16[256,16,1,448]{0,3,2,1:T(8,128)(2,1)} %bitcast.59), calls=%async_computation | async-start | bytes 7340032 | tf_op jit(solution)/shard_map/all_to_all | solution.py:68
  72.4 5.9 %copy-start.7 = (s32[1,6]{1,0:T(1,128)S(1)}, s32[1,6]{1,0:T(1,128)}, u32[]{:S(2)}) copy-start(s32[1,6]{1,0:T(1,128)} %param.9) | copy-start | bytes 76
  72.4 6.2 %copy-start.8 = (s32[1,8,1]{1,2,0:T(1,128)S(1)}, s32[1,8,1]{1,2,0:T(1,128)}, u32[]{:S(2)}) copy-start(s32[1,8,1]{1,2,0:T(1,128)} %param.11) | copy-start | bytes 100
  112.0 51.3 %all-to-all-start.2 = ((bf16[256,16,1,448]{0,3,2,1:T(8,128)(2,1)}), bf16[256,16,1,448]{0,3,2,1:T(8,128)(2,1)}, u32[]{:S(2)}, u32[]{:S(2)}) async-start(bf16[256,16,1,448]{0,3,2,1:T(8,128)(2,1)} %bitcast.58), calls=%async_computation.2 | async-start | bytes 7340032 | tf_op jit(solution)/shard_map/all_to_all | solution.py:70
  127.2 22.1 %copy-start = (bf16[56,8,16,256]{3,1,2,0:T(8,128)(2,1)}, bf16[56,8,16,256]{3,1,2,0:T(8,128)(2,1)S(1)}, u32[]{:S(2)}) copy-start(bf16[56,8,16,256]{3,1,2,0:T(8,128)(2,1)S(1)} %copy.73) | copy-start | bytes 11010052
  131.0 18.2 %copy-start.2 = (bf16[56,8,16,256]{3,1,2,0:T(8,128)(2,1)}, bf16[56,8,16,256]{3,1,2,0:T(8,128)(2,1)S(1)}, u32[]{:S(2)}) copy-start(bf16[56,8,16,256]{3,1,2,0:T(8,128)(2,1)S(1)} %copy.72) | copy-start | bytes 11010052
  163.3 108.5 %all-to-all-start.4 = ((bf16[8,2,2,16,2,3584]{5,0,4,2,1,3:T(8,128)(2,1)}), bf16[8,2,2,16,2,3584]{5,0,4,2,1,3:T(8,128)(2,1)}, u32[]{:S(2)}, u32[]{:S(2)}) async-start(bf16[8,2,2,16,2,3584]{5,0,4,2,1,3:T(8,128)(2,1)} %copy.64), calls=%async_computation.4 | async-start | bytes 14680064 | tf_op jit(solution)/shard_map/all_to_all | solution.py:101
  169.0 2.7 copy-start.5
  169.0 2.7 copy-start.6
  172.1 2.0 copy-start.1
  172.1 3.2 copy-start.3
  179.2 1.9 copy-start.4
  191.2 3.2 slice-start.4
  191.2 3.5 slice-start.6
  192.7 2.3 slice-start.5
  192.8 2.6 slice-start.7
  212.1 6.2 %slice-start = ((s8[7340032]{0:T(1024)(128)(4,1)}), s8[4194304]{0:T(1024)(128)(4,1)S(1)}, s32[]{:S(2)}) async-start(s8[7340032]{0:T(1024)(128)(4,1)} %bitcast.64), calls=%async_computation.6 | async-start | bytes 8388608
  212.1 6.2 %slice-start.2 = ((s8[7340032]{0:T(1024)(128)(4,1)}), s8[4194304]{0:T(1024)(128)(4,1)S(1)}, s32[]{:S(2)}) async-start(s8[7340032]{0:T(1024)(128)(4,1)} %bitcast.66), calls=%async_computation.8 | async-start | bytes 8388608
  212.1 6.2 %slice-start.1 = ((s8[7340032]{0:T(1024)(128)(4,1)}), s8[3145728]{0:T(1024)(128)(4,1)S(1)}, s32[]{:S(2)}) async-start(s8[7340032]{0:T(1024)(128)(4,1)} %bitcast.64), calls=%async_computation.7 | async-start | bytes 6291456
  212.1 6.2 %slice-start.3 = ((s8[7340032]{0:T(1024)(128)(4,1)}), s8[3145728]{0:T(1024)(128)(4,1)S(1)}, s32[]{:S(2)}) async-start(s8[7340032]{0:T(1024)(128)(4,1)} %bitcast.66), calls=%async_computation.9 | async-start | bytes 6291456
  271.8 52.8 %all-to-all-start.3 = ((bf16[16,2,57344]{2,1,0:T(2,128)(2,1)}), bf16[16,2,57344]{2,1,0:T(2,128)(2,1)}, u32[]{:S(2)}, u32[]{:S(2)}) async-start(bf16[16,2,57344]{2,1,0:T(2,128)(2,1)} %reshape.155), calls=%async_computation.3 | async-start | bytes 7340032 | tf_op jit(solution)/shard_map/all_to_all | solution.py:74
  324.5 87.5 %all-to-all-start.5 = ((bf16[8,2,2,16,2,3584]{5,4,3,2,1,0:T(2,128)(2,1)}), bf16[8,2,2,16,2,3584]{5,4,3,2,1,0:T(2,128)(2,1)}, u32[]{:S(2)}, u32[]{:S(2)}) async-start(bf16[8,2,2,16,2,3584]{5,4,3,2,1,0:T(2,128)(2,1)} %copy.65), calls=%async_computation.5 | async-start | bytes 14680064 | tf_op jit(solution)/shard_map/all_to_all | solution.py:100
where the time goes:
time: 427 us; the launch traced here: 420 us
  waiting for transfers between devices  153 us (36%)
  local copies, waits for them, and re-layouts  121 us (28%)
  matrix products  74.7 us (17%)
  starting transfers between devices  38.4 us (9%)
  other arithmetic  32.1 us (8%)
    unnamed x46, local copies, waits for them, and re-layouts  82.9 us
    all_to_all x1, waiting for transfers between devices, relocate(): lax.all_to_all(lax.all_to_all(outgoing, 'tok', split_axis=3, concat_axis=...  43.8 us
    dot_general x16, matrix products, attend_item(): lax.dot_general(query_block, key_block, (((1,), (1,)), ((), ())), preferr...  41.7 us
    all_to_all x1, waiting for transfers between devices, regroup_attend(): lax.all_to_all(by_group(key_rows), 'tok', split_axis=1, concat_axis=0, ti...  39.6 us
    all_to_all x1, waiting for transfers between devices, regroup_attend(): lax.all_to_all(mixed, 'tok', split_axis=0, concat_axis=1, tiled=True)  33.7 us
    all_to_all x1, waiting for transfers between devices, regroup_attend(): lax.all_to_all(by_group(query_rows), 'tok', split_axis=1, concat_axis=0,...  26.1 us
    dot_general x16, matrix products, attend_item(): jnp.dot(weights.astype(jnp.bfloat16), value_block, preferred_element_type...  25.8 us
    reduce_sum x8, other arithmetic, attend_item(): row_total = jnp.sum(weights, axis=1, keepdims=True)  19.1 us
  transfers between devices with their start and end apart: 6, of which 5 were waited for; matrix products, arithmetic and copies ran while one was open for 50% of the time, Pallas kernels for 0%

commit v1 on v0

v1 whole, which is shorter than its diff:
```python
import functools

import jax
import jax.numpy as jnp
from jax import lax
from jax.experimental import pallas as pl
from jax.experimental.pallas import tpu as pltpu
from jax.sharding import PartitionSpec as P

HD = 224
CAP = 2
BLOCK = 512
NEG = -1e30


def segment_ids(lengths_row, span_length):
    ends = jnp.cumsum(lengths_row)
    positions = jnp.arange(span_length, dtype=jnp.int32)
    return jnp.sum((positions[:, None] >= ends[None, :]).astype(jnp.int32), axis=1)


def attention_kernel(first_block_ref, q_ref, k_ref, v_ref, qseg_ref, kseg_ref, o_ref, m_ref, l_ref, acc_ref):
    qi = pl.program_id(0)
    rows, width = q_ref.shape
    heads_here = width // HD
    columns = lax.broadcasted_iota(jnp.int32, (1, width), 1)
    head_masks = [(columns >= h * HD) & (columns < (h + 1) * HD) for h in range(heads_here)]
    q = q_ref[...]
    zero = jnp.zeros((), q.dtype)
    queries = [jnp.where(mask, q, zero) for mask in head_masks]
    query_seg = qseg_ref[...]
    query_pos = qi * rows + lax.broadcasted_iota(jnp.int32, (rows, 1), 0)
    m_ref[...] = jnp.full(m_ref.shape, NEG, jnp.float32)
    l_ref[...] = jnp.zeros(l_ref.shape, jnp.float32)
    acc_ref[...] = jnp.zeros(acc_ref.shape, jnp.float32)
    scale = HD ** (-0.5)

    def body(kb, carry):
        start = pl.multiple_of(kb * rows, rows)
        keys = k_ref[pl.ds(start, rows), :]
        values = v_ref[pl.ds(start, rows), :]
        key_seg = kseg_ref[:, pl.ds(start, rows)]
        key_pos = start + lax.broadcasted_iota(jnp.int32, (1, rows), 1)
        visible = (query_seg == key_seg) & (query_pos >= key_pos)
        alpha_cols = jnp.zeros((rows, width), jnp.float32)
        update = jnp.zeros((rows, width), jnp.float32)
        for h in range(heads_here):
            scores = lax.dot_general(
                queries[h], keys, (((1,), (1,)), ((), ())), preferred_element_type=jnp.float32
            ) * scale
            scores = jnp.where(visible, scores, NEG)
            m_old = m_ref[h]
            m_new = jnp.maximum(m_old, jnp.max(scores, axis=1, keepdims=True))
            alpha = jnp.exp(m_old - m_new)
            weights = jnp.where(visible, jnp.exp(scores - m_new), 0.0)
            l_ref[h] = alpha * l_ref[h] + jnp.sum(weights, axis=1, keepdims=True)
            m_ref[h] = m_new
            masked_values = jnp.where(head_masks[h], values, zero)
            update = update + jnp.dot(
                weights.astype(jnp.bfloat16), masked_values, preferred_element_type=jnp.float32
            )
            alpha_cols = jnp.where(head_masks[h], alpha, alpha_cols)
        acc_ref[...] = alpha_cols * acc_ref[...] + update
        return carry

    lax.fori_loop(first_block_ref[qi], qi + 1, body, 0)
    totals = jnp.ones((rows, width), jnp.float32)
    for h in range(heads_here):
        totals = jnp.where(head_masks[h], l_ref[h], totals)
    o_ref[...] = (acc_ref[...] / totals).astype(o_ref.dtype)


def attend_local(query, key, value, segments):
    length, width = query.shape
    heads_here = width // HD
    blocks = length // BLOCK
    ends = jnp.cumsum(jnp.bincount(segments, length=8))
    starts = ends - jnp.bincount(segments, length=8)
    first_query = segments[::BLOCK]
    first_block = (starts[first_query] // BLOCK).astype(jnp.int32)
    qseg = segments.reshape(length, 1)
    kseg = segments.reshape(1, length)
    visible_pairs = length * length // 2
    cost = pl.CostEstimate(
        flops=int(8 * visible_pairs * width),
        transcendentals=int(heads_here * visible_pairs),
        bytes_accessed=int(4 * length * width * 2),
    )
    return pl.pallas_call(
        attention_kernel,
        out_shape=jax.ShapeDtypeStruct((length, width), query.dtype),
        grid_spec=pltpu.PrefetchScalarGridSpec(
            num_scalar_prefetch=1,
            grid=(blocks,),
            in_specs=[
                pl.BlockSpec((BLOCK, width), lambda i, fb: (i, 0)),
                pl.BlockSpec((length, width), lambda i, fb: (0, 0), pipeline_mode=pl.Buffered(1)),
                pl.BlockSpec((length, width), lambda i, fb: (0, 0), pipeline_mode=pl.Buffered(1)),
                pl.BlockSpec((BLOCK, 1), lambda i, fb: (i, 0)),
                pl.BlockSpec((1, length), lambda i, fb: (0, 0)),
            ],
            out_specs=pl.BlockSpec((BLOCK, width), lambda i, fb: (i, 0)),
            scratch_shapes=[
                pltpu.VMEM((heads_here, BLOCK, 1), jnp.float32),
                pltpu.VMEM((heads_here, BLOCK, 1), jnp.float32),
                pltpu.VMEM((BLOCK, width), jnp.float32),
            ],
        ),
        compiler_params=pltpu.CompilerParams(dimension_semantics=("arbitrary",)),
        cost_estimate=cost,
    )(first_block, query, key, value, qseg, kseg)


def regroup_attend(query_rows, key_rows, value_rows, segments):
    tok_count = lax.axis_size("tok")
    token_rows = query_rows.shape[1]
    feature_width = query_rows.shape[2]
    group_width = feature_width // tok_count

    def to_heads(rows_in):
        split = rows_in[0].reshape(token_rows, tok_count, group_width)
        gathered = lax.all_to_all(split, "tok", split_axis=1, concat_axis=0, tiled=True)
        return gathered.reshape(token_rows * tok_count, group_width)

    attended = attend_local(to_heads(query_rows), to_heads(key_rows), to_heads(value_rows), segments)
    by_source = attended.reshape(tok_count, token_rows, group_width).transpose(1, 0, 2)
    returned = lax.all_to_all(by_source, "tok", split_axis=1, concat_axis=1, tiled=True)
    return returned.reshape(1, token_rows, feature_width)


def relocate(cache_blocks, destinations):
    groups = lax.axis_size("req")
    tok_count = lax.axis_size("tok")
    local_blocks = cache_blocks[0]
    block_count, kv_count, heads_all, entries = local_blocks.shape
    split = local_blocks.reshape(block_count, kv_count, tok_count, heads_all // tok_count, entries)
    by_head = lax.all_to_all(split, "tok", split_axis=2, concat_axis=2, tiled=True)
    targets = lax.all_gather(destinations[0, :, 0], "tok")
    positions = jnp.arange(block_count, dtype=jnp.int32)
    earlier = (targets[:, :, None] == targets[:, None, :]) & (positions[None, None, :] < positions[None, :, None])
    slot_rank = jnp.sum(earlier.astype(jnp.int32), axis=2)
    group_ids = jnp.arange(groups, dtype=jnp.int32)
    slot_ids = jnp.arange(CAP, dtype=jnp.int32)
    placing = (
        (targets[:, :, None, None] == group_ids[None, None, :, None])
        & (slot_rank[:, :, None, None] == slot_ids[None, None, None, :])
    ).astype(cache_blocks.dtype)
    outgoing = jnp.einsum(
        "tbgc,bktjy->gcktjy", placing, by_head, preferred_element_type=jnp.float32
    ).astype(cache_blocks.dtype)
    arrived = lax.all_to_all(outgoing, "req", split_axis=0, concat_axis=0, tiled=True)
    return arrived[None]


def on_device(query_rows, key_rows, value_rows, lengths, cache_blocks, destinations):
    span_length = query_rows.shape[1] * lax.axis_size("tok")
    segments = segment_ids(lengths[0], span_length)
    attended = regroup_attend(query_rows, key_rows, value_rows, segments)
    moved_cache = relocate(cache_blocks, destinations)
    return (attended, moved_cache)


def solution(mesh):
    return jax.shard_map(
        on_device,
        mesh=mesh,
        in_specs=(
            P("req", "tok", None),
            P("req", "tok", None),
            P("req", "tok", None),
            P("req", None),
            P("req", "tok", None, None, None),
            P("req", "tok", None),
        ),
        out_specs=(P("req", "tok", None), P("req", None, None, None, None, "tok", None)),
        check_vma=False,
    )
```

time: 427 us -> 460 us (1.077); the launches traced: 420 us -> 458 us
  matrix products: 74.7 us -> 4.08 us
  blocking collectives: 0 us -> 58.7 us
  Pallas kernels: 0 us -> 47.3 us
  local copies, waits for them, and re-layouts: 121 us -> 75.2 us
  waiting for transfers between devices: 153 us -> 195 us
  starting transfers between devices: 38.4 us -> 47.7 us
    dot_general x33 -> x1, matrix products: 74.7 us -> 4.08 us  [relocate(): jnp.einsum('tbgc,bktjy->gcktjy', placing, by_head, preferred_element_type...]
    all_gather x0 -> x1, blocking collectives: none -> 58.7 us  [relocate(): targets = lax.all_gather(destinations[0, :, 0], 'tok')]
    pallas_call x0 -> x1, Pallas kernels: none -> 47.3 us  [attend_local(): pl.pallas_call(attention_kernel, out_shape=jax.ShapeDtypeStruct((length,...]
    unnamed x46 -> x12, local copies, waits for them, and re-layouts: 82.9 us -> 36.9 us
    all_to_all x6, waiting for transfers between devices: 153 us -> 195 us  [the longest x3 118 us: to_heads(): lax.all_to_all(split, 'tok', split_axis=1, concat_axis=0, tiled=True)]
    scatter-add x0 -> x1, other arithmetic: none -> 28.8 us  [attend_local(): ends = jnp.cumsum(jnp.bincount(segments, length=8))]
    reduce_sum x9 -> x1, other arithmetic: 19.2 us -> 0.1 us  [relocate(): slot_rank = jnp.sum(earlier.astype(jnp.int32), axis=2)]
    all_to_all x6, starting transfers between devices: 38.4 us -> 47.7 us  [the longest x3 19.8 us: to_heads(): lax.all_to_all(split, 'tok', split_axis=1, concat_axis=0, tiled=True)]
  transfers between devices with their start and end apart: 6 -> 6, of which waited for: 5 -> 4; matrix products, arithmetic and copies ran while one was open for 50% -> 21% of each run, Pallas kernels for 0% -> 10%
where the time goes in v1:
time: 460 us; the launch traced here: 458 us
  waiting for transfers between devices  195 us (42%)
  local copies, waits for them, and re-layouts  75.2 us (16%)
  blocking collectives  58.7 us (13%)
  starting transfers between devices  47.7 us (10%)
  Pallas kernels  47.3 us (10%)
  other arithmetic  30 us (7%)
    all_to_all x3, waiting for transfers between devices, to_heads(): lax.all_to_all(split, 'tok', split_axis=1, concat_axis=0, tiled=True)  118 us
    all_to_all x1, waiting for transfers between devices, relocate(): lax.all_to_all(outgoing, 'req', split_axis=0, concat_axis=0, tiled=True)  76.6 us
    all_gather x1, blocking collectives, relocate(): targets = lax.all_gather(destinations[0, :, 0], 'tok')  58.7 us
    pallas_call x1, Pallas kernels, attend_local(): pl.pallas_call(attention_kernel, out_shape=jax.ShapeDtypeStruct((length,...  47.3 us
    unnamed x12, local copies, waits for them, and re-layouts  36.9 us
    scatter-add x1, other arithmetic, attend_local(): ends = jnp.cumsum(jnp.bincount(segments, length=8))  28.8 us
    all_to_all x3, starting transfers between devices, to_heads(): lax.all_to_all(split, 'tok', split_axis=1, concat_axis=0, tiled=True)  19.8 us
    all_to_all x3, local copies, waits for them, and re-layouts, to_heads(): lax.all_to_all(split, 'tok', split_axis=1, concat_axis=0, tiled=True)  18.4 us
  transfers between devices with their start and end apart: 6, of which 4 were waited for; matrix products, arithmetic and copies ran while one was open for 21% of the time, Pallas kernels for 10%

profile of v1, /device:TPU:1, one launch (start us, length us, event | category | flops | bytes accessed | tf_op | source)
XLA Modules:
  0.0 458.4 jit_solution(11779514691995795940)
XLA Ops:
  0.6 5.9 %copy.49 = bf16[1,256,7168]{1,2,0:T(8,128)(2,1)} copy(bf16[1,256,7168]{2,1,0:T(8,128)(2,1)} %param.7) | data formatting | bytes 7340032 | tf_op args[1]
  6.5 9.3 %all-to-all-start.1 = ((bf16[256,16,448]{0,2,1:T(8,128)(2,1)}), bf16[256,16,448]{0,2,1:T(8,128)(2,1)}, u32[]{:S(2)}, u32[]{:S(2)}) async-start(bf16[256,16,448]{0,2,1:T(8,128)(2,1)} %bitcast.47), calls=%async_computation.1 | async-start | bytes 7340032 | tf_op jit(solution)/shard_map/all_to_all | solution.py:122
  15.8 5.9 %copy.51 = bf16[1,256,7168]{1,2,0:T(8,128)(2,1)} copy(bf16[1,256,7168]{2,1,0:T(8,128)(2,1)} %param.8) | data formatting | bytes 7340032 | tf_op args[2]
  21.7 39.6 %all-to-all-done.1 = bf16[256,16,448]{0,2,1:T(8,128)(2,1)} async-done(((bf16[256,16,448]{0,2,1:T(8,128)(2,1)}), bf16[256,16,448]{0,2,1:T(8,128)(2,1)}, u32[]{:S(2)}, u32[]{:S(2)}) %all-to-all-start.1) | async-done | bytes 3670048 | tf_op jit(solution)/shard_map/all_to_all | solution.py:122
  61.3 5.2 %all-to-all-start.2 = ((bf16[256,16,448]{0,2,1:T(8,128)(2,1)}), bf16[256,16,448]{0,2,1:T(8,128)(2,1)}, u32[]{:S(2)}, u32[]{:S(2)}) async-start(bf16[256,16,448]{0,2,1:T(8,128)(2,1)} %bitcast.46), calls=%async_computation.2 | async-start | bytes 7340032 | tf_op jit(solution)/shard_map/all_to_all | solution.py:122
  66.5 5.9 %copy.47 = bf16[1,256,7168]{1,2,0:T(8,128)(2,1)} copy(bf16[1,256,7168]{2,1,0:T(8,128)(2,1)} %param.6) | data formatting | bytes 7340032 | tf_op args[0]
  72.4 39.6 %all-to-all-done.2 = bf16[256,16,448]{0,2,1:T(8,128)(2,1)} async-done(((bf16[256,16,448]{0,2,1:T(8,128)(2,1)}), bf16[256,16,448]{0,2,1:T(8,128)(2,1)}, u32[]{:S(2)}, u32[]{:S(2)}) %all-to-all-start.2) | async-done | bytes 3670048 | tf_op jit(solution)/shard_map/all_to_all | solution.py:122
  112.1 0.0 copy-start.2
  112.1 5.3 %all-to-all-start = ((bf16[256,16,448]{0,2,1:T(8,128)(2,1)}), bf16[256,16,448]{0,2,1:T(8,128)(2,1)}, u32[]{:S(2)}, u32[]{:S(2)}) async-start(bf16[256,16,448]{0,2,1:T(8,128)(2,1)} %bitcast.45), calls=%async_computation | async-start | bytes 7340032 | tf_op jit(solution)/shard_map/all_to_all | solution.py:122
  117.4 0.0 copy-done.2
  117.4 0.2 reduce-window.17
  117.6 0.1 convert_reduce_fusion
  117.7 0.0 copy-start
  117.7 0.1 slice.3
  117.8 4.1 copy.58
  121.8 2.1 copy.59
  123.9 39.0 %all-to-all-done = bf16[256,16,448]{0,2,1:T(8,128)(2,1)} async-done(((bf16[256,16,448]{0,2,1:T(8,128)(2,1)}), bf16[256,16,448]{0,2,1:T(8,128)(2,1)}, u32[]{:S(2)}, u32[]{:S(2)}) %all-to-all-start) | async-done | bytes 3670048 | tf_op jit(solution)/shard_map/all_to_all | solution.py:122
  162.9 5.2 %all-to-all-start.4 = ((bf16[8,2,16,2,3584]{4,0,3,1,2:T(8,128)(2,1)}), bf16[8,2,16,2,3584]{4,0,3,1,2:T(8,128)(2,1)}, u32[]{:S(2)}, u32[]{:S(2)}) async-start(bf16[8,2,16,2,3584]{4,0,3,1,2:T(8,128)(2,1)} %copy.59), calls=%async_computation.4 | async-start | bytes 7340032 | tf_op jit(solution)/shard_map/all_to_all | solution.py:137
  168.1 0.0 copy-done
  168.1 2.0 copy.53.qseg_ref
  170.1 28.8 %scatter_custom_fusion = s32[8]{0:T(128)S(1)} fusion(s32[4096]{0:T(1024)S(1)} %bitcast.59, s32[4096]{0:T(1024)S(1)} %broadcast.65, s32[]{:T(128)} %constant.24.clone.1), kind=kCustom, calls=%fused_computation.23 | custom fusion | flops 4096 | bytes 36 | tf_op jit(solution)/shard_map/scatter-add | solution.py:77
  198.9 0.2 reduce-window.18
  199.1 0.6 gather_fusion
  199.7 0.5 and_select_fusion.first_block_ref
  200.3 6.1 %copy.50 = bf16[16,256,1,448]{3,1,0,2:T(8,128)(2,1)} copy(bf16[16,256,1,448]{1,3,0,2:T(8,128)(2,1)} %bitcast.12) | data formatting | bytes 7340032 | tf_op jit(solution)/shard_map/all_to_all | solution.py:122
  206.4 6.1 %copy.52 = bf16[16,256,1,448]{3,1,0,2:T(8,128)(2,1)} copy(bf16[16,256,1,448]{1,3,0,2:T(8,128)(2,1)} %bitcast.16) | data formatting | bytes 7340032 | tf_op jit(solution)/shard_map/all_to_all | solution.py:122
  212.5 6.1 %copy.48 = bf16[16,256,1,448]{3,1,0,2:T(8,128)(2,1)} copy(bf16[16,256,1,448]{1,3,0,2:T(8,128)(2,1)} %bitcast.8) | data formatting | bytes 7340032 | tf_op jit(solution)/shard_map/all_to_all | solution.py:122
  218.7 47.3 %shard_map.77 = bf16[4096,448]{1,0:T(8,128)(2,1)} custom-call(s32[8]{0:T(128)} %and_select_fusion.first_block_ref, bf16[4096,448]{1,0:T(8,128)(2,1)} %bitcast.52, bf16[4096,448]{1,0:T(8,128)(2,1)} %bitcast.50, bf16[4096,448]{1,0:T(8,128)(2,1)} %bitcast.51, s32[4096,1]{1,0:T(8,128)} %copy.53.qseg_ref, s32[1,4096]{1,0:T(1,128)} %bitcast.56), custom_call_target="tpu_custom_call" | custom-call | flops 30064771072 | bytes 14680064 | tf_op jit(solution)/shard_map/pallas_call | solution.py:89
  265.9 6.2 %copy.54 = bf16[16,256,448]{1,2,0:T(8,128)(2,1)} copy(bf16[16,256,448]{2,1,0:T(8,128)(2,1)} %bitcast.53) | data formatting | bytes 7340032 | tf_op jit(solution)/shard_map/reshape | solution.py:126
  272.1 0.0 all-to-all-done.4
  272.1 0.0 copy-start.1
  272.1 7.4 %all-to-all-start.3 = ((bf16[256,16,448]{0,2,1:T(8,128)(2,1)}), bf16[256,16,448]{0,2,1:T(8,128)(2,1)}, u32[]{:S(2)}, u32[]{:S(2)}) async-start(bf16[256,16,448]{0,2,1:T(8,128)(2,1)} %bitcast.49), calls=%async_computation.3 | async-start | bytes 7340032 | tf_op jit(solution)/shard_map/all_to_all | solution.py:127
  279.5 0.0 copy-done.1
  279.5 58.7 %all-gather = s32[16,8,1]{1,2,0:T(1,128)S(1)} all-gather(s32[1,8,1]{1,2,0:T(1,128)S(1)} %copy-done.1), channel_id=2, replica_groups=mesh['tok'=16,'req'=8] {'tok'}, dimensions={0}, use_global_device_ids=true | all-gather | bytes 544 | tf_op jit(solution)/shard_map/all_gather | solution.py:138
  338.3 0.1 convert_reduce_fusion.1
  338.4 4.1 fusion
  342.5 8.9 %copy.60 = bf16[8,2,2,16,2,3584]{5,4,2,1,3,0:T(2,128)(2,1)} copy(bf16[8,2,2,16,2,3584]{5,0,4,2,1,3:T(8,128)(2,1)S(1)} %fusion) | data formatting | bytes 14680064 | tf_op jit(solution)/shard_map/convert_element_type | solution.py:150
  351.4 0.0 all-to-all-done.3
  351.4 15.3 %all-to-all-start.5 = ((bf16[8,2,2,16,2,3584]{5,4,2,1,3,0:T(2,128)(2,1)}), bf16[8,2,2,16,2,3584]{5,4,2,1,3,0:T(2,128)(2,1)}, u32[]{:S(2)}, u32[]{:S(2)}) async-start(bf16[8,2,2,16,2,3584]{5,4,2,1,3,0:T(2,128)(2,1)} %copy.60), calls=%async_computation.5 | async-start | bytes 14680064 | tf_op jit(solution)/shard_map/all_to_all | solution.py:151
  366.7 5.9 %copy.61 = bf16[1,256,7168]{2,1,0:T(8,128)(2,1)} copy(bf16[1,256,7168]{1,2,0:T(8,128)(2,1)} %bitcast.21) | data formatting | bytes 7340032
  372.6 76.6 %all-to-all-done.5 = bf16[8,2,2,16,2,3584]{5,4,2,1,3,0:T(2,128)(2,1)} async-done(((bf16[8,2,2,16,2,3584]{5,4,2,1,3,0:T(2,128)(2,1)}), bf16[8,2,2,16,2,3584]{5,4,2,1,3,0:T(2,128)(2,1)}, u32[]{:S(2)}, u32[]{:S(2)}) %all-to-all-start.5) | async-done | bytes 7340064 | tf_op jit(solution)/shard_map/all_to_all | solution.py:151
  449.2 9.2 %copy.62 = bf16[1,8,2,2,16,2,3584]{6,5,4,3,2,1,0:T(2,128)(2,1)} copy(bf16[1,8,2,2,16,2,3584]{6,5,3,2,4,1,0:T(2,128)(2,1)} %bitcast.31) | data formatting | bytes 14680064
  (8 shorter events, 0.1 us)
Async XLA Ops:
  6.5 54.8 %all-to-all-start.1 = ((bf16[256,16,448]{0,2,1:T(8,128)(2,1)}), bf16[256,16,448]{0,2,1:T(8,128)(2,1)}, u32[]{:S(2)}, u32[]{:S(2)}) async-start(bf16[256,16,448]{0,2,1:T(8,128)(2,1)} %bitcast.47), calls=%async_computation.1 | async-start | bytes 7340032 | tf_op jit(solution)/shard_map/all_to_all | solution.py:122
  61.3 50.7 %all-to-all-start.2 = ((bf16[256,16,448]{0,2,1:T(8,128)(2,1)}), bf16[256,16,448]{0,2,1:T(8,128)(2,1)}, u32[]{:S(2)}, u32[]{:S(2)}) async-start(bf16[256,16,448]{0,2,1:T(8,128)(2,1)} %bitcast.46), calls=%async_computation.2 | async-start | bytes 7340032 | tf_op jit(solution)/shard_map/all_to_all | solution.py:122
  112.1 5.3 %copy-start.2 = (s32[1,6]{1,0:T(1,128)S(1)}, s32[1,6]{1,0:T(1,128)}, u32[]{:S(2)}) copy-start(s32[1,6]{1,0:T(1,128)} %param.9) | copy-start | bytes 76
  112.1 50.9 %all-to-all-start = ((bf16[256,16,448]{0,2,1:T(8,128)(2,1)}), bf16[256,16,448]{0,2,1:T(8,128)(2,1)}, u32[]{:S(2)}, u32[]{:S(2)}) async-start(bf16[256,16,448]{0,2,1:T(8,128)(2,1)} %bitcast.45), calls=%async_computation | async-start | bytes 7340032 | tf_op jit(solution)/shard_map/all_to_all | solution.py:122
  117.7 50.4 %copy-start = (s32[4096]{0:T(1024)}, s32[4096]{0:T(1024)S(1)}, u32[]{:S(2)}) copy-start(s32[4096]{0:T(1024)S(1)} %convert_reduce_fusion) | copy-start | bytes 49156
  162.9 109.2 %all-to-all-start.4 = ((bf16[8,2,16,2,3584]{4,0,3,1,2:T(8,128)(2,1)}), bf16[8,2,16,2,3584]{4,0,3,1,2:T(8,128)(2,1)}, u32[]{:S(2)}, u32[]{:S(2)}) async-start(bf16[8,2,16,2,3584]{4,0,3,1,2:T(8,128)(2,1)} %copy.59), calls=%async_computation.4 | async-start | bytes 7340032 | tf_op jit(solution)/shard_map/all_to_all | solution.py:137
  272.1 7.4 %copy-start.1 = (s32[1,8,1]{1,2,0:T(1,128)S(1)}, s32[1,8,1]{1,2,0:T(1,128)}, u32[]{:S(2)}) copy-start(s32[1,8,1]{1,2,0:T(1,128)} %param.11) | copy-start | bytes 100
  272.1 79.3 %all-to-all-start.3 = ((bf16[256,16,448]{0,2,1:T(8,128)(2,1)}), bf16[256,16,448]{0,2,1:T(8,128)(2,1)}, u32[]{:S(2)}, u32[]{:S(2)}) async-start(bf16[256,16,448]{0,2,1:T(8,128)(2,1)} %bitcast.49), calls=%async_computation.3 | async-start | bytes 7340032 | tf_op jit(solution)/shard_map/all_to_all | solution.py:127
  351.4 97.8 %all-to-all-start.5 = ((bf16[8,2,2,16,2,3584]{5,4,2,1,3,0:T(2,128)(2,1)}), bf16[8,2,2,16,2,3584]{5,4,2,1,3,0:T(2,128)(2,1)}, u32[]{:S(2)}, u32[]{:S(2)}) async-start(bf16[8,2,2,16,2,3584]{5,4,2,1,3,0:T(2,128)(2,1)} %copy.60), calls=%async_computation.5 | async-start | bytes 14680064 | tf_op jit(solution)/shard_map/all_to_all | solution.py:151

commit v2 on v1

v2 whole, which is shorter than its diff:
```python
import functools

import jax
import jax.numpy as jnp
from jax import lax
from jax.experimental import pallas as pl
from jax.experimental.pallas import tpu as pltpu
from jax.sharding import PartitionSpec as P

HD = 224
CAP = 2
NEG = -1e30


def segment_ids(lengths_row, span_length):
    ends = jnp.cumsum(lengths_row)
    positions = jnp.arange(span_length, dtype=jnp.int32)
    return jnp.sum((positions[:, None] >= ends[None, :]).astype(jnp.int32), axis=1)


def attention_kernel(first_ref, seg_first_ref, seg_last_ref, q_ref, k_ref, v_ref, qseg_ref, kseg_ref, o_ref,
                     m_ref, l_ref, acc_ref, q_sc):
    qi = pl.program_id(0)
    width, rows = q_ref.shape[1], q_ref.shape[2]
    heads_here = width // HD
    eye_rows = lax.broadcasted_iota(jnp.int32, (rows, rows), 0) == lax.broadcasted_iota(jnp.int32, (rows, rows), 1)
    eye = eye_rows.astype(jnp.bfloat16)
    nt = (((1,), (1,)), ((), ()))
    for h in range(heads_here):
        q_sc[h] = lax.dot_general(
            eye, q_ref[0, h * HD:(h + 1) * HD, :], nt, preferred_element_type=jnp.float32
        ).astype(jnp.bfloat16)
    m_ref[...] = jnp.full(m_ref.shape, NEG, jnp.float32)
    l_ref[...] = jnp.zeros(l_ref.shape, jnp.float32)
    acc_ref[...] = jnp.zeros(acc_ref.shape, jnp.float32)
    scale = HD ** (-0.5)
    query_seg = qseg_ref[...]
    query_pos = qi * rows + lax.broadcasted_iota(jnp.int32, (rows, 1), 0)

    def step(kb, masked):
        if masked:
            key_seg = kseg_ref[kb]
            key_pos = kb * rows + lax.broadcasted_iota(jnp.int32, (1, rows), 1)
            visible = (query_seg == key_seg) & (query_pos >= key_pos)
        for h in range(heads_here):
            keys = k_ref[kb, h * HD:(h + 1) * HD, :]
            scores = jnp.dot(q_sc[h], keys, preferred_element_type=jnp.float32) * scale
            if masked:
                scores = jnp.where(visible, scores, NEG)
            m_old = m_ref[h]
            m_new = jnp.maximum(m_old, jnp.max(scores, axis=1, keepdims=True))
            alpha = jnp.exp(m_old - m_new)
            weights = jnp.exp(scores - m_new)
            if masked:
                weights = jnp.where(visible, weights, 0.0)
            l_ref[h] = alpha * l_ref[h] + jnp.sum(weights, axis=1, keepdims=True)
            m_ref[h] = m_new
            values = v_ref[kb, h * HD:(h + 1) * HD, :]
            acc_ref[h] = alpha * acc_ref[h] + lax.dot_general(
                weights.astype(jnp.bfloat16), values, nt, preferred_element_type=jnp.float32
            )

    def body(kb, carry):
        full = (kb < qi) & (seg_first_ref[kb] == seg_last_ref[qi])

        @pl.when(full)
        def _():
            step(kb, False)

        @pl.when(jnp.logical_not(full))
        def _():
            step(kb, True)

        return carry

    lax.fori_loop(first_ref[qi], qi + 1, body, 0)
    eye_out = (lax.broadcasted_iota(jnp.int32, (HD, HD), 0) == lax.broadcasted_iota(jnp.int32, (HD, HD), 1)).astype(jnp.bfloat16)
    for h in range(heads_here):
        out_rows = (acc_ref[h] / l_ref[h]).astype(jnp.bfloat16)
        o_ref[0, h * HD:(h + 1) * HD, :] = lax.dot_general(
            eye_out, out_rows, nt, preferred_element_type=jnp.float32
        ).astype(o_ref.dtype)


def attend_local(query_t, key_t, value_t, lengths_row, segments):
    chunks, width, rows = query_t.shape
    heads_here = width // HD
    length = chunks * rows
    ends = jnp.cumsum(lengths_row)
    starts = ends - lengths_row
    seg_first = segments[::rows]
    seg_last = segments[rows - 1::rows]
    first_start = jnp.sum(
        jnp.where(seg_first[:, None] == jnp.arange(lengths_row.shape[0])[None, :], starts[None, :], 0), axis=1
    )
    first_chunk = (first_start // rows).astype(jnp.int32)
    qseg = segments.reshape(length, 1)
    kseg = segments.reshape(chunks, 1, rows)
    visible_pairs = length * length // 2
    cost = pl.CostEstimate(
        flops=int(4 * visible_pairs * width),
        transcendentals=int(heads_here * visible_pairs),
        bytes_accessed=int(4 * length * width * 2),
    )
    return pl.pallas_call(
        attention_kernel,
        out_shape=jax.ShapeDtypeStruct(query_t.shape, query_t.dtype),
        grid_spec=pltpu.PrefetchScalarGridSpec(
            num_scalar_prefetch=3,
            grid=(chunks,),
            in_specs=[
                pl.BlockSpec((1, width, rows), lambda i, *_: (i, 0, 0)),
                pl.BlockSpec((chunks, width, rows), lambda i, *_: (0, 0, 0), pipeline_mode=pl.Buffered(1)),
                pl.BlockSpec((chunks, width, rows), lambda i, *_: (0, 0, 0), pipeline_mode=pl.Buffered(1)),
                pl.BlockSpec((rows, 1), lambda i, *_: (i, 0)),
                pl.BlockSpec((chunks, 1, rows), lambda i, *_: (0, 0, 0)),
            ],
            out_specs=pl.BlockSpec((1, width, rows), lambda i, *_: (i, 0, 0)),
            scratch_shapes=[
                pltpu.VMEM((heads_here, rows, 1), jnp.float32),
                pltpu.VMEM((heads_here, rows, 1), jnp.float32),
                pltpu.VMEM((heads_here, rows, HD), jnp.float32),
                pltpu.VMEM((heads_here, rows, HD), jnp.bfloat16),
            ],
        ),
        compiler_params=pltpu.CompilerParams(dimension_semantics=("arbitrary",)),
        cost_estimate=cost,
    )(first_chunk, seg_first, seg_last, query_t, key_t, value_t, qseg, kseg)


def regroup_attend(query_rows, key_rows, value_rows, lengths_row, segments):
    tok_count = lax.axis_size("tok")
    token_rows = query_rows.shape[1]
    feature_width = query_rows.shape[2]
    group_width = feature_width // tok_count

    def to_heads(rows_in):
        split = rows_in[0].reshape(token_rows, tok_count, group_width)
        gathered = lax.all_to_all(split, "tok", split_axis=1, concat_axis=1, tiled=True)
        return gathered.transpose(1, 2, 0)

    attended_t = attend_local(
        to_heads(query_rows), to_heads(key_rows), to_heads(value_rows), lengths_row, segments
    )
    by_source = attended_t.transpose(2, 0, 1)
    returned = lax.all_to_all(by_source, "tok", split_axis=1, concat_axis=1, tiled=True)
    return returned.reshape(1, token_rows, feature_width)


def relocate(cache_blocks, targets):
    groups = lax.axis_size("req")
    tok_count = lax.axis_size("tok")
    local_blocks = cache_blocks[0]
    block_count, kv_count, heads_all, entries = local_blocks.shape
    split = local_blocks.reshape(block_count, kv_count, tok_count, heads_all // tok_count, entries)
    by_head = lax.all_to_all(split, "tok", split_axis=2, concat_axis=2, tiled=True)
    positions = jnp.arange(block_count, dtype=jnp.int32)
    earlier = (targets[:, :, None] == targets[:, None, :]) & (positions[None, None, :] < positions[None, :, None])
    slot_rank = jnp.sum(earlier.astype(jnp.int32), axis=2)
    group_ids = jnp.arange(groups, dtype=jnp.int32)
    slot_ids = jnp.arange(CAP, dtype=jnp.int32)
    placing = (
        (targets[:, :, None, None] == group_ids[None, None, :, None])
        & (slot_rank[:, :, None, None] == slot_ids[None, None, None, :])
    ).astype(cache_blocks.dtype)
    outgoing = jnp.einsum(
        "tbgc,bktjy->gcktjy", placing, by_head, preferred_element_type=jnp.float32
    ).astype(cache_blocks.dtype)
    arrived = lax.all_to_all(outgoing, "req", split_axis=0, concat_axis=0, tiled=True)
    return arrived[None]


def on_device(query_rows, key_rows, value_rows, lengths, cache_blocks, destinations):
    span_length = query_rows.shape[1] * lax.axis_size("tok")
    segments = segment_ids(lengths[0], span_length)
    targets = lax.all_gather(destinations[0, :, 0], "tok")
    targets, query_rows, key_rows, value_rows, cache_blocks = lax.optimization_barrier(
        (targets, query_rows, key_rows, value_rows, cache_blocks)
    )
    attended = regroup_attend(query_rows, key_rows, value_rows, lengths[0], segments)
    moved_cache = relocate(cache_blocks, targets)
    return (attended, moved_cache)


def solution(mesh):
    return jax.shard_map(
        on_device,
        mesh=mesh,
        in_specs=(
            P("req", "tok", None),
            P("req", "tok", None),
            P("req", "tok", None),
            P("req", None),
            P("req", "tok", None, None, None),
            P("req", "tok", None),
        ),
        out_specs=(P("req", "tok", None), P("req", None, None, None, None, "tok", None)),
        check_vma=False,
    )
```

time: 460 us -> 439 us (0.954)
  Pallas kernels: 47.3 us -> 90.6 us
  waiting for transfers between devices: 195 us -> 228 us
  blocking collectives: 58.7 us -> 26.8 us
  other arithmetic: 30 us -> 1.07 us
  local copies, waits for them, and re-layouts: 75.2 us -> 53.2 us
  starting transfers between devices: 47.7 us -> 33.5 us
    pallas_call x1, Pallas kernels: 47.3 us -> 90.6 us  [attend_local(): pl.pallas_call(attention_kernel, out_shape=jax.ShapeDtypeStruct(query_t.s...]
    all_to_all x1, waiting for transfers between devices: 0.01 us -> 32.3 us  [regroup_attend(): lax.all_to_all(by_source, 'tok', split_axis=1, concat_axis=1, tiled=True)]
    all_gather x1, blocking collectives: 58.7 us -> 26.8 us  [on_device(): targets = lax.all_gather(destinations[0, :, 0], 'tok')]
    scatter-add x1 -> x0, other arithmetic: 28.8 us -> none  [attend_local(): ends = jnp.cumsum(jnp.bincount(segments, length=8))]
    optimization_barrier x0 -> x5, local copies, waits for them, and re-layouts: none -> 21.8 us  [on_device(): lax.optimization_barrier((targets, query_rows, key_rows, value_rows, cach...]
    unnamed x12 -> x8, local copies, waits for them, and re-layouts: 36.9 us -> 17.6 us
    all_to_all x3 -> x0, local copies, waits for them, and re-layouts: 18.4 us -> none  [to_heads(): lax.all_to_all(split, 'tok', split_axis=1, concat_axis=0, tiled=True)]
    all_to_all x1, starting transfers between devices: 15.3 us -> 6.27 us  [relocate(): lax.all_to_all(outgoing, 'req', split_axis=0, concat_axis=0, tiled=True)]
  transfers between devices with their start and end apart: 6 -> 6, of which waited for: 4 -> 5; matrix products, arithmetic and copies ran while one was open for 21% -> 9% of each run, Pallas kernels for 10% -> 21%
where the time goes in v2:
time: 439 us; the launch traced here: 438 us
  waiting for transfers between devices  228 us (52%)
  Pallas kernels  90.6 us (21%)
  local copies, waits for them, and re-layouts  53.2 us (12%)
  starting transfers between devices  33.5 us (8%)
  blocking collectives  26.8 us (6%)
    all_to_all x3, waiting for transfers between devices, to_heads(): lax.all_to_all(split, 'tok', split_axis=1, concat_axis=1, tiled=True)  119 us
    pallas_call x1, Pallas kernels, attend_local(): pl.pallas_call(attention_kernel, out_shape=jax.ShapeDtypeStruct(query_t.s...  90.6 us
    all_to_all x1, waiting for transfers between devices, relocate(): lax.all_to_all(outgoing, 'req', split_axis=0, concat_axis=0, tiled=True)  76.7 us
    all_to_all x1, waiting for transfers between devices, regroup_attend(): lax.all_to_all(by_source, 'tok', split_axis=1, concat_axis=1, tiled=True)  32.3 us
    all_gather x1, blocking collectives, on_device(): targets = lax.all_gather(destinations[0, :, 0], 'tok')  26.8 us
    optimization_barrier x5, local copies, waits for them, and re-layouts, on_device(): lax.optimization_barrier((targets, query_rows, key_rows, value_rows, cach...  21.8 us
    unnamed x8, local copies, waits for them, and re-layouts  17.6 us
    all_to_all x3, starting transfers between devices, to_heads(): lax.all_to_all(split, 'tok', split_axis=1, concat_axis=1, tiled=True)  14.8 us
  transfers between devices with their start and end apart: 6, of which 5 were waited for; matrix products, arithmetic and copies ran while one was open for 9% of the time, Pallas kernels for 21%

profile of v2, /device:TPU:1, one launch (start us, length us, event | category | flops | bytes accessed | tf_op | source)
XLA Modules:
  0.0 437.6 jit_solution(18074070881013810973)
XLA Ops:
  0.6 26.8 %all-gather = s32[16,8,1]{1,2,0:T(1,128)S(1)} all-gather(s32[1,8,1]{1,2,0:T(1,128)} %param.11), channel_id=2, replica_groups=mesh['tok'=16,'req'=8] {'tok'}, dimensions={0}, use_global_device_ids=true | all-gather | bytes 544 | tf_op jit(solution)/shard_map/all_gather | solution.py:176
  27.4 0.1 copy.39
  27.5 5.9 %copy.40 = bf16[1,256,7168]{1,2,0:T(8,128)(2,1)} copy(bf16[1,256,7168]{2,1,0:T(8,128)(2,1)} %param.6) | data formatting | bytes 7340032 | tf_op jit(solution)/shard_map/optimization_barrier | solution.py:177
  33.4 4.4 %all-to-all-start = ((bf16[256,16,448]{0,2,1:T(8,128)(2,1)}), bf16[256,16,448]{0,2,1:T(8,128)(2,1)}, u32[]{:S(2)}, u32[]{:S(2)}) async-start(bf16[256,16,448]{0,2,1:T(8,128)(2,1)} %bitcast.35), calls=%async_computation | async-start | bytes 7340032 | tf_op jit(solution)/shard_map/all_to_all | solution.py:139
  37.8 5.9 %copy.41 = bf16[1,256,7168]{1,2,0:T(8,128)(2,1)} copy(bf16[1,256,7168]{2,1,0:T(8,128)(2,1)} %param.7) | data formatting | bytes 7340032 | tf_op jit(solution)/shard_map/optimization_barrier | solution.py:177
  43.7 39.6 %all-to-all-done = bf16[256,16,448]{0,2,1:T(8,128)(2,1)} async-done(((bf16[256,16,448]{0,2,1:T(8,128)(2,1)}), bf16[256,16,448]{0,2,1:T(8,128)(2,1)}, u32[]{:S(2)}, u32[]{:S(2)}) %all-to-all-start) | async-done | bytes 3670048 | tf_op jit(solution)/shard_map/all_to_all | solution.py:139
  83.4 5.2 %all-to-all-start.1 = ((bf16[256,16,448]{0,2,1:T(8,128)(2,1)}), bf16[256,16,448]{0,2,1:T(8,128)(2,1)}, u32[]{:S(2)}, u32[]{:S(2)}) async-start(bf16[256,16,448]{0,2,1:T(8,128)(2,1)} %bitcast.34), calls=%async_computation.1 | async-start | bytes 7340032 | tf_op jit(solution)/shard_map/all_to_all | solution.py:139
  88.6 5.9 %copy.42 = bf16[1,256,7168]{1,2,0:T(8,128)(2,1)} copy(bf16[1,256,7168]{2,1,0:T(8,128)(2,1)} %param.8) | data formatting | bytes 7340032 | tf_op jit(solution)/shard_map/optimization_barrier | solution.py:177
  94.5 39.6 %all-to-all-done.1 = bf16[256,16,448]{0,2,1:T(8,128)(2,1)} async-done(((bf16[256,16,448]{0,2,1:T(8,128)(2,1)}), bf16[256,16,448]{0,2,1:T(8,128)(2,1)}, u32[]{:S(2)}, u32[]{:S(2)}) %all-to-all-start.1) | async-done | bytes 3670048 | tf_op jit(solution)/shard_map/all_to_all | solution.py:139
  134.1 5.2 %all-to-all-start.2 = ((bf16[256,16,448]{0,2,1:T(8,128)(2,1)}), bf16[256,16,448]{0,2,1:T(8,128)(2,1)}, u32[]{:S(2)}, u32[]{:S(2)}) async-start(bf16[256,16,448]{0,2,1:T(8,128)(2,1)} %bitcast.33), calls=%async_computation.2 | async-start | bytes 7340032 | tf_op jit(solution)/shard_map/all_to_all | solution.py:139
  139.3 4.0 copy.44
  143.4 2.1 copy.45
  145.4 0.0 copy-start.1
  145.4 39.4 %all-to-all-done.2 = bf16[256,16,448]{0,2,1:T(8,128)(2,1)} async-done(((bf16[256,16,448]{0,2,1:T(8,128)(2,1)}), bf16[256,16,448]{0,2,1:T(8,128)(2,1)}, u32[]{:S(2)}, u32[]{:S(2)}) %all-to-all-start.2) | async-done | bytes 3670048 | tf_op jit(solution)/shard_map/all_to_all | solution.py:139
  184.9 5.2 %all-to-all-start.4 = ((bf16[8,2,16,2,3584]{4,0,3,1,2:T(8,128)(2,1)}), bf16[8,2,16,2,3584]{4,0,3,1,2:T(8,128)(2,1)}, u32[]{:S(2)}, u32[]{:S(2)}) async-start(bf16[8,2,16,2,3584]{4,0,3,1,2:T(8,128)(2,1)} %copy.45), calls=%async_computation.4 | async-start | bytes 7340032 | tf_op jit(solution)/shard_map/all_to_all | solution.py:156
  190.0 0.0 copy-done.1
  190.0 0.2 reduce-window.4
  190.2 0.1 convert_reduce_fusion
  190.3 0.0 copy-start
  190.4 0.1 slice.6.seg_first_ref
  190.5 0.0 copy-start.2
  190.5 0.6 slice.7.seg_last_ref
  191.1 2.0 copy.43.qseg_ref
  193.0 0.1 select_reduce_fusion
  193.1 0.5 and_select_fusion.first_ref
  193.7 0.0 copy-done
  193.7 0.0 copy-done.2
  193.7 90.6 %shard_map.77 = bf16[16,448,256]{2,1,0:T(8,128)(2,1)} custom-call(s32[16]{0:T(128)} %and_select_fusion.first_ref, s32[16]{0:T(128)} %copy-done.2, s32[16]{0:T(128)} %slice.7.seg_last_ref, bf16[16,448,256]{2,1,0:T(8,128)(2,1)} %bitcast.6.q_ref, bf16[16,448,256]{2,1,0:T(8,128)(2,1)} %bitcast.8.k_ref, bf16[16,448,256]{2,1,0:T(8,128)(2,1)} %bitcast.10.v_ref, ...), custom_call_target="tpu_custom_call" | custom-call | flops 15032385536 | bytes 14680064 | tf_op jit(solution)/shard_map/pallas_call | solution.py:105
  284.3 0.0 all-to-all-done.4
  284.3 7.3 %all-to-all-start.3 = ((bf16[256,16,448]{0,2,1:T(8,128)(2,1)}), bf16[256,16,448]{0,2,1:T(8,128)(2,1)}, u32[]{:S(2)}, u32[]{:S(2)}) async-start(bf16[256,16,448]{0,2,1:T(8,128)(2,1)} %bitcast.37), calls=%async_computation.3 | async-start | bytes 7340032 | tf_op jit(solution)/shard_map/all_to_all | solution.py:146
  291.5 0.1 copy.46
  291.6 0.1 convert_reduce_fusion.1
  291.8 4.1 fusion
  295.8 8.9 %copy.48 = bf16[8,2,2,16,2,3584]{5,1,4,2,3,0:T(2,128)(2,1)} copy(bf16[8,2,2,16,2,3584]{5,0,1,4,2,3:T(8,128)(2,1)S(1)} %fusion) | data formatting | bytes 14680064 | tf_op jit(solution)/shard_map/convert_element_type | solution.py:168
  304.8 32.3 %all-to-all-done.3 = bf16[256,16,448]{0,2,1:T(8,128)(2,1)} async-done(((bf16[256,16,448]{0,2,1:T(8,128)(2,1)}), bf16[256,16,448]{0,2,1:T(8,128)(2,1)}, u32[]{:S(2)}, u32[]{:S(2)}) %all-to-all-start.3) | async-done | bytes 3670048 | tf_op jit(solution)/shard_map/all_to_all | solution.py:146
  337.0 6.3 %all-to-all-start.5 = ((bf16[8,2,2,16,2,3584]{5,1,4,2,3,0:T(2,128)(2,1)}), bf16[8,2,2,16,2,3584]{5,1,4,2,3,0:T(2,128)(2,1)}, u32[]{:S(2)}, u32[]{:S(2)}) async-start(bf16[8,2,2,16,2,3584]{5,1,4,2,3,0:T(2,128)(2,1)} %copy.48), calls=%async_computation.5 | async-start | bytes 14680064 | tf_op jit(solution)/shard_map/all_to_all | solution.py:169
  343.3 5.9 %copy.49 = bf16[1,256,7168]{2,1,0:T(8,128)(2,1)} copy(bf16[1,256,7168]{1,2,0:T(8,128)(2,1)} %bitcast.14) | data formatting | bytes 7340032
  349.2 76.7 %all-to-all-done.5 = bf16[8,2,2,16,2,3584]{5,1,4,2,3,0:T(2,128)(2,1)} async-done(((bf16[8,2,2,16,2,3584]{5,1,4,2,3,0:T(2,128)(2,1)}), bf16[8,2,2,16,2,3584]{5,1,4,2,3,0:T(2,128)(2,1)}, u32[]{:S(2)}, u32[]{:S(2)}) %all-to-all-start.5) | async-done | bytes 7340064 | tf_op jit(solution)/shard_map/all_to_all | solution.py:169
  425.9 11.7 %copy.50 = bf16[1,8,2,2,16,2,3584]{6,5,4,3,2,1,0:T(2,128)(2,1)} copy(bf16[1,8,2,2,16,2,3584]{6,2,5,3,4,1,0:T(2,128)(2,1)} %bitcast.21) | data formatting | bytes 14680064
  (4 shorter events, 0.0 us)
Async XLA Ops:
  33.4 50.0 %all-to-all-start = ((bf16[256,16,448]{0,2,1:T(8,128)(2,1)}), bf16[256,16,448]{0,2,1:T(8,128)(2,1)}, u32[]{:S(2)}, u32[]{:S(2)}) async-start(bf16[256,16,448]{0,2,1:T(8,128)(2,1)} %bitcast.35), calls=%async_computation | async-start | bytes 7340032 | tf_op jit(solution)/shard_map/all_to_all | solution.py:139
  83.4 50.7 %all-to-all-start.1 = ((bf16[256,16,448]{0,2,1:T(8,128)(2,1)}), bf16[256,16,448]{0,2,1:T(8,128)(2,1)}, u32[]{:S(2)}, u32[]{:S(2)}) async-start(bf16[256,16,448]{0,2,1:T(8,128)(2,1)} %bitcast.34), calls=%async_computation.1 | async-start | bytes 7340032 | tf_op jit(solution)/shard_map/all_to_all | solution.py:139
  134.1 50.7 %all-to-all-start.2 = ((bf16[256,16,448]{0,2,1:T(8,128)(2,1)}), bf16[256,16,448]{0,2,1:T(8,128)(2,1)}, u32[]{:S(2)}, u32[]{:S(2)}) async-start(bf16[256,16,448]{0,2,1:T(8,128)(2,1)} %bitcast.33), calls=%async_computation.2 | async-start | bytes 7340032 | tf_op jit(solution)/shard_map/all_to_all | solution.py:139
  145.4 44.6 %copy-start.1 = (s32[1,6]{1,0:T(1,128)S(1)}, s32[1,6]{1,0:T(1,128)}, u32[]{:S(2)}) copy-start(s32[1,6]{1,0:T(1,128)} %param.9) | copy-start | bytes 76
  184.9 99.4 %all-to-all-start.4 = ((bf16[8,2,16,2,3584]{4,0,3,1,2:T(8,128)(2,1)}), bf16[8,2,16,2,3584]{4,0,3,1,2:T(8,128)(2,1)}, u32[]{:S(2)}, u32[]{:S(2)}) async-start(bf16[8,2,16,2,3584]{4,0,3,1,2:T(8,128)(2,1)} %copy.45), calls=%async_computation.4 | async-start | bytes 7340032 | tf_op jit(solution)/shard_map/all_to_all | solution.py:156
  190.3 3.3 copy-start
  190.5 3.2 copy-start.2
  284.3 52.8 %all-to-all-start.3 = ((bf16[256,16,448]{0,2,1:T(8,128)(2,1)}), bf16[256,16,448]{0,2,1:T(8,128)(2,1)}, u32[]{:S(2)}, u32[]{:S(2)}) async-start(bf16[256,16,448]{0,2,1:T(8,128)(2,1)} %bitcast.37), calls=%async_computation.3 | async-start | bytes 7340032 | tf_op jit(solution)/shard_map/all_to_all | solution.py:146
  337.0 88.9 %all-to-all-start.5 = ((bf16[8,2,2,16,2,3584]{5,1,4,2,3,0:T(2,128)(2,1)}), bf16[8,2,2,16,2,3584]{5,1,4,2,3,0:T(2,128)(2,1)}, u32[]{:S(2)}, u32[]{:S(2)}) async-start(bf16[8,2,2,16,2,3584]{5,1,4,2,3,0:T(2,128)(2,1)} %copy.48), calls=%async_computation.5 | async-start | bytes 14680064 | tf_op jit(solution)/shard_map/all_to_all | solution.py:169

commit v3 on v2

--- a/solution.py
+++ b/solution.py
@@ -128,32 +128,32 @@
     )(first_chunk, seg_first, seg_last, query_t, key_t, value_t, qseg, kseg)
 
 
-def regroup_attend(query_rows, key_rows, value_rows, lengths_row, segments):
+def to_heads(rows_in):
     tok_count = lax.axis_size("tok")
-    token_rows = query_rows.shape[1]
-    feature_width = query_rows.shape[2]
-    group_width = feature_width // tok_count
-
-    def to_heads(rows_in):
-        split = rows_in[0].reshape(token_rows, tok_count, group_width)
-        gathered = lax.all_to_all(split, "tok", split_axis=1, concat_axis=1, tiled=True)
-        return gathered.transpose(1, 2, 0)
-
-    attended_t = attend_local(
-        to_heads(query_rows), to_heads(key_rows), to_heads(value_rows), lengths_row, segments
-    )
+    token_rows, feature_width = rows_in.shape[1], rows_in.shape[2]
+    split = rows_in[0].reshape(token_rows, tok_count, feature_width // tok_count)
+    gathered = lax.all_to_all(split, "tok", split_axis=1, concat_axis=1, tiled=True)
+    return gathered.transpose(1, 2, 0)
+
+
+def from_heads(attended_t):
+    token_rows = attended_t.shape[2]
     by_source = attended_t.transpose(2, 0, 1)
     returned = lax.all_to_all(by_source, "tok", split_axis=1, concat_axis=1, tiled=True)
-    return returned.reshape(1, token_rows, feature_width)
-
-
-def relocate(cache_blocks, targets):
-    groups = lax.axis_size("req")
+    return returned.reshape(1, token_rows, -1)
+
+
+def relocate_by_head(cache_blocks):
     tok_count = lax.axis_size("tok")
     local_blocks = cache_blocks[0]
     block_count, kv_count, heads_all, entries = local_blocks.shape
     split = local_blocks.reshape(block_count, kv_count, tok_count, heads_all // tok_count, entries)
-    by_head = lax.all_to_all(split, "tok", split_axis=2, concat_axis=2, tiled=True)
+    return lax.all_to_all(split, "tok", split_axis=2, concat_axis=2, tiled=True)
+
+
+def place_slots(by_head, targets):
+    groups = lax.axis_size("req")
+    block_count = by_head.shape[0]
     positions = jnp.arange(block_count, dtype=jnp.int32)
     earlier = (targets[:, :, None] == targets[:, None, :]) & (positions[None, None, :] < positions[None, :, None])
     slot_rank = jnp.sum(earlier.astype(jnp.int32), axis=2)
@@ -162,10 +162,13 @@
     placing = (
         (targets[:, :, None, None] == group_ids[None, None, :, None])
         & (slot_rank[:, :, None, None] == slot_ids[None, None, None, :])
-    ).astype(cache_blocks.dtype)
-    outgoing = jnp.einsum(
+    ).astype(by_head.dtype)
+    return jnp.einsum(
         "tbgc,bktjy->gcktjy", placing, by_head, preferred_element_type=jnp.float32
-    ).astype(cache_blocks.dtype)
+    ).astype(by_head.dtype)
+
+
+def relocate_groups(outgoing):
     arrived = lax.all_to_all(outgoing, "req", split_axis=0, concat_axis=0, tiled=True)
     return arrived[None]
 
@@ -174,11 +177,18 @@
     span_length = query_rows.shape[1] * lax.axis_size("tok")
     segments = segment_ids(lengths[0], span_length)
     targets = lax.all_gather(destinations[0, :, 0], "tok")
-    targets, query_rows, key_rows, value_rows, cache_blocks = lax.optimization_barrier(
-        (targets, query_rows, key_rows, value_rows, cache_blocks)
-    )
-    attended = regroup_attend(query_rows, key_rows, value_rows, lengths[0], segments)
-    moved_cache = relocate(cache_blocks, targets)
+    targets, cache_blocks = lax.optimization_barrier((targets, cache_blocks))
+    by_head = relocate_by_head(cache_blocks)
+    by_head, query_rows, key_rows, value_rows = lax.optimization_barrier(
+        (by_head, query_rows, key_rows, value_rows)
+    )
+    outgoing = place_slots(by_head, targets)
+    query_t, key_t, value_t = to_heads(query_rows), to_heads(key_rows), to_heads(value_rows)
+    outgoing, query_t, key_t, value_t = lax.optimization_barrier((outgoing, query_t, key_t, value_t))
+    moved_cache = relocate_groups(outgoing)
+    attended_t = attend_local(query_t, key_t, value_t, lengths[0], segments)
+    moved_cache, attended_t = lax.optimization_barrier((moved_cache, attended_t))
+    attended = from_heads(attended_t)
     return (attended, moved_cache)
 
 

time: 439 us -> 427 us (0.973)
  the two profiles are of different devices: /device:TPU:1 before, /device:TPU:16 now
where the time goes in v3:
time: 427 us; the launch traced here: 426 us
  waiting for transfers between devices  154 us (36%)
  Pallas kernels  101 us (24%)
  blocking collectives  74.9 us (18%)
  local copies, waits for them, and re-layouts  63.2 us (15%)
  starting transfers between devices  23.3 us (5%)
  matrix products  7.13 us (2%)
    all_to_all x3, waiting for transfers between devices, to_heads(): lax.all_to_all(split, 'tok', split_axis=1, concat_axis=1, tiled=True)  119 us
    pallas_call x1, Pallas kernels, attend_local(): pl.pallas_call(attention_kernel, out_shape=jax.ShapeDtypeStruct(query_t.s...  101 us
    all_to_all x1, blocking collectives, relocate_by_head(): return lax.all_to_all(split, 'tok', split_axis=2, concat_axis=2, tiled=True)  49.4 us
    all_to_all x1, waiting for transfers between devices, from_heads(): lax.all_to_all(by_source, 'tok', split_axis=1, concat_axis=1, tiled=True)  34.5 us
    all_gather x1, blocking collectives, on_device(): targets = lax.all_gather(destinations[0, :, 0], 'tok')  25.5 us
    optimization_barrier x3, local copies, waits for them, and re-layouts, on_device(): lax.optimization_barrier((by_head, query_rows, key_rows, value_rows))  17.8 us
    unnamed x8, local copies, waits for them, and re-layouts  17.6 us
    all_to_all x3, starting transfers between devices, to_heads(): lax.all_to_all(split, 'tok', split_axis=1, concat_axis=1, tiled=True)  13.6 us
  transfers between devices with their start and end apart: 5, of which 4 were waited for; matrix products, arithmetic and copies ran while one was open for 8% of the time, Pallas kernels for 24%

profile of v3, /device:TPU:16, one launch (start us, length us, event | category | flops | bytes accessed | tf_op | source)
XLA Modules:
  0.0 425.5 jit_solution(13457124977743656262)
XLA Ops:
  0.6 25.5 %all-gather = s32[16,8,1]{1,2,0:T(1,128)S(1)} all-gather(s32[1,8,1]{1,2,0:T(1,128)} %param.11), channel_id=2, replica_groups=mesh['tok'=16,'req'=8] {'tok'}, dimensions={0}, use_global_device_ids=true | all-gather | bytes 544 | tf_op jit(solution)/shard_map/all_gather | solution.py:179
  26.1 0.1 copy.38
  26.2 8.1 %reshape_squeeze.12 = bf16[8,2,16,2,3584]{4,3,2,1,0:T(2,128)(2,1)} reshape(bf16[1,8,2,32,3584]{4,3,2,1,0:T(8,128)(2,1)} %param.10) | data formatting | bytes 7340032 | tf_op jit(solution)/shard_map/reshape;squeeze | solution.py:150
  34.3 5.1 %copy.39 = bf16[8,2,16,2,3584]{4,0,3,1,2:T(8,128)(2,1)S(1)} copy(bf16[8,2,16,2,3584]{4,3,2,1,0:T(2,128)(2,1)} %reshape_squeeze.12) | data formatting | bytes 7340032 | tf_op jit(solution)/shard_map/reshape;squeeze | solution.py:150
  39.4 49.4 %all_to_all.30 = bf16[8,2,16,2,3584]{4,0,3,1,2:T(8,128)(2,1)} all-to-all(bf16[8,2,16,2,3584]{4,0,3,1,2:T(8,128)(2,1)S(1)} %copy.39), channel_id=1, replica_groups=mesh['tok'=16,'req'=8] {'tok'}, dimensions={2} | all-to-all | bytes 7340032 | tf_op jit(solution)/shard_map/all_to_all | solution.py:151
  88.8 5.9 %copy.44 = bf16[1,256,7168]{1,2,0:T(8,128)(2,1)} copy(bf16[1,256,7168]{2,1,0:T(8,128)(2,1)} %param.8) | data formatting | bytes 7340032 | tf_op jit(solution)/shard_map/optimization_barrier | solution.py:182
  94.7 4.5 %all-to-all-start.3 = ((bf16[256,16,448]{0,2,1:T(8,128)(2,1)}), bf16[256,16,448]{0,2,1:T(8,128)(2,1)}, u32[]{:S(2)}, u32[]{:S(2)}) async-start(bf16[256,16,448]{0,2,1:T(8,128)(2,1)} %bitcast.36), calls=%async_computation.3 | async-start | bytes 7340032 | tf_op jit(solution)/shard_map/all_to_all | solution.py:135
  99.2 5.9 %copy.42 = bf16[1,256,7168]{1,2,0:T(8,128)(2,1)} copy(bf16[1,256,7168]{2,1,0:T(8,128)(2,1)} %param.6) | data formatting | bytes 7340032 | tf_op jit(solution)/shard_map/optimization_barrier | solution.py:182
  105.1 40.3 %all-to-all-done.3 = bf16[256,16,448]{0,2,1:T(8,128)(2,1)} async-done(((bf16[256,16,448]{0,2,1:T(8,128)(2,1)}), bf16[256,16,448]{0,2,1:T(8,128)(2,1)}, u32[]{:S(2)}, u32[]{:S(2)}) %all-to-all-start.3) | async-done | bytes 3670048 | tf_op jit(solution)/shard_map/all_to_all | solution.py:135
  145.4 4.5 %all-to-all-start.1 = ((bf16[256,16,448]{0,2,1:T(8,128)(2,1)}), bf16[256,16,448]{0,2,1:T(8,128)(2,1)}, u32[]{:S(2)}, u32[]{:S(2)}) async-start(bf16[256,16,448]{0,2,1:T(8,128)(2,1)} %bitcast.35), calls=%async_computation.1 | async-start | bytes 7340032 | tf_op jit(solution)/shard_map/all_to_all | solution.py:135
  150.0 5.9 %copy.43 = bf16[1,256,7168]{1,2,0:T(8,128)(2,1)} copy(bf16[1,256,7168]{2,1,0:T(8,128)(2,1)} %param.7) | data formatting | bytes 7340032 | tf_op jit(solution)/shard_map/optimization_barrier | solution.py:182
  155.9 40.3 %all-to-all-done.1 = bf16[256,16,448]{0,2,1:T(8,128)(2,1)} async-done(((bf16[256,16,448]{0,2,1:T(8,128)(2,1)}), bf16[256,16,448]{0,2,1:T(8,128)(2,1)}, u32[]{:S(2)}, u32[]{:S(2)}) %all-to-all-start.1) | async-done | bytes 3670048 | tf_op jit(solution)/shard_map/all_to_all | solution.py:135
  196.2 4.5 %all-to-all-start.2 = ((bf16[256,16,448]{0,2,1:T(8,128)(2,1)}), bf16[256,16,448]{0,2,1:T(8,128)(2,1)}, u32[]{:S(2)}, u32[]{:S(2)}) async-start(bf16[256,16,448]{0,2,1:T(8,128)(2,1)} %bitcast.34), calls=%async_computation.2 | async-start | bytes 7340032 | tf_op jit(solution)/shard_map/all_to_all | solution.py:135
  200.7 0.1 copy.40
  200.8 0.1 convert_reduce_fusion.1
  200.9 7.1 %fusion = bf16[8,2,2,16,2,3584]{5,0,1,4,2,3:T(8,128)(2,1)} fusion(bf16[8,2,16,2,3584]{4,0,3,1,2:T(8,128)(2,1)} %all_to_all.30, pred[16,8,2]{1,2,0:T(4,128)(4,1)S(1)} %iota_compare_fusion.2, pred[16,8,8]{1,2,0:T(8,128)(4,1)S(1)} %iota_compare_fusion.1), kind=kOutput, calls=%fused_computation.1 | convolution fusion | flops 62392320 | bytes 11011328 | tf_op jit(solution)/shard_map/tbgc,bktjy->gcktjy/dot_general | solution.py:166
  208.1 38.9 %all-to-all-done.2 = bf16[256,16,448]{0,2,1:T(8,128)(2,1)} async-done(((bf16[256,16,448]{0,2,1:T(8,128)(2,1)}), bf16[256,16,448]{0,2,1:T(8,128)(2,1)}, u32[]{:S(2)}, u32[]{:S(2)}) %all-to-all-start.2) | async-done | bytes 3670048 | tf_op jit(solution)/shard_map/all_to_all | solution.py:135
  246.9 11.8 %copy.45 = bf16[8,2,2,16,2,3584]{5,1,4,2,3,0:T(2,128)(2,1)} copy(bf16[8,2,2,16,2,3584]{5,0,1,4,2,3:T(8,128)(2,1)} %fusion) | data formatting | bytes 14680064 | tf_op jit(solution)/shard_map/optimization_barrier | solution.py:187
  258.7 0.0 copy-start.1
  258.7 5.2 %all-to-all-start.4 = ((bf16[8,2,2,16,2,3584]{5,1,4,2,3,0:T(2,128)(2,1)}), bf16[8,2,2,16,2,3584]{5,1,4,2,3,0:T(2,128)(2,1)}, u32[]{:S(2)}, u32[]{:S(2)}) async-start(bf16[8,2,2,16,2,3584]{5,1,4,2,3,0:T(2,128)(2,1)} %copy.45), calls=%async_computation.4 | async-start | bytes 14680064 | tf_op jit(solution)/shard_map/all_to_all | solution.py:172
  263.9 0.0 copy-done.1
  263.9 0.2 reduce-window.4
  264.1 0.1 convert_reduce_fusion
  264.2 0.0 copy-start
  264.2 0.1 slice.6.seg_first_ref
  264.3 0.0 copy-start.2
  264.3 0.6 slice.7.seg_last_ref
  265.0 2.0 copy.46.qseg_ref
  266.9 0.1 select_reduce_fusion
  267.0 0.5 and_select_fusion.first_ref
  267.5 0.0 copy-done
  267.6 0.0 copy-done.2
  267.6 101.3 %shard_map.77 = bf16[16,448,256]{2,1,0:T(8,128)(2,1)} custom-call(s32[16]{0:T(128)} %and_select_fusion.first_ref, s32[16]{0:T(128)} %copy-done.2, s32[16]{0:T(128)} %slice.7.seg_last_ref, bf16[16,448,256]{2,1,0:T(8,128)(2,1)} %bitcast.7.q_ref, bf16[16,448,256]{2,1,0:T(8,128)(2,1)} %bitcast.9.k_ref, bf16[16,448,256]{2,1,0:T(8,128)(2,1)} %bitcast.11.v_ref, ...), custom_call_target="tpu_custom_call" | custom-call | flops 15032385536 | bytes 14680064 | tf_op jit(solution)/shard_map/pallas_call | solution.py:105
  368.9 0.0 all-to-all-done.4
  368.9 4.5 %all-to-all-start.5 = ((bf16[256,16,448]{0,2,1:T(8,128)(2,1)}), bf16[256,16,448]{0,2,1:T(8,128)(2,1)}, u32[]{:S(2)}, u32[]{:S(2)}) async-start(bf16[256,16,448]{0,2,1:T(8,128)(2,1)} %bitcast.37), calls=%async_computation.5 | async-start | bytes 7340032 | tf_op jit(solution)/shard_map/all_to_all | solution.py:142
  373.4 11.7 %copy.48 = bf16[1,8,2,2,16,2,3584]{6,5,4,3,2,1,0:T(2,128)(2,1)} copy(bf16[1,8,2,2,16,2,3584]{6,2,5,3,4,1,0:T(2,128)(2,1)} %bitcast.12) | data formatting | bytes 14680064
  385.1 34.5 %all-to-all-done.5 = bf16[256,16,448]{0,2,1:T(8,128)(2,1)} async-done(((bf16[256,16,448]{0,2,1:T(8,128)(2,1)}), bf16[256,16,448]{0,2,1:T(8,128)(2,1)}, u32[]{:S(2)}, u32[]{:S(2)}) %all-to-all-start.5) | async-done | bytes 3670048 | tf_op jit(solution)/shard_map/all_to_all | solution.py:142
  419.6 5.9 %copy.47 = bf16[1,256,7168]{2,1,0:T(8,128)(2,1)} copy(bf16[1,256,7168]{1,2,0:T(8,128)(2,1)} %bitcast.20) | data formatting | bytes 7340032
  (4 shorter events, 0.0 us)
Async XLA Ops:
  94.7 50.7 %all-to-all-start.3 = ((bf16[256,16,448]{0,2,1:T(8,128)(2,1)}), bf16[256,16,448]{0,2,1:T(8,128)(2,1)}, u32[]{:S(2)}, u32[]{:S(2)}) async-start(bf16[256,16,448]{0,2,1:T(8,128)(2,1)} %bitcast.36), calls=%async_computation.3 | async-start | bytes 7340032 | tf_op jit(solution)/shard_map/all_to_all | solution.py:135
  145.4 50.7 %all-to-all-start.1 = ((bf16[256,16,448]{0,2,1:T(8,128)(2,1)}), bf16[256,16,448]{0,2,1:T(8,128)(2,1)}, u32[]{:S(2)}, u32[]{:S(2)}) async-start(bf16[256,16,448]{0,2,1:T(8,128)(2,1)} %bitcast.35), calls=%async_computation.1 | async-start | bytes 7340032 | tf_op jit(solution)/shard_map/all_to_all | solution.py:135
  196.2 50.7 %all-to-all-start.2 = ((bf16[256,16,448]{0,2,1:T(8,128)(2,1)}), bf16[256,16,448]{0,2,1:T(8,128)(2,1)}, u32[]{:S(2)}, u32[]{:S(2)}) async-start(bf16[256,16,448]{0,2,1:T(8,128)(2,1)} %bitcast.34), calls=%async_computation.2 | async-start | bytes 7340032 | tf_op jit(solution)/shard_map/all_to_all | solution.py:135
  258.7 5.2 %copy-start.1 = (s32[1,6]{1,0:T(1,128)S(1)}, s32[1,6]{1,0:T(1,128)}, u32[]{:S(2)}) copy-start(s32[1,6]{1,0:T(1,128)} %param.9) | copy-start | bytes 76
  258.7 110.2 %all-to-all-start.4 = ((bf16[8,2,2,16,2,3584]{5,1,4,2,3,0:T(2,128)(2,1)}), bf16[8,2,2,16,2,3584]{5,1,4,2,3,0:T(2,128)(2,1)}, u32[]{:S(2)}, u32[]{:S(2)}) async-start(bf16[8,2,2,16,2,3584]{5,1,4,2,3,0:T(2,128)(2,1)} %copy.45), calls=%async_computation.4 | async-start | bytes 14680064 | tf_op jit(solution)/shard_map/all_to_all | solution.py:172
  264.2 3.3 copy-start
  264.3 3.2 copy-start.2
  368.9 50.7 %all-to-all-start.5 = ((bf16[256,16,448]{0,2,1:T(8,128)(2,1)}), bf16[256,16,448]{0,2,1:T(8,128)(2,1)}, u32[]{:S(2)}, u32[]{:S(2)}) async-start(bf16[256,16,448]{0,2,1:T(8,128)(2,1)} %bitcast.37), calls=%async_computation.5 | async-start | bytes 7340032 | tf_op jit(solution)/shard_map/all_to_all | solution.py:142

commit v4 on v3

--- a/solution.py
+++ b/solution.py
@@ -19,45 +19,57 @@
 
 
 def attention_kernel(first_ref, seg_first_ref, seg_last_ref, q_ref, k_ref, v_ref, qseg_ref, kseg_ref, o_ref,
-                     m_ref, l_ref, acc_ref, q_sc):
+                     m_ref, l_ref, acc_ref, k_sc):
     qi = pl.program_id(0)
-    width, rows = q_ref.shape[1], q_ref.shape[2]
+    chunks, width, rows = k_ref.shape
     heads_here = width // HD
-    eye_rows = lax.broadcasted_iota(jnp.int32, (rows, rows), 0) == lax.broadcasted_iota(jnp.int32, (rows, rows), 1)
-    eye = eye_rows.astype(jnp.bfloat16)
     nt = (((1,), (1,)), ((), ()))
-    for h in range(heads_here):
-        q_sc[h] = lax.dot_general(
-            eye, q_ref[0, h * HD:(h + 1) * HD, :], nt, preferred_element_type=jnp.float32
+
+    @pl.when(qi == 0)
+    def _():
+        eye = (
+            lax.broadcasted_iota(jnp.int32, (rows, rows), 0) == lax.broadcasted_iota(jnp.int32, (rows, rows), 1)
         ).astype(jnp.bfloat16)
+
+        def fill(c, carry):
+            start = pl.multiple_of(c * rows, rows)
+            for h in range(heads_here):
+                k_sc[h, pl.ds(start, rows), :] = lax.dot_general(
+                    eye, k_ref[c, h * HD:(h + 1) * HD, :], nt, preferred_element_type=jnp.float32
+                ).astype(jnp.bfloat16)
+            return carry
+
+        lax.fori_loop(0, chunks, fill, 0)
+
     m_ref[...] = jnp.full(m_ref.shape, NEG, jnp.float32)
     l_ref[...] = jnp.zeros(l_ref.shape, jnp.float32)
     acc_ref[...] = jnp.zeros(acc_ref.shape, jnp.float32)
     scale = HD ** (-0.5)
     query_seg = qseg_ref[...]
-    query_pos = qi * rows + lax.broadcasted_iota(jnp.int32, (rows, 1), 0)
+    query_pos = qi * rows + lax.broadcasted_iota(jnp.int32, (1, rows), 1)
 
     def step(kb, masked):
+        start = pl.multiple_of(kb * rows, rows)
         if masked:
-            key_seg = kseg_ref[kb]
-            key_pos = kb * rows + lax.broadcasted_iota(jnp.int32, (1, rows), 1)
-            visible = (query_seg == key_seg) & (query_pos >= key_pos)
+            key_seg = kseg_ref[pl.ds(start, rows), :]
+            key_pos = start + lax.broadcasted_iota(jnp.int32, (rows, 1), 0)
+            visible = (key_seg == query_seg) & (key_pos <= query_pos)
         for h in range(heads_here):
-            keys = k_ref[kb, h * HD:(h + 1) * HD, :]
-            scores = jnp.dot(q_sc[h], keys, preferred_element_type=jnp.float32) * scale
+            keys = k_sc[h, pl.ds(start, rows), :]
+            scores = jnp.dot(keys, q_ref[0, h * HD:(h + 1) * HD, :], preferred_element_type=jnp.float32) * scale
             if masked:
                 scores = jnp.where(visible, scores, NEG)
             m_old = m_ref[h]
-            m_new = jnp.maximum(m_old, jnp.max(scores, axis=1, keepdims=True))
+            m_new = jnp.maximum(m_old, jnp.max(scores, axis=0, keepdims=True))
             alpha = jnp.exp(m_old - m_new)
             weights = jnp.exp(scores - m_new)
             if masked:
                 weights = jnp.where(visible, weights, 0.0)
-            l_ref[h] = alpha * l_ref[h] + jnp.sum(weights, axis=1, keepdims=True)
+            l_ref[h] = alpha * l_ref[h] + jnp.sum(weights, axis=0, keepdims=True)
             m_ref[h] = m_new
             values = v_ref[kb, h * HD:(h + 1) * HD, :]
-            acc_ref[h] = alpha * acc_ref[h] + lax.dot_general(
-                weights.astype(jnp.bfloat16), values, nt, preferred_element_type=jnp.float32
+            acc_ref[h] = alpha * acc_ref[h] + jnp.dot(
+                values, weights.astype(jnp.bfloat16), preferred_element_type=jnp.float32
             )
 
     def body(kb, carry):
@@ -74,12 +86,8 @@
         return carry
 
     lax.fori_loop(first_ref[qi], qi + 1, body, 0)
-    eye_out = (lax.broadcasted_iota(jnp.int32, (HD, HD), 0) == lax.broadcasted_iota(jnp.int32, (HD, HD), 1)).astype(jnp.bfloat16)
     for h in range(heads_here):
-        out_rows = (acc_ref[h] / l_ref[h]).astype(jnp.bfloat16)
-        o_ref[0, h * HD:(h + 1) * HD, :] = lax.dot_general(
-            eye_out, out_rows, nt, preferred_element_type=jnp.float32
-        ).astype(o_ref.dtype)
+        o_ref[0, h * HD:(h + 1) * HD, :] = (acc_ref[h] / l_ref[h]).astype(o_ref.dtype)
 
 
 def attend_local(query_t, key_t, value_t, lengths_row, segments):
@@ -94,8 +102,8 @@
         jnp.where(seg_first[:, None] == jnp.arange(lengths_row.shape[0])[None, :], starts[None, :], 0), axis=1
     )
     first_chunk = (first_start // rows).astype(jnp.int32)
-    qseg = segments.reshape(length, 1)
-    kseg = segments.reshape(chunks, 1, rows)
+    qseg = segments.reshape(chunks, 1, rows)
+    kseg = segments.reshape(length, 1)
     visible_pairs = length * length // 2
     cost = pl.CostEstimate(
         flops=int(4 * visible_pairs * width),
@@ -112,15 +120,15 @@
                 pl.BlockSpec((1, width, rows), lambda i, *_: (i, 0, 0)),
                 pl.BlockSpec((chunks, width, rows), lambda i, *_: (0, 0, 0), pipeline_mode=pl.Buffered(1)),
                 pl.BlockSpec((chunks, width, rows), lambda i, *_: (0, 0, 0), pipeline_mode=pl.Buffered(1)),
-                pl.BlockSpec((rows, 1), lambda i, *_: (i, 0)),
-                pl.BlockSpec((chunks, 1, rows), lambda i, *_: (0, 0, 0)),
+                pl.BlockSpec((None, 1, rows), lambda i, *_: (i, 0, 0)),
+                pl.BlockSpec((length, 1), lambda i, *_: (0, 0), pipeline_mode=pl.Buffered(1)),
             ],
             out_specs=pl.BlockSpec((1, width, rows), lambda i, *_: (i, 0, 0)),
             scratch_shapes=[
-                pltpu.VMEM((heads_here, rows, 1), jnp.float32),
-                pltpu.VMEM((heads_here, rows, 1), jnp.float32),
-                pltpu.VMEM((heads_here, rows, HD), jnp.float32),
-                pltpu.VMEM((heads_here, rows, HD), jnp.bfloat16),
+                pltpu.VMEM((heads_here, 1, rows), jnp.float32),
+                pltpu.VMEM((heads_here, 1, rows), jnp.float32),
+                pltpu.VMEM((heads_here, HD, rows), jnp.float32),
+                pltpu.VMEM((heads_here, length, HD), jnp.bfloat16),
             ],
         ),
         compiler_params=pltpu.CompilerParams(dimension_semantics=("arbitrary",)),
@@ -176,7 +184,12 @@
 def on_device(query_rows, key_rows, value_rows, lengths, cache_blocks, destinations):
     span_length = query_rows.shape[1] * lax.axis_size("tok")
     segments = segment_ids(lengths[0], span_length)
-    targets = lax.all_gather(destinations[0, :, 0], "tok")
+    tok_count = lax.axis_size("tok")
+    own_targets = destinations[0, :, 0]
+    targets = lax.all_to_all(
+        jnp.broadcast_to(own_targets[None, :], (tok_count, own_targets.shape[0])),
+        "tok", split_axis=0, concat_axis=0, tiled=True,
+    )
     targets, cache_blocks = lax.optimization_barrier((targets, cache_blocks))
     by_head = relocate_by_head(cache_blocks)
     by_head, query_rows, key_rows, value_rows = lax.optimization_barrier(

time: 427 us -> 395 us (0.925)
  the two profiles are of different devices: /device:TPU:16 before, /device:TPU:1 now
where the time goes in v4:
time: 395 us; the launch traced here: 394 us
  waiting for transfers between devices  176 us (45%)
  blocking collectives  65 us (16%)
  local copies, waits for them, and re-layouts  63.8 us (16%)
  Pallas kernels  54.1 us (14%)
  starting transfers between devices  25.7 us (7%)
  matrix products  7.13 us (2%)
    all_to_all x3, waiting for transfers between devices, to_heads(): lax.all_to_all(split, 'tok', split_axis=1, concat_axis=1, tiled=True)  117 us
    pallas_call x1, Pallas kernels, attend_local(): pl.pallas_call(attention_kernel, out_shape=jax.ShapeDtypeStruct(query_t.s...  54.1 us
    all_to_all x1, blocking collectives, relocate_by_head(): return lax.all_to_all(split, 'tok', split_axis=2, concat_axis=2, tiled=True)  48.9 us
    all_to_all x1, waiting for transfers between devices, from_heads(): lax.all_to_all(by_source, 'tok', split_axis=1, concat_axis=1, tiled=True)  33.9 us
    all_to_all x1, waiting for transfers between devices, relocate_groups(): lax.all_to_all(outgoing, 'req', split_axis=0, concat_axis=0, tiled=True)  24.9 us
    optimization_barrier x3, local copies, waits for them, and re-layouts, on_device(): lax.optimization_barrier((by_head, query_rows, key_rows, value_rows))  17.7 us
    unnamed x8, local copies, waits for them, and re-layouts  17.6 us
    all_to_all x1, blocking collectives, on_device(): lax.all_to_all(jnp.broadcast_to(own_targets[None, :], (tok_count, own_tar...  16.1 us
  transfers between devices with their start and end apart: 5, of which 5 were waited for; matrix products, arithmetic and copies ran while one was open for 9% of the time, Pallas kernels for 14%

profile of v4, /device:TPU:1, one launch (start us, length us, event | category | flops | bytes accessed | tf_op | source)
XLA Modules:
  0.0 393.7 jit_solution(8469228410704065700)
XLA Ops:
  0.6 0.7 broadcast_in_dim.17
  1.3 16.1 %all_to_all.39 = s32[16,1,8]{2,1,0:T(1,128)S(1)} all-to-all(s32[16,1,8]{2,1,0:T(1,128)S(1)} %broadcast_in_dim.17), channel_id=1, replica_groups=mesh['tok'=16,'req'=8] {'tok'}, dimensions={0} | all-to-all | bytes 1024 | tf_op jit(solution)/shard_map/all_to_all | solution.py:189
  17.4 0.1 copy.36
  17.4 8.1 %reshape_squeeze.12 = bf16[8,2,16,2,3584]{4,3,2,1,0:T(2,128)(2,1)} reshape(bf16[1,8,2,32,3584]{4,3,2,1,0:T(8,128)(2,1)} %param.10) | data formatting | bytes 7340032 | tf_op jit(solution)/shard_map/reshape;squeeze | solution.py:158
  25.5 5.1 %copy.37 = bf16[8,2,16,2,3584]{4,0,3,1,2:T(8,128)(2,1)S(1)} copy(bf16[8,2,16,2,3584]{4,3,2,1,0:T(2,128)(2,1)} %reshape_squeeze.12) | data formatting | bytes 7340032 | tf_op jit(solution)/shard_map/reshape;squeeze | solution.py:158
  30.6 48.9 %all_to_all.40 = bf16[8,2,16,2,3584]{4,0,3,1,2:T(8,128)(2,1)} all-to-all(bf16[8,2,16,2,3584]{4,0,3,1,2:T(8,128)(2,1)S(1)} %copy.37), channel_id=1, replica_groups=mesh['tok'=16,'req'=8] {'tok'}, dimensions={2} | all-to-all | bytes 7340032 | tf_op jit(solution)/shard_map/all_to_all | solution.py:159
  79.5 5.9 %copy.41 = bf16[1,256,7168]{1,2,0:T(8,128)(2,1)} copy(bf16[1,256,7168]{2,1,0:T(8,128)(2,1)} %param.7) | data formatting | bytes 7340032 | tf_op jit(solution)/shard_map/optimization_barrier | solution.py:195
  85.4 5.4 %all-to-all-start.3 = ((bf16[256,16,448]{0,2,1:T(8,128)(2,1)}), bf16[256,16,448]{0,2,1:T(8,128)(2,1)}, u32[]{:S(2)}, u32[]{:S(2)}) async-start(bf16[256,16,448]{0,2,1:T(8,128)(2,1)} %bitcast.37), calls=%async_computation.3 | async-start | bytes 7340032 | tf_op jit(solution)/shard_map/all_to_all | solution.py:143
  90.8 5.9 %copy.42 = bf16[1,256,7168]{1,2,0:T(8,128)(2,1)} copy(bf16[1,256,7168]{2,1,0:T(8,128)(2,1)} %param.8) | data formatting | bytes 7340032 | tf_op jit(solution)/shard_map/optimization_barrier | solution.py:195
  96.8 39.6 %all-to-all-done.3 = bf16[256,16,448]{0,2,1:T(8,128)(2,1)} async-done(((bf16[256,16,448]{0,2,1:T(8,128)(2,1)}), bf16[256,16,448]{0,2,1:T(8,128)(2,1)}, u32[]{:S(2)}, u32[]{:S(2)}) %all-to-all-start.3) | async-done | bytes 3670048 | tf_op jit(solution)/shard_map/all_to_all | solution.py:143
  136.4 5.2 %all-to-all-start.4 = ((bf16[256,16,448]{0,2,1:T(8,128)(2,1)}), bf16[256,16,448]{0,2,1:T(8,128)(2,1)}, u32[]{:S(2)}, u32[]{:S(2)}) async-start(bf16[256,16,448]{0,2,1:T(8,128)(2,1)} %bitcast.36), calls=%async_computation.4 | async-start | bytes 7340032 | tf_op jit(solution)/shard_map/all_to_all | solution.py:143
  141.6 5.9 %copy.40 = bf16[1,256,7168]{1,2,0:T(8,128)(2,1)} copy(bf16[1,256,7168]{2,1,0:T(8,128)(2,1)} %param.6) | data formatting | bytes 7340032 | tf_op jit(solution)/shard_map/optimization_barrier | solution.py:195
  147.5 39.6 %all-to-all-done.4 = bf16[256,16,448]{0,2,1:T(8,128)(2,1)} async-done(((bf16[256,16,448]{0,2,1:T(8,128)(2,1)}), bf16[256,16,448]{0,2,1:T(8,128)(2,1)}, u32[]{:S(2)}, u32[]{:S(2)}) %all-to-all-start.4) | async-done | bytes 3670048 | tf_op jit(solution)/shard_map/all_to_all | solution.py:143
  187.1 5.2 %all-to-all-start.2 = ((bf16[256,16,448]{0,2,1:T(8,128)(2,1)}), bf16[256,16,448]{0,2,1:T(8,128)(2,1)}, u32[]{:S(2)}, u32[]{:S(2)}) async-start(bf16[256,16,448]{0,2,1:T(8,128)(2,1)} %bitcast.35), calls=%async_computation.2 | async-start | bytes 7340032 | tf_op jit(solution)/shard_map/all_to_all | solution.py:143
  192.3 0.1 copy.38
  192.4 0.1 convert_reduce_fusion.1
  192.6 7.1 %fusion = bf16[8,2,2,16,2,3584]{5,0,1,4,2,3:T(8,128)(2,1)} fusion(bf16[8,2,16,2,3584]{4,0,3,1,2:T(8,128)(2,1)} %all_to_all.40, pred[16,8,2]{1,2,0:T(4,128)(4,1)S(1)} %iota_compare_fusion.2, pred[16,8,8]{1,2,0:T(8,128)(4,1)S(1)} %iota_compare_fusion.1), kind=kOutput, calls=%fused_computation.1 | convolution fusion | flops 62392320 | bytes 11011328 | tf_op jit(solution)/shard_map/tbgc,bktjy->gcktjy/dot_general | solution.py:174
  199.7 38.2 %all-to-all-done.2 = bf16[256,16,448]{0,2,1:T(8,128)(2,1)} async-done(((bf16[256,16,448]{0,2,1:T(8,128)(2,1)}), bf16[256,16,448]{0,2,1:T(8,128)(2,1)}, u32[]{:S(2)}, u32[]{:S(2)}) %all-to-all-start.2) | async-done | bytes 3670048 | tf_op jit(solution)/shard_map/all_to_all | solution.py:143
  237.9 11.8 %copy.43 = bf16[8,2,2,16,2,3584]{5,1,4,2,3,0:T(2,128)(2,1)} copy(bf16[8,2,2,16,2,3584]{5,0,1,4,2,3:T(8,128)(2,1)} %fusion) | data formatting | bytes 14680064 | tf_op jit(solution)/shard_map/optimization_barrier | solution.py:200
  249.7 0.0 copy-start.1
  249.7 5.0 %all-to-all-start.5 = ((bf16[8,2,2,16,2,3584]{5,1,4,2,3,0:T(2,128)(2,1)}), bf16[8,2,2,16,2,3584]{5,1,4,2,3,0:T(2,128)(2,1)}, u32[]{:S(2)}, u32[]{:S(2)}) async-start(bf16[8,2,2,16,2,3584]{5,1,4,2,3,0:T(2,128)(2,1)} %copy.43), calls=%async_computation.5 | async-start | bytes 14680064 | tf_op jit(solution)/shard_map/all_to_all | solution.py:180
  254.7 0.0 copy-done.1
  254.7 0.2 reduce-window.4
  254.9 0.1 convert_reduce_fusion
  255.0 0.0 copy-start
  255.0 0.1 slice.6.seg_first_ref
  255.1 0.0 copy-start.2
  255.1 0.6 slice.7.seg_last_ref
  255.7 2.0 copy.44.kseg_ref
  257.7 0.1 select_reduce_fusion
  257.8 0.5 and_select_fusion.first_ref
  258.3 0.0 copy-done
  258.3 0.0 copy-done.2
  258.3 54.1 %shard_map.77 = bf16[16,448,256]{2,1,0:T(8,128)(2,1)} custom-call(s32[16]{0:T(128)} %and_select_fusion.first_ref, s32[16]{0:T(128)} %copy-done.2, s32[16]{0:T(128)} %slice.7.seg_last_ref, bf16[16,448,256]{2,1,0:T(8,128)(2,1)} %bitcast.8.q_ref, bf16[16,448,256]{2,1,0:T(8,128)(2,1)} %bitcast.10.k_ref, bf16[16,448,256]{2,1,0:T(8,128)(2,1)} %bitcast.12.v_ref, ...), custom_call_target="tpu_custom_call" | custom-call | flops 15032385536 | bytes 14680064 | tf_op jit(solution)/shard_map/pallas_call | solution.py:113
  312.4 24.9 %all-to-all-done.5 = bf16[8,2,2,16,2,3584]{5,1,4,2,3,0:T(2,128)(2,1)} async-done(((bf16[8,2,2,16,2,3584]{5,1,4,2,3,0:T(2,128)(2,1)}), bf16[8,2,2,16,2,3584]{5,1,4,2,3,0:T(2,128)(2,1)}, u32[]{:S(2)}, u32[]{:S(2)}) %all-to-all-start.5) | async-done | bytes 7340064 | tf_op jit(solution)/shard_map/all_to_all | solution.py:180
  337.3 4.9 %all-to-all-start.6 = ((bf16[256,16,448]{0,2,1:T(8,128)(2,1)}), bf16[256,16,448]{0,2,1:T(8,128)(2,1)}, u32[]{:S(2)}, u32[]{:S(2)}) async-start(bf16[256,16,448]{0,2,1:T(8,128)(2,1)} %bitcast.38), calls=%async_computation.6 | async-start | bytes 7340032 | tf_op jit(solution)/shard_map/all_to_all | solution.py:150
  342.2 11.7 %copy.46 = bf16[1,8,2,2,16,2,3584]{6,5,4,3,2,1,0:T(2,128)(2,1)} copy(bf16[1,8,2,2,16,2,3584]{6,2,5,3,4,1,0:T(2,128)(2,1)} %bitcast.13) | data formatting | bytes 14680064
  353.9 33.9 %all-to-all-done.6 = bf16[256,16,448]{0,2,1:T(8,128)(2,1)} async-done(((bf16[256,16,448]{0,2,1:T(8,128)(2,1)}), bf16[256,16,448]{0,2,1:T(8,128)(2,1)}, u32[]{:S(2)}, u32[]{:S(2)}) %all-to-all-start.6) | async-done | bytes 3670048 | tf_op jit(solution)/shard_map/all_to_all | solution.py:150
  387.7 5.9 %copy.45 = bf16[1,256,7168]{2,1,0:T(8,128)(2,1)} copy(bf16[1,256,7168]{1,2,0:T(8,128)(2,1)} %bitcast.21) | data formatting | bytes 7340032
  (4 shorter events, 0.0 us)
Async XLA Ops:
  85.4 51.0 %all-to-all-start.3 = ((bf16[256,16,448]{0,2,1:T(8,128)(2,1)}), bf16[256,16,448]{0,2,1:T(8,128)(2,1)}, u32[]{:S(2)}, u32[]{:S(2)}) async-start(bf16[256,16,448]{0,2,1:T(8,128)(2,1)} %bitcast.37), calls=%async_computation.3 | async-start | bytes 7340032 | tf_op jit(solution)/shard_map/all_to_all | solution.py:143
  136.4 50.7 %all-to-all-start.4 = ((bf16[256,16,448]{0,2,1:T(8,128)(2,1)}), bf16[256,16,448]{0,2,1:T(8,128)(2,1)}, u32[]{:S(2)}, u32[]{:S(2)}) async-start(bf16[256,16,448]{0,2,1:T(8,128)(2,1)} %bitcast.36), calls=%async_computation.4 | async-start | bytes 7340032 | tf_op jit(solution)/shard_map/all_to_all | solution.py:143
  187.1 50.7 %all-to-all-start.2 = ((bf16[256,16,448]{0,2,1:T(8,128)(2,1)}), bf16[256,16,448]{0,2,1:T(8,128)(2,1)}, u32[]{:S(2)}, u32[]{:S(2)}) async-start(bf16[256,16,448]{0,2,1:T(8,128)(2,1)} %bitcast.35), calls=%async_computation.2 | async-start | bytes 7340032 | tf_op jit(solution)/shard_map/all_to_all | solution.py:143
  249.7 5.0 %copy-start.1 = (s32[1,6]{1,0:T(1,128)S(1)}, s32[1,6]{1,0:T(1,128)}, u32[]{:S(2)}) copy-start(s32[1,6]{1,0:T(1,128)} %param.9) | copy-start | bytes 76
  249.7 87.6 %all-to-all-start.5 = ((bf16[8,2,2,16,2,3584]{5,1,4,2,3,0:T(2,128)(2,1)}), bf16[8,2,2,16,2,3584]{5,1,4,2,3,0:T(2,128)(2,1)}, u32[]{:S(2)}, u32[]{:S(2)}) async-start(bf16[8,2,2,16,2,3584]{5,1,4,2,3,0:T(2,128)(2,1)} %copy.43), calls=%async_computation.5 | async-start | bytes 14680064 | tf_op jit(solution)/shard_map/all_to_all | solution.py:180
  255.0 3.3 copy-start
  255.1 3.2 copy-start.2
  337.3 50.5 %all-to-all-start.6 = ((bf16[256,16,448]{0,2,1:T(8,128)(2,1)}), bf16[256,16,448]{0,2,1:T(8,128)(2,1)}, u32[]{:S(2)}, u32[]{:S(2)}) async-start(bf16[256,16,448]{0,2,1:T(8,128)(2,1)} %bitcast.38), calls=%async_computation.6 | async-start | bytes 7340032 | tf_op jit(solution)/shard_map/all_to_all | solution.py:150

commit v5 on v4

--- a/solution.py
+++ b/solution.py
@@ -190,13 +190,11 @@
         jnp.broadcast_to(own_targets[None, :], (tok_count, own_targets.shape[0])),
         "tok", split_axis=0, concat_axis=0, tiled=True,
     )
-    targets, cache_blocks = lax.optimization_barrier((targets, cache_blocks))
+    query_t = to_heads(query_rows)
     by_head = relocate_by_head(cache_blocks)
-    by_head, query_rows, key_rows, value_rows = lax.optimization_barrier(
-        (by_head, query_rows, key_rows, value_rows)
-    )
+    by_head, key_rows, value_rows = lax.optimization_barrier((by_head, key_rows, value_rows))
     outgoing = place_slots(by_head, targets)
-    query_t, key_t, value_t = to_heads(query_rows), to_heads(key_rows), to_heads(value_rows)
+    key_t, value_t = to_heads(key_rows), to_heads(value_rows)
     outgoing, query_t, key_t, value_t = lax.optimization_barrier((outgoing, query_t, key_t, value_t))
     moved_cache = relocate_groups(outgoing)
     attended_t = attend_local(query_t, key_t, value_t, lengths[0], segments)

time: 395 us -> 388 us (0.982)
  blocking collectives: 65 us -> 0 us
  waiting for transfers between devices: 176 us -> 211 us
  starting transfers between devices: 25.7 us -> 42 us
  Pallas kernels: 54.1 us -> 58.8 us
    all_to_all x2 -> x0, blocking collectives: 65 us -> none  [the longest x1 48.9 us: relocate_by_head(): return lax.all_to_all(split, 'tok', split_axis=2, concat_axis=2, tiled=True)]
    all_to_all x0 -> x2, waiting for transfers between devices: none -> 39.6 us  [the longest x1 39.6 us: relocate_by_head(): return lax.all_to_all(split, 'tok', split_axis=2, concat_axis=2, tiled=True)]
    all_to_all x0 -> x2, starting transfers between devices: none -> 16.5 us  [the longest x1 9.29 us: on_device(): lax.all_to_all(jnp.broadcast_to(own_targets[None, :], (tok_count, own_tar...]
    optimization_barrier x4 -> x2, local copies, waits for them, and re-layouts: 17.8 us -> 11.8 us  [on_device(): lax.optimization_barrier((by_head, key_rows, value_rows))]
    unnamed x8 -> x9, local copies, waits for them, and re-layouts: 17.6 us -> 23.5 us
    all_to_all x1, waiting for transfers between devices: 24.9 us -> 20 us  [relocate_groups(): lax.all_to_all(outgoing, 'req', split_axis=0, concat_axis=0, tiled=True)]
    pallas_call x1, Pallas kernels: 54.1 us -> 58.8 us  [attend_local(): pl.pallas_call(attention_kernel, out_shape=jax.ShapeDtypeStruct(query_t.s...]
  transfers between devices with their start and end apart: 5 -> 7, of which waited for: 5 -> 6; matrix products, arithmetic and copies ran while one was open for 9% -> 14% of each run, Pallas kernels for 14% -> 15%
where the time goes in v5:
time: 388 us; the launch traced here: 387 us
  waiting for transfers between devices  211 us (54%)
  local copies, waits for them, and re-layouts  66.1 us (17%)
  Pallas kernels  58.8 us (15%)
  starting transfers between devices  42 us (11%)
  matrix products  7.13 us (2%)
    all_to_all x3, waiting for transfers between devices, to_heads(): lax.all_to_all(split, 'tok', split_axis=1, concat_axis=1, tiled=True)  118 us
    pallas_call x1, Pallas kernels, attend_local(): pl.pallas_call(attention_kernel, out_shape=jax.ShapeDtypeStruct(query_t.s...  58.8 us
    all_to_all x1, waiting for transfers between devices, relocate_by_head(): return lax.all_to_all(split, 'tok', split_axis=2, concat_axis=2, tiled=True)  39.6 us
    all_to_all x1, waiting for transfers between devices, from_heads(): lax.all_to_all(by_source, 'tok', split_axis=1, concat_axis=1, tiled=True)  33.9 us
    unnamed x9, local copies, waits for them, and re-layouts  23.5 us
    all_to_all x1, waiting for transfers between devices, relocate_groups(): lax.all_to_all(outgoing, 'req', split_axis=0, concat_axis=0, tiled=True)  20 us
    all_to_all x3, starting transfers between devices, to_heads(): lax.all_to_all(split, 'tok', split_axis=1, concat_axis=1, tiled=True)  15.5 us
    another operation x2, local copies, waits for them, and re-layouts, relocate_by_head(): local_blocks.reshape(block_count, kv_count, tok_count, heads_all // tok_c...  15 us
  transfers between devices with their start and end apart: 7, of which 6 were waited for; matrix products, arithmetic and copies ran while one was open for 14% of the time, Pallas kernels for 15%

profile of v5, /device:TPU:1, one launch (start us, length us, event | category | flops | bytes accessed | tf_op | source)
XLA Modules:
  0.0 386.8 jit_solution(6610607478620129072)
XLA Ops:
  0.6 1.3 broadcast_in_dim.17
  1.9 9.3 %all-to-all-start.1 = ((s32[16,1,8]{2,1,0:T(1,128)}), s32[16,1,8]{2,1,0:T(1,128)S(1)}, u32[]{:S(2)}, u32[]{:S(2)}) async-start(s32[16,1,8]{2,1,0:T(1,128)} %broadcast_in_dim.17), calls=%async_computation.1 | async-start | bytes 16384 | tf_op jit(solution)/shard_map/all_to_all | solution.py:189
  11.2 8.1 %reshape_squeeze.12 = bf16[8,2,16,2,3584]{4,3,2,1,0:T(2,128)(2,1)} reshape(bf16[1,8,2,32,3584]{4,3,2,1,0:T(8,128)(2,1)} %param.10) | data formatting | bytes 7340032 | tf_op jit(solution)/shard_map/reshape;squeeze | solution.py:158
  19.3 6.9 %copy.36 = bf16[8,2,16,2,3584]{4,0,3,1,2:T(8,128)(2,1)} copy(bf16[8,2,16,2,3584]{4,3,2,1,0:T(2,128)(2,1)} %reshape_squeeze.12) | data formatting | bytes 7340032 | tf_op jit(solution)/shard_map/reshape;squeeze | solution.py:158
  26.2 0.0 all-to-all-done.1
  26.2 7.2 %all-to-all-start = ((bf16[8,2,16,2,3584]{4,0,3,1,2:T(8,128)(2,1)}), bf16[8,2,16,2,3584]{4,0,3,1,2:T(8,128)(2,1)}, u32[]{:S(2)}, u32[]{:S(2)}) async-start(bf16[8,2,16,2,3584]{4,0,3,1,2:T(8,128)(2,1)} %copy.36), calls=%async_computation | async-start | bytes 7340032 | tf_op jit(solution)/shard_map/all_to_all | solution.py:159
  33.4 5.9 %copy.40 = bf16[1,256,7168]{1,2,0:T(8,128)(2,1)} copy(bf16[1,256,7168]{2,1,0:T(8,128)(2,1)} %param.6) | data formatting | bytes 7340032 | tf_op args[0]
  39.3 39.6 %all-to-all-done = bf16[8,2,16,2,3584]{4,0,3,1,2:T(8,128)(2,1)} async-done(((bf16[8,2,16,2,3584]{4,0,3,1,2:T(8,128)(2,1)}), bf16[8,2,16,2,3584]{4,0,3,1,2:T(8,128)(2,1)}, u32[]{:S(2)}, u32[]{:S(2)}) %all-to-all-start) | async-done | bytes 3670048 | tf_op jit(solution)/shard_map/all_to_all | solution.py:159
  78.9 5.2 %all-to-all-start.2 = ((bf16[256,16,448]{0,2,1:T(8,128)(2,1)}), bf16[256,16,448]{0,2,1:T(8,128)(2,1)}, u32[]{:S(2)}, u32[]{:S(2)}) async-start(bf16[256,16,448]{0,2,1:T(8,128)(2,1)} %bitcast.40), calls=%async_computation.2 | async-start | bytes 7340032 | tf_op jit(solution)/shard_map/all_to_all | solution.py:143
  84.1 5.9 %copy.41 = bf16[1,256,7168]{1,2,0:T(8,128)(2,1)} copy(bf16[1,256,7168]{2,1,0:T(8,128)(2,1)} %param.7) | data formatting | bytes 7340032 | tf_op jit(solution)/shard_map/optimization_barrier | solution.py:195
  90.0 39.6 %all-to-all-done.2 = bf16[256,16,448]{0,2,1:T(8,128)(2,1)} async-done(((bf16[256,16,448]{0,2,1:T(8,128)(2,1)}), bf16[256,16,448]{0,2,1:T(8,128)(2,1)}, u32[]{:S(2)}, u32[]{:S(2)}) %all-to-all-start.2) | async-done | bytes 3670048 | tf_op jit(solution)/shard_map/all_to_all | solution.py:143
  129.6 5.2 %all-to-all-start.3 = ((bf16[256,16,448]{0,2,1:T(8,128)(2,1)}), bf16[256,16,448]{0,2,1:T(8,128)(2,1)}, u32[]{:S(2)}, u32[]{:S(2)}) async-start(bf16[256,16,448]{0,2,1:T(8,128)(2,1)} %bitcast.41), calls=%async_computation.3 | async-start | bytes 7340032 | tf_op jit(solution)/shard_map/all_to_all | solution.py:143
  134.8 5.9 %copy.42 = bf16[1,256,7168]{1,2,0:T(8,128)(2,1)} copy(bf16[1,256,7168]{2,1,0:T(8,128)(2,1)} %param.8) | data formatting | bytes 7340032 | tf_op jit(solution)/shard_map/optimization_barrier | solution.py:195
  140.7 39.6 %all-to-all-done.3 = bf16[256,16,448]{0,2,1:T(8,128)(2,1)} async-done(((bf16[256,16,448]{0,2,1:T(8,128)(2,1)}), bf16[256,16,448]{0,2,1:T(8,128)(2,1)}, u32[]{:S(2)}, u32[]{:S(2)}) %all-to-all-start.3) | async-done | bytes 3670048 | tf_op jit(solution)/shard_map/all_to_all | solution.py:143
  180.4 5.2 %all-to-all-start.4 = ((bf16[256,16,448]{0,2,1:T(8,128)(2,1)}), bf16[256,16,448]{0,2,1:T(8,128)(2,1)}, u32[]{:S(2)}, u32[]{:S(2)}) async-start(bf16[256,16,448]{0,2,1:T(8,128)(2,1)} %bitcast.39), calls=%async_computation.4 | async-start | bytes 7340032 | tf_op jit(solution)/shard_map/all_to_all | solution.py:143
  185.5 0.1 convert_reduce_fusion.1
  185.7 7.1 %fusion = bf16[8,2,2,16,2,3584]{5,0,1,4,2,3:T(8,128)(2,1)} fusion(bf16[8,2,16,2,3584]{4,0,3,1,2:T(8,128)(2,1)} %all-to-all-done, pred[16,8,2]{1,2,0:T(4,128)(4,1)S(1)} %iota_compare_fusion.2, pred[16,8,8]{1,2,0:T(8,128)(4,1)S(1)} %iota_compare_fusion.1), kind=kOutput, calls=%fused_computation.1 | convolution fusion | flops 62392320 | bytes 11011328 | tf_op jit(solution)/shard_map/tbgc,bktjy->gcktjy/dot_general | solution.py:174
  192.8 38.3 %all-to-all-done.4 = bf16[256,16,448]{0,2,1:T(8,128)(2,1)} async-done(((bf16[256,16,448]{0,2,1:T(8,128)(2,1)}), bf16[256,16,448]{0,2,1:T(8,128)(2,1)}, u32[]{:S(2)}, u32[]{:S(2)}) %all-to-all-start.4) | async-done | bytes 3670048 | tf_op jit(solution)/shard_map/all_to_all | solution.py:143
  231.1 11.8 %copy.43 = bf16[8,2,2,16,2,3584]{5,1,4,2,3,0:T(2,128)(2,1)} copy(bf16[8,2,2,16,2,3584]{5,0,1,4,2,3:T(8,128)(2,1)} %fusion) | data formatting | bytes 14680064 | tf_op jit(solution)/shard_map/optimization_barrier | solution.py:198
  242.9 0.0 copy-start.1
  242.9 5.0 %all-to-all-start.5 = ((bf16[8,2,2,16,2,3584]{5,1,4,2,3,0:T(2,128)(2,1)}), bf16[8,2,2,16,2,3584]{5,1,4,2,3,0:T(2,128)(2,1)}, u32[]{:S(2)}, u32[]{:S(2)}) async-start(bf16[8,2,2,16,2,3584]{5,1,4,2,3,0:T(2,128)(2,1)} %copy.43), calls=%async_computation.5 | async-start | bytes 14680064 | tf_op jit(solution)/shard_map/all_to_all | solution.py:180
  247.9 0.0 copy-done.1
  247.9 0.2 reduce-window.4
  248.1 0.1 convert_reduce_fusion
  248.2 0.0 copy-start
  248.2 0.1 slice.6.seg_first_ref
  248.3 0.0 copy-start.2
  248.3 0.7 slice.7.seg_last_ref
  249.0 2.0 copy.44.kseg_ref
  250.9 0.1 select_reduce_fusion
  251.0 0.5 and_select_fusion.first_ref
  251.5 0.0 copy-done
  251.5 0.0 copy-done.2
  251.5 58.8 %shard_map.77 = bf16[16,448,256]{2,1,0:T(8,128)(2,1)} custom-call(s32[16]{0:T(128)} %and_select_fusion.first_ref, s32[16]{0:T(128)} %copy-done.2, s32[16]{0:T(128)} %slice.7.seg_last_ref, bf16[16,448,256]{2,1,0:T(8,128)(2,1)} %bitcast.10.q_ref, bf16[16,448,256]{2,1,0:T(8,128)(2,1)} %bitcast.12.k_ref, bf16[16,448,256]{2,1,0:T(8,128)(2,1)} %bitcast.14.v_ref, ...), custom_call_target="tpu_custom_call" | custom-call | flops 15032385536 | bytes 14680064 | tf_op jit(solution)/shard_map/pallas_call | solution.py:113
  310.4 20.0 %all-to-all-done.5 = bf16[8,2,2,16,2,3584]{5,1,4,2,3,0:T(2,128)(2,1)} async-done(((bf16[8,2,2,16,2,3584]{5,1,4,2,3,0:T(2,128)(2,1)}), bf16[8,2,2,16,2,3584]{5,1,4,2,3,0:T(2,128)(2,1)}, u32[]{:S(2)}, u32[]{:S(2)}) %all-to-all-start.5) | async-done | bytes 7340064 | tf_op jit(solution)/shard_map/all_to_all | solution.py:180
  330.4 4.9 %all-to-all-start.6 = ((bf16[256,16,448]{0,2,1:T(8,128)(2,1)}), bf16[256,16,448]{0,2,1:T(8,128)(2,1)}, u32[]{:S(2)}, u32[]{:S(2)}) async-start(bf16[256,16,448]{0,2,1:T(8,128)(2,1)} %bitcast.42), calls=%async_computation.6 | async-start | bytes 7340032 | tf_op jit(solution)/shard_map/all_to_all | solution.py:150
  335.3 11.7 %copy.46 = bf16[1,8,2,2,16,2,3584]{6,5,4,3,2,1,0:T(2,128)(2,1)} copy(bf16[1,8,2,2,16,2,3584]{6,2,5,3,4,1,0:T(2,128)(2,1)} %bitcast.15) | data formatting | bytes 14680064
  347.0 33.9 %all-to-all-done.6 = bf16[256,16,448]{0,2,1:T(8,128)(2,1)} async-done(((bf16[256,16,448]{0,2,1:T(8,128)(2,1)}), bf16[256,16,448]{0,2,1:T(8,128)(2,1)}, u32[]{:S(2)}, u32[]{:S(2)}) %all-to-all-start.6) | async-done | bytes 3670048 | tf_op jit(solution)/shard_map/all_to_all | solution.py:150
  380.9 5.9 %copy.45 = bf16[1,256,7168]{2,1,0:T(8,128)(2,1)} copy(bf16[1,256,7168]{1,2,0:T(8,128)(2,1)} %bitcast.23) | data formatting | bytes 7340032
  (4 shorter events, 0.0 us)
Async XLA Ops:
  1.9 24.3 %all-to-all-start.1 = ((s32[16,1,8]{2,1,0:T(1,128)}), s32[16,1,8]{2,1,0:T(1,128)S(1)}, u32[]{:S(2)}, u32[]{:S(2)}) async-start(s32[16,1,8]{2,1,0:T(1,128)} %broadcast_in_dim.17), calls=%async_computation.1 | async-start | bytes 16384 | tf_op jit(solution)/shard_map/all_to_all | solution.py:189
  26.2 52.7 %all-to-all-start = ((bf16[8,2,16,2,3584]{4,0,3,1,2:T(8,128)(2,1)}), bf16[8,2,16,2,3584]{4,0,3,1,2:T(8,128)(2,1)}, u32[]{:S(2)}, u32[]{:S(2)}) async-start(bf16[8,2,16,2,3584]{4,0,3,1,2:T(8,128)(2,1)} %copy.36), calls=%async_computation | async-start | bytes 7340032 | tf_op jit(solution)/shard_map/all_to_all | solution.py:159
  78.9 50.7 %all-to-all-start.2 = ((bf16[256,16,448]{0,2,1:T(8,128)(2,1)}), bf16[256,16,448]{0,2,1:T(8,128)(2,1)}, u32[]{:S(2)}, u32[]{:S(2)}) async-start(bf16[256,16,448]{0,2,1:T(8,128)(2,1)} %bitcast.40), calls=%async_computation.2 | async-start | bytes 7340032 | tf_op jit(solution)/shard_map/all_to_all | solution.py:143
  129.6 50.7 %all-to-all-start.3 = ((bf16[256,16,448]{0,2,1:T(8,128)(2,1)}), bf16[256,16,448]{0,2,1:T(8,128)(2,1)}, u32[]{:S(2)}, u32[]{:S(2)}) async-start(bf16[256,16,448]{0,2,1:T(8,128)(2,1)} %bitcast.41), calls=%async_computation.3 | async-start | bytes 7340032 | tf_op jit(solution)/shard_map/all_to_all | solution.py:143
  180.4 50.7 %all-to-all-start.4 = ((bf16[256,16,448]{0,2,1:T(8,128)(2,1)}), bf16[256,16,448]{0,2,1:T(8,128)(2,1)}, u32[]{:S(2)}, u32[]{:S(2)}) async-start(bf16[256,16,448]{0,2,1:T(8,128)(2,1)} %bitcast.39), calls=%async_computation.4 | async-start | bytes 7340032 | tf_op jit(solution)/shard_map/all_to_all | solution.py:143
  242.9 5.0 %copy-start.1 = (s32[1,6]{1,0:T(1,128)S(1)}, s32[1,6]{1,0:T(1,128)}, u32[]{:S(2)}) copy-start(s32[1,6]{1,0:T(1,128)} %param.9) | copy-start | bytes 76
  242.9 87.5 %all-to-all-start.5 = ((bf16[8,2,2,16,2,3584]{5,1,4,2,3,0:T(2,128)(2,1)}), bf16[8,2,2,16,2,3584]{5,1,4,2,3,0:T(2,128)(2,1)}, u32[]{:S(2)}, u32[]{:S(2)}) async-start(bf16[8,2,2,16,2,3584]{5,1,4,2,3,0:T(2,128)(2,1)} %copy.43), calls=%async_computation.5 | async-start | bytes 14680064 | tf_op jit(solution)/shard_map/all_to_all | solution.py:180
  248.2 3.4 copy-start
  248.3 3.3 copy-start.2
  330.4 50.5 %all-to-all-start.6 = ((bf16[256,16,448]{0,2,1:T(8,128)(2,1)}), bf16[256,16,448]{0,2,1:T(8,128)(2,1)}, u32[]{:S(2)}, u32[]{:S(2)}) async-start(bf16[256,16,448]{0,2,1:T(8,128)(2,1)} %bitcast.42), calls=%async_computation.6 | async-start | bytes 7340032 | tf_op jit(solution)/shard_map/all_to_all | solution.py:150

commit v6 on v5

--- a/solution.py
+++ b/solution.py
@@ -185,12 +185,13 @@
     span_length = query_rows.shape[1] * lax.axis_size("tok")
     segments = segment_ids(lengths[0], span_length)
     tok_count = lax.axis_size("tok")
+    query_t = to_heads(query_rows)
+    query_t, destinations = lax.optimization_barrier((query_t, destinations))
     own_targets = destinations[0, :, 0]
     targets = lax.all_to_all(
         jnp.broadcast_to(own_targets[None, :], (tok_count, own_targets.shape[0])),
         "tok", split_axis=0, concat_axis=0, tiled=True,
     )
-    query_t = to_heads(query_rows)
     by_head = relocate_by_head(cache_blocks)
     by_head, key_rows, value_rows = lax.optimization_barrier((by_head, key_rows, value_rows))
     outgoing = place_slots(by_head, targets)

time: 388 us -> 383 us (0.987)
    all_to_all x3, waiting for transfers between devices: 118 us -> 108 us  [to_heads(): lax.all_to_all(split, 'tok', split_axis=1, concat_axis=1, tiled=True)]
    all_to_all x1, waiting for transfers between devices: 39.6 us -> 45.6 us  [relocate_by_head(): return lax.all_to_all(split, 'tok', split_axis=2, concat_axis=2, tiled=True)]
    all_to_all x3, starting transfers between devices: 15.5 us -> 20.7 us  [to_heads(): lax.all_to_all(split, 'tok', split_axis=1, concat_axis=1, tiled=True)]
    all_to_all x1, starting transfers between devices: 9.29 us -> 4.19 us  [on_device(): lax.all_to_all(jnp.broadcast_to(own_targets[None, :], (tok_count, own_tar...]
    unnamed x9 -> x11, local copies, waits for them, and re-layouts: 23.5 us -> 23.5 us
  transfers between devices with their start and end apart: 7 -> 7, of which waited for: 6 -> 7; matrix products, arithmetic and copies ran while one was open for 14% -> 13% of each run, Pallas kernels for 15% -> 16%
where the time goes in v6:
time: 383 us; the launch traced here: 382 us
  waiting for transfers between devices  208 us (54%)
  local copies, waits for them, and re-layouts  65.5 us (17%)
  Pallas kernels  59.6 us (16%)
  starting transfers between devices  40 us (10%)
  matrix products  7.13 us (2%)
    all_to_all x3, waiting for transfers between devices, to_heads(): lax.all_to_all(split, 'tok', split_axis=1, concat_axis=1, tiled=True)  108 us
    pallas_call x1, Pallas kernels, attend_local(): pl.pallas_call(attention_kernel, out_shape=jax.ShapeDtypeStruct(query_t.s...  59.6 us
    all_to_all x1, waiting for transfers between devices, relocate_by_head(): return lax.all_to_all(split, 'tok', split_axis=2, concat_axis=2, tiled=True)  45.6 us
    all_to_all x1, waiting for transfers between devices, from_heads(): lax.all_to_all(by_source, 'tok', split_axis=1, concat_axis=1, tiled=True)  33.9 us
    unnamed x11, local copies, waits for them, and re-layouts  23.5 us
    all_to_all x3, starting transfers between devices, to_heads(): lax.all_to_all(split, 'tok', split_axis=1, concat_axis=1, tiled=True)  20.7 us
    all_to_all x1, waiting for transfers between devices, relocate_groups(): lax.all_to_all(outgoing, 'req', split_axis=0, concat_axis=0, tiled=True)  19.2 us
    another operation x2, local copies, waits for them, and re-layouts, relocate_by_head(): local_blocks.reshape(block_count, kv_count, tok_count, heads_all // tok_c...  15 us
  transfers between devices with their start and end apart: 7, of which 7 were waited for; matrix products, arithmetic and copies ran while one was open for 13% of the time, Pallas kernels for 16%

profile of v6, /device:TPU:1, one launch (start us, length us, event | category | flops | bytes accessed | tf_op | source)
XLA Modules:
  0.0 382.0 jit_solution(5167461335248426531)
XLA Ops:
  0.6 5.9 %copy.37 = bf16[1,256,7168]{1,2,0:T(8,128)(2,1)} copy(bf16[1,256,7168]{2,1,0:T(8,128)(2,1)} %param.6) | data formatting | bytes 7340032 | tf_op args[0]
  6.5 9.3 %all-to-all-start.1 = ((bf16[256,16,448]{0,2,1:T(8,128)(2,1)}), bf16[256,16,448]{0,2,1:T(8,128)(2,1)}, u32[]{:S(2)}, u32[]{:S(2)}) async-start(bf16[256,16,448]{0,2,1:T(8,128)(2,1)} %bitcast.41), calls=%async_computation.1 | async-start | bytes 7340032 | tf_op jit(solution)/shard_map/all_to_all | solution.py:143
  15.8 8.1 %reshape_squeeze.12 = bf16[8,2,16,2,3584]{4,3,2,1,0:T(2,128)(2,1)} reshape(bf16[1,8,2,32,3584]{4,3,2,1,0:T(8,128)(2,1)} %param.10) | data formatting | bytes 7340032 | tf_op jit(solution)/shard_map/reshape;squeeze | solution.py:158
  23.9 6.9 %copy.36 = bf16[8,2,16,2,3584]{4,0,3,1,2:T(8,128)(2,1)} copy(bf16[8,2,16,2,3584]{4,3,2,1,0:T(2,128)(2,1)} %reshape_squeeze.12) | data formatting | bytes 7340032 | tf_op jit(solution)/shard_map/reshape;squeeze | solution.py:158
  30.8 0.0 copy-start.1
  30.8 30.5 %all-to-all-done.1 = bf16[256,16,448]{0,2,1:T(8,128)(2,1)} async-done(((bf16[256,16,448]{0,2,1:T(8,128)(2,1)}), bf16[256,16,448]{0,2,1:T(8,128)(2,1)}, u32[]{:S(2)}, u32[]{:S(2)}) %all-to-all-start.1) | async-done | bytes 3670048 | tf_op jit(solution)/shard_map/all_to_all | solution.py:143
  61.3 5.2 %all-to-all-start = ((bf16[8,2,16,2,3584]{4,0,3,1,2:T(8,128)(2,1)}), bf16[8,2,16,2,3584]{4,0,3,1,2:T(8,128)(2,1)}, u32[]{:S(2)}, u32[]{:S(2)}) async-start(bf16[8,2,16,2,3584]{4,0,3,1,2:T(8,128)(2,1)} %copy.36), calls=%async_computation | async-start | bytes 7340032 | tf_op jit(solution)/shard_map/all_to_all | solution.py:159
  66.5 45.6 %all-to-all-done = bf16[8,2,16,2,3584]{4,0,3,1,2:T(8,128)(2,1)} async-done(((bf16[8,2,16,2,3584]{4,0,3,1,2:T(8,128)(2,1)}), bf16[8,2,16,2,3584]{4,0,3,1,2:T(8,128)(2,1)}, u32[]{:S(2)}, u32[]{:S(2)}) %all-to-all-start) | async-done | bytes 3670048 | tf_op jit(solution)/shard_map/all_to_all | solution.py:159
  112.0 0.0 copy-done.1
  112.0 0.6 broadcast_in_dim.17
  112.6 4.2 %all-to-all-start.2 = ((s32[16,1,8]{2,1,0:T(1,128)}), s32[16,1,8]{2,1,0:T(1,128)S(1)}, u32[]{:S(2)}, u32[]{:S(2)}) async-start(s32[16,1,8]{2,1,0:T(1,128)} %broadcast_in_dim.17), calls=%async_computation.2 | async-start | bytes 16384 | tf_op jit(solution)/shard_map/all_to_all | solution.py:191
  116.8 5.9 %copy.41 = bf16[1,256,7168]{1,2,0:T(8,128)(2,1)} copy(bf16[1,256,7168]{2,1,0:T(8,128)(2,1)} %param.7) | data formatting | bytes 7340032 | tf_op jit(solution)/shard_map/optimization_barrier | solution.py:196
  122.7 1.1 all-to-all-done.2
  123.8 6.2 %all-to-all-start.3 = ((bf16[256,16,448]{0,2,1:T(8,128)(2,1)}), bf16[256,16,448]{0,2,1:T(8,128)(2,1)}, u32[]{:S(2)}, u32[]{:S(2)}) async-start(bf16[256,16,448]{0,2,1:T(8,128)(2,1)} %bitcast.40), calls=%async_computation.3 | async-start | bytes 7340032 | tf_op jit(solution)/shard_map/all_to_all | solution.py:143
  130.0 5.9 %copy.42 = bf16[1,256,7168]{1,2,0:T(8,128)(2,1)} copy(bf16[1,256,7168]{2,1,0:T(8,128)(2,1)} %param.8) | data formatting | bytes 7340032 | tf_op jit(solution)/shard_map/optimization_barrier | solution.py:196
  136.0 39.5 %all-to-all-done.3 = bf16[256,16,448]{0,2,1:T(8,128)(2,1)} async-done(((bf16[256,16,448]{0,2,1:T(8,128)(2,1)}), bf16[256,16,448]{0,2,1:T(8,128)(2,1)}, u32[]{:S(2)}, u32[]{:S(2)}) %all-to-all-start.3) | async-done | bytes 3670048 | tf_op jit(solution)/shard_map/all_to_all | solution.py:143
  175.5 5.2 %all-to-all-start.4 = ((bf16[256,16,448]{0,2,1:T(8,128)(2,1)}), bf16[256,16,448]{0,2,1:T(8,128)(2,1)}, u32[]{:S(2)}, u32[]{:S(2)}) async-start(bf16[256,16,448]{0,2,1:T(8,128)(2,1)} %bitcast.39), calls=%async_computation.4 | async-start | bytes 7340032 | tf_op jit(solution)/shard_map/all_to_all | solution.py:143
  180.7 0.1 convert_reduce_fusion.1
  180.8 7.1 %fusion = bf16[8,2,2,16,2,3584]{5,0,1,4,2,3:T(8,128)(2,1)} fusion(bf16[8,2,16,2,3584]{4,0,3,1,2:T(8,128)(2,1)} %all-to-all-done, pred[16,8,2]{1,2,0:T(4,128)(4,1)S(1)} %iota_compare_fusion.2, pred[16,8,8]{1,2,0:T(8,128)(4,1)S(1)} %iota_compare_fusion.1), kind=kOutput, calls=%fused_computation.1 | convolution fusion | flops 62392320 | bytes 11011328 | tf_op jit(solution)/shard_map/tbgc,bktjy->gcktjy/dot_general | solution.py:174
  188.0 38.3 %all-to-all-done.4 = bf16[256,16,448]{0,2,1:T(8,128)(2,1)} async-done(((bf16[256,16,448]{0,2,1:T(8,128)(2,1)}), bf16[256,16,448]{0,2,1:T(8,128)(2,1)}, u32[]{:S(2)}, u32[]{:S(2)}) %all-to-all-start.4) | async-done | bytes 3670048 | tf_op jit(solution)/shard_map/all_to_all | solution.py:143
  226.2 11.8 %copy.43 = bf16[8,2,2,16,2,3584]{5,1,4,2,3,0:T(2,128)(2,1)} copy(bf16[8,2,2,16,2,3584]{5,0,1,4,2,3:T(8,128)(2,1)} %fusion) | data formatting | bytes 14680064 | tf_op jit(solution)/shard_map/optimization_barrier | solution.py:199
  238.0 0.0 copy-start.2
  238.0 5.0 %all-to-all-start.5 = ((bf16[8,2,2,16,2,3584]{5,1,4,2,3,0:T(2,128)(2,1)}), bf16[8,2,2,16,2,3584]{5,1,4,2,3,0:T(2,128)(2,1)}, u32[]{:S(2)}, u32[]{:S(2)}) async-start(bf16[8,2,2,16,2,3584]{5,1,4,2,3,0:T(2,128)(2,1)} %copy.43), calls=%async_computation.5 | async-start | bytes 14680064 | tf_op jit(solution)/shard_map/all_to_all | solution.py:180
  243.1 0.0 copy-done.2
  243.1 0.2 reduce-window.4
  243.3 0.1 convert_reduce_fusion
  243.4 0.0 copy-start
  243.4 0.1 slice.6.seg_first_ref
  243.5 0.0 copy-start.3
  243.5 0.7 slice.7.seg_last_ref
  244.2 2.0 copy.44.kseg_ref
  246.1 0.1 select_reduce_fusion
  246.2 0.5 and_select_fusion.first_ref
  246.7 0.0 copy-done
  246.7 0.0 copy-done.3
  246.7 59.6 %shard_map.77 = bf16[16,448,256]{2,1,0:T(8,128)(2,1)} custom-call(s32[16]{0:T(128)} %and_select_fusion.first_ref, s32[16]{0:T(128)} %copy-done.3, s32[16]{0:T(128)} %slice.7.seg_last_ref, bf16[16,448,256]{2,1,0:T(8,128)(2,1)} %bitcast.3.q_ref, bf16[16,448,256]{2,1,0:T(8,128)(2,1)} %bitcast.12.k_ref, bf16[16,448,256]{2,1,0:T(8,128)(2,1)} %bitcast.14.v_ref, ...), custom_call_target="tpu_custom_call" | custom-call | flops 15032385536 | bytes 14680064 | tf_op jit(solution)/shard_map/pallas_call | solution.py:113
  306.4 19.2 %all-to-all-done.5 = bf16[8,2,2,16,2,3584]{5,1,4,2,3,0:T(2,128)(2,1)} async-done(((bf16[8,2,2,16,2,3584]{5,1,4,2,3,0:T(2,128)(2,1)}), bf16[8,2,2,16,2,3584]{5,1,4,2,3,0:T(2,128)(2,1)}, u32[]{:S(2)}, u32[]{:S(2)}) %all-to-all-start.5) | async-done | bytes 7340064 | tf_op jit(solution)/shard_map/all_to_all | solution.py:180
  325.6 5.0 %all-to-all-start.6 = ((bf16[256,16,448]{0,2,1:T(8,128)(2,1)}), bf16[256,16,448]{0,2,1:T(8,128)(2,1)}, u32[]{:S(2)}, u32[]{:S(2)}) async-start(bf16[256,16,448]{0,2,1:T(8,128)(2,1)} %bitcast.42), calls=%async_computation.6 | async-start | bytes 7340032 | tf_op jit(solution)/shard_map/all_to_all | solution.py:150
  330.5 11.7 %copy.46 = bf16[1,8,2,2,16,2,3584]{6,5,4,3,2,1,0:T(2,128)(2,1)} copy(bf16[1,8,2,2,16,2,3584]{6,2,5,3,4,1,0:T(2,128)(2,1)} %bitcast.15) | data formatting | bytes 14680064
  342.2 33.9 %all-to-all-done.6 = bf16[256,16,448]{0,2,1:T(8,128)(2,1)} async-done(((bf16[256,16,448]{0,2,1:T(8,128)(2,1)}), bf16[256,16,448]{0,2,1:T(8,128)(2,1)}, u32[]{:S(2)}, u32[]{:S(2)}) %all-to-all-start.6) | async-done | bytes 3670048 | tf_op jit(solution)/shard_map/all_to_all | solution.py:150
  376.1 5.9 %copy.45 = bf16[1,256,7168]{2,1,0:T(8,128)(2,1)} copy(bf16[1,256,7168]{1,2,0:T(8,128)(2,1)} %bitcast.23) | data formatting | bytes 7340032
  (4 shorter events, 0.0 us)
Async XLA Ops:
  6.5 54.8 %all-to-all-start.1 = ((bf16[256,16,448]{0,2,1:T(8,128)(2,1)}), bf16[256,16,448]{0,2,1:T(8,128)(2,1)}, u32[]{:S(2)}, u32[]{:S(2)}) async-start(bf16[256,16,448]{0,2,1:T(8,128)(2,1)} %bitcast.41), calls=%async_computation.1 | async-start | bytes 7340032 | tf_op jit(solution)/shard_map/all_to_all | solution.py:143
  30.8 81.2 %copy-start.1 = (s32[1,8,1]{1,2,0:T(1,128)S(1)}, s32[1,8,1]{1,2,0:T(1,128)}, u32[]{:S(2)}) copy-start(s32[1,8,1]{1,2,0:T(1,128)} %param.11) | copy-start | bytes 100
  61.3 50.7 %all-to-all-start = ((bf16[8,2,16,2,3584]{4,0,3,1,2:T(8,128)(2,1)}), bf16[8,2,16,2,3584]{4,0,3,1,2:T(8,128)(2,1)}, u32[]{:S(2)}, u32[]{:S(2)}) async-start(bf16[8,2,16,2,3584]{4,0,3,1,2:T(8,128)(2,1)} %copy.36), calls=%async_computation | async-start | bytes 7340032 | tf_op jit(solution)/shard_map/all_to_all | solution.py:159
  112.6 11.2 %all-to-all-start.2 = ((s32[16,1,8]{2,1,0:T(1,128)}), s32[16,1,8]{2,1,0:T(1,128)S(1)}, u32[]{:S(2)}, u32[]{:S(2)}) async-start(s32[16,1,8]{2,1,0:T(1,128)} %broadcast_in_dim.17), calls=%async_computation.2 | async-start | bytes 16384 | tf_op jit(solution)/shard_map/all_to_all | solution.py:191
  123.8 51.7 %all-to-all-start.3 = ((bf16[256,16,448]{0,2,1:T(8,128)(2,1)}), bf16[256,16,448]{0,2,1:T(8,128)(2,1)}, u32[]{:S(2)}, u32[]{:S(2)}) async-start(bf16[256,16,448]{0,2,1:T(8,128)(2,1)} %bitcast.40), calls=%async_computation.3 | async-start | bytes 7340032 | tf_op jit(solution)/shard_map/all_to_all | solution.py:143
  175.5 50.7 %all-to-all-start.4 = ((bf16[256,16,448]{0,2,1:T(8,128)(2,1)}), bf16[256,16,448]{0,2,1:T(8,128)(2,1)}, u32[]{:S(2)}, u32[]{:S(2)}) async-start(bf16[256,16,448]{0,2,1:T(8,128)(2,1)} %bitcast.39), calls=%async_computation.4 | async-start | bytes 7340032 | tf_op jit(solution)/shard_map/all_to_all | solution.py:143
  238.0 5.0 %copy-start.2 = (s32[1,6]{1,0:T(1,128)S(1)}, s32[1,6]{1,0:T(1,128)}, u32[]{:S(2)}) copy-start(s32[1,6]{1,0:T(1,128)} %param.9) | copy-start | bytes 76
  238.0 87.5 %all-to-all-start.5 = ((bf16[8,2,2,16,2,3584]{5,1,4,2,3,0:T(2,128)(2,1)}), bf16[8,2,2,16,2,3584]{5,1,4,2,3,0:T(2,128)(2,1)}, u32[]{:S(2)}, u32[]{:S(2)}) async-start(bf16[8,2,2,16,2,3584]{5,1,4,2,3,0:T(2,128)(2,1)} %copy.43), calls=%async_computation.5 | async-start | bytes 14680064 | tf_op jit(solution)/shard_map/all_to_all | solution.py:180
  243.4 3.4 copy-start
  243.5 3.3 copy-start.3
  325.6 50.5 %all-to-all-start.6 = ((bf16[256,16,448]{0,2,1:T(8,128)(2,1)}), bf16[256,16,448]{0,2,1:T(8,128)(2,1)}, u32[]{:S(2)}, u32[]{:S(2)}) async-start(bf16[256,16,448]{0,2,1:T(8,128)(2,1)} %bitcast.42), calls=%async_computation.6 | async-start | bytes 7340032 | tf_op jit(solution)/shard_map/all_to_all | solution.py:150

commit v7 on v6

--- a/solution.py
+++ b/solution.py
@@ -167,13 +167,14 @@
     slot_rank = jnp.sum(earlier.astype(jnp.int32), axis=2)
     group_ids = jnp.arange(groups, dtype=jnp.int32)
     slot_ids = jnp.arange(CAP, dtype=jnp.int32)
-    placing = (
-        (targets[:, :, None, None] == group_ids[None, None, :, None])
-        & (slot_rank[:, :, None, None] == slot_ids[None, None, None, :])
-    ).astype(by_head.dtype)
-    return jnp.einsum(
-        "tbgc,bktjy->gcktjy", placing, by_head, preferred_element_type=jnp.float32
-    ).astype(by_head.dtype)
+    match = (
+        (targets.T[None, None, :, :] == group_ids[:, None, None, None])
+        & (slot_rank.T[None, None, :, :] == slot_ids[None, :, None, None])
+    )
+    picked = jnp.where(
+        match[:, :, :, None, :, None, None], by_head[None, None], jnp.zeros((), by_head.dtype)
+    )
+    return jnp.sum(picked, axis=2, dtype=by_head.dtype)
 
 
 def relocate_groups(outgoing):

time: 383 us -> 372 us (0.971)
  other arithmetic: 1.03 us -> 17.1 us
  waiting for transfers between devices: 208 us -> 195 us
  local copies, waits for them, and re-layouts: 65.5 us -> 56.6 us
  matrix products: 7.13 us -> 0 us
    reduce_sum x0 -> x1, other arithmetic: none -> 16 us  [place_slots(): return jnp.sum(picked, axis=2, dtype=by_head.dtype)]
    optimization_barrier x1 -> x0, local copies, waits for them, and re-layouts: 11.8 us -> none  [on_device(): lax.optimization_barrier((outgoing, query_t, key_t, value_t))]
    another operation x2 -> x1, local copies, waits for them, and re-layouts: 15 us -> 5.17 us  [relocate_by_head(): local_blocks.reshape(block_count, kv_count, tok_count, heads_all // tok_c...]
    all_to_all x3, waiting for transfers between devices: 108 us -> 99.3 us  [to_heads(): lax.all_to_all(split, 'tok', split_axis=1, concat_axis=1, tiled=True)]
    dot_general x1 -> x0, matrix products: 7.13 us -> none  [place_slots(): jnp.einsum('tbgc,bktjy->gcktjy', placing, by_head, preferred_element_type...]
    unnamed x11 -> x12, local copies, waits for them, and re-layouts: 23.5 us -> 30.4 us
    optimization_barrier x2 -> x3, local copies, waits for them, and re-layouts: 11.8 us -> 17.7 us  [on_device(): lax.optimization_barrier((by_head, key_rows, value_rows))]
  transfers between devices with their start and end apart: 7 -> 7, of which waited for: 7 -> 7; matrix products, arithmetic and copies ran while one was open for 13% -> 17% of each run, Pallas kernels for 16% -> 16%
where the time goes in v7:
time: 372 us; the launch traced here: 370 us
  waiting for transfers between devices  195 us (52%)
  Pallas kernels  60.4 us (16%)
  local copies, waits for them, and re-layouts  56.6 us (15%)
  starting transfers between devices  40.1 us (11%)
  other arithmetic  17.1 us (5%)
    all_to_all x3, waiting for transfers between devices, to_heads(): lax.all_to_all(split, 'tok', split_axis=1, concat_axis=1, tiled=True)  99.3 us
    pallas_call x1, Pallas kernels, attend_local(): pl.pallas_call(attention_kernel, out_shape=jax.ShapeDtypeStruct(query_t.s...  60.4 us
    all_to_all x1, waiting for transfers between devices, relocate_by_head(): return lax.all_to_all(split, 'tok', split_axis=2, concat_axis=2, tiled=True)  45.6 us
    all_to_all x1, waiting for transfers between devices, from_heads(): lax.all_to_all(by_source, 'tok', split_axis=1, concat_axis=1, tiled=True)  31.1 us
    unnamed x12, local copies, waits for them, and re-layouts  30.4 us
    all_to_all x3, starting transfers between devices, to_heads(): lax.all_to_all(split, 'tok', split_axis=1, concat_axis=1, tiled=True)  20.7 us
    all_to_all x1, waiting for transfers between devices, relocate_groups(): lax.all_to_all(outgoing, 'req', split_axis=0, concat_axis=0, tiled=True)  18.5 us
    optimization_barrier x3, local copies, waits for them, and re-layouts, on_device(): lax.optimization_barrier((by_head, key_rows, value_rows))  17.7 us
  transfers between devices with their start and end apart: 7, of which 7 were waited for; matrix products, arithmetic and copies ran while one was open for 17% of the time, Pallas kernels for 16%

profile of v7, /device:TPU:1, one launch (start us, length us, event | category | flops | bytes accessed | tf_op | source)
XLA Modules:
  0.0 370.4 jit_solution(15636630814878587476)
XLA Ops:
  0.6 5.9 %copy.41 = bf16[1,256,7168]{1,2,0:T(8,128)(2,1)} copy(bf16[1,256,7168]{2,1,0:T(8,128)(2,1)} %param.6) | data formatting | bytes 7340032 | tf_op args[0]
  6.5 9.3 %all-to-all-start = ((bf16[256,16,448]{0,2,1:T(8,128)(2,1)}), bf16[256,16,448]{0,2,1:T(8,128)(2,1)}, u32[]{:S(2)}, u32[]{:S(2)}) async-start(bf16[256,16,448]{0,2,1:T(8,128)(2,1)} %bitcast.27), calls=%async_computation | async-start | bytes 7340032 | tf_op jit(solution)/shard_map/all_to_all | solution.py:143
  15.8 4.0 %copy.43 = bf16[1,8,2,32,3584]{4,1,3,2,0:T(8,128)(2,1)S(1)} copy(bf16[1,8,2,32,3584]{4,3,2,1,0:T(8,128)(2,1)} %param.10) | data formatting | bytes 7340032 | tf_op args[4]
  19.9 5.2 %copy.44 = bf16[8,2,16,2,3584]{4,3,1,0,2:T(2,128)(2,1)} copy(bf16[8,2,16,2,3584]{4,0,3,2,1:T(8,128)(2,1)S(1)} %bitcast.28) | data formatting | bytes 7340032 | tf_op jit(solution)/shard_map/reshape;squeeze | solution.py:158
  25.1 0.0 copy-start.1
  25.1 36.3 %all-to-all-done = bf16[256,16,448]{0,2,1:T(8,128)(2,1)} async-done(((bf16[256,16,448]{0,2,1:T(8,128)(2,1)}), bf16[256,16,448]{0,2,1:T(8,128)(2,1)}, u32[]{:S(2)}, u32[]{:S(2)}) %all-to-all-start) | async-done | bytes 3670048 | tf_op jit(solution)/shard_map/all_to_all | solution.py:143
  61.3 5.2 %all-to-all-start.2 = ((bf16[8,2,16,2,3584]{4,3,1,0,2:T(2,128)(2,1)}), bf16[8,2,16,2,3584]{4,3,1,0,2:T(2,128)(2,1)}, u32[]{:S(2)}, u32[]{:S(2)}) async-start(bf16[8,2,16,2,3584]{4,3,1,0,2:T(2,128)(2,1)} %copy.44), calls=%async_computation.2 | async-start | bytes 7340032 | tf_op jit(solution)/shard_map/all_to_all | solution.py:159
  66.5 45.6 %all-to-all-done.2 = bf16[8,2,16,2,3584]{4,3,1,0,2:T(2,128)(2,1)} async-done(((bf16[8,2,16,2,3584]{4,3,1,0,2:T(2,128)(2,1)}), bf16[8,2,16,2,3584]{4,3,1,0,2:T(2,128)(2,1)}, u32[]{:S(2)}, u32[]{:S(2)}) %all-to-all-start.2) | async-done | bytes 3670048 | tf_op jit(solution)/shard_map/all_to_all | solution.py:159
  112.0 0.0 copy-done.1
  112.0 0.6 broadcast_in_dim.60
  112.6 4.2 %all-to-all-start.1 = ((s32[16,1,8]{2,1,0:T(1,128)}), s32[16,1,8]{2,1,0:T(1,128)S(1)}, u32[]{:S(2)}, u32[]{:S(2)}) async-start(s32[16,1,8]{2,1,0:T(1,128)} %broadcast_in_dim.60), calls=%async_computation.1 | async-start | bytes 16384 | tf_op jit(solution)/shard_map/all_to_all | solution.py:192
  116.8 5.9 %copy.47 = bf16[1,256,7168]{1,2,0:T(8,128)(2,1)} copy(bf16[1,256,7168]{2,1,0:T(8,128)(2,1)} %param.8) | data formatting | bytes 7340032 | tf_op jit(solution)/shard_map/optimization_barrier | solution.py:197
  122.7 1.1 all-to-all-done.1
  123.8 6.2 %all-to-all-start.4 = ((bf16[256,16,448]{0,2,1:T(8,128)(2,1)}), bf16[256,16,448]{0,2,1:T(8,128)(2,1)}, u32[]{:S(2)}, u32[]{:S(2)}) async-start(bf16[256,16,448]{0,2,1:T(8,128)(2,1)} %bitcast.26), calls=%async_computation.4 | async-start | bytes 7340032 | tf_op jit(solution)/shard_map/all_to_all | solution.py:143
  130.0 5.9 %copy.46 = bf16[1,256,7168]{1,2,0:T(8,128)(2,1)} copy(bf16[1,256,7168]{2,1,0:T(8,128)(2,1)} %param.7) | data formatting | bytes 7340032 | tf_op jit(solution)/shard_map/optimization_barrier | solution.py:197
  135.9 39.6 %all-to-all-done.4 = bf16[256,16,448]{0,2,1:T(8,128)(2,1)} async-done(((bf16[256,16,448]{0,2,1:T(8,128)(2,1)}), bf16[256,16,448]{0,2,1:T(8,128)(2,1)}, u32[]{:S(2)}, u32[]{:S(2)}) %all-to-all-start.4) | async-done | bytes 3670048 | tf_op jit(solution)/shard_map/all_to_all | solution.py:143
  175.5 5.2 %all-to-all-start.3 = ((bf16[256,16,448]{0,2,1:T(8,128)(2,1)}), bf16[256,16,448]{0,2,1:T(8,128)(2,1)}, u32[]{:S(2)}, u32[]{:S(2)}) async-start(bf16[256,16,448]{0,2,1:T(8,128)(2,1)} %bitcast.25), calls=%async_computation.3 | async-start | bytes 7340032 | tf_op jit(solution)/shard_map/all_to_all | solution.py:143
  180.7 5.9 %copy.45 = bf16[8,2,16,2,3584]{4,2,3,1,0:T(8,128)(2,1)} copy(bf16[8,2,16,2,3584]{4,3,1,0,2:T(2,128)(2,1)} %all-to-all-done.2) | data formatting | bytes 7340032 | tf_op jit(solution)/shard_map/optimization_barrier | solution.py:197
  186.6 0.1 copy.42
  186.7 0.1 convert_reduce_fusion.1
  186.8 16.0 %select_reduce_fusion = bf16[8,2,2,16,2,3584]{5,3,4,2,1,0:T(8,128)(2,1)} fusion(pred[8,2,8,16]{3,2,1,0:T(8,128)(4,1)S(1)} %broadcast_and_fusion, bf16[8,2,16,2,3584]{4,2,3,1,0:T(8,128)(2,1)} %copy.45), kind=kLoop, calls=%fused_computation | loop fusion | flops 55050240 | bytes 11012096 | tf_op jit(solution)/shard_map/reduce_sum | solution.py:177
  202.8 23.5 %all-to-all-done.3 = bf16[256,16,448]{0,2,1:T(8,128)(2,1)} async-done(((bf16[256,16,448]{0,2,1:T(8,128)(2,1)}), bf16[256,16,448]{0,2,1:T(8,128)(2,1)}, u32[]{:S(2)}, u32[]{:S(2)}) %all-to-all-start.3) | async-done | bytes 3670048 | tf_op jit(solution)/shard_map/all_to_all | solution.py:143
  226.3 0.0 copy-start.2
  226.3 5.2 %all-to-all-start.5 = ((bf16[8,2,2,16,2,3584]{5,3,4,2,1,0:T(8,128)(2,1)}), bf16[8,2,2,16,2,3584]{5,3,4,2,1,0:T(8,128)(2,1)}, u32[]{:S(2)}, u32[]{:S(2)}) async-start(bf16[8,2,2,16,2,3584]{5,3,4,2,1,0:T(8,128)(2,1)} %select_reduce_fusion), calls=%async_computation.5 | async-start | bytes 14680064 | tf_op jit(solution)/shard_map/all_to_all | solution.py:181
  231.4 0.0 copy-done.2
  231.4 0.2 reduce-window.4
  231.6 0.1 convert_reduce_fusion
  231.7 0.0 copy-start
  231.7 0.1 slice.6.seg_first_ref
  231.8 0.0 copy-start.3
  231.9 0.6 slice.7.seg_last_ref
  232.5 2.0 copy.48.kseg_ref
  234.4 0.1 select_reduce_fusion.1
  234.5 0.6 and_select_fusion.first_ref
  235.1 0.0 copy-done
  235.1 0.0 copy-done.3
  235.1 60.4 %shard_map.77 = bf16[16,448,256]{2,1,0:T(8,128)(2,1)} custom-call(s32[16]{0:T(128)} %and_select_fusion.first_ref, s32[16]{0:T(128)} %copy-done.3, s32[16]{0:T(128)} %slice.7.seg_last_ref, bf16[16,448,256]{2,1,0:T(8,128)(2,1)} %bitcast.1.q_ref, bf16[16,448,256]{2,1,0:T(8,128)(2,1)} %bitcast.8.k_ref, bf16[16,448,256]{2,1,0:T(8,128)(2,1)} %bitcast.10.v_ref, ...), custom_call_target="tpu_custom_call" | custom-call | flops 15032385536 | bytes 14680064 | tf_op jit(solution)/shard_map/pallas_call | solution.py:113
  295.5 18.5 %all-to-all-done.5 = bf16[8,2,2,16,2,3584]{5,3,4,2,1,0:T(8,128)(2,1)} async-done(((bf16[8,2,2,16,2,3584]{5,3,4,2,1,0:T(8,128)(2,1)}), bf16[8,2,2,16,2,3584]{5,3,4,2,1,0:T(8,128)(2,1)}, u32[]{:S(2)}, u32[]{:S(2)}) %all-to-all-start.5) | async-done | bytes 7340064 | tf_op jit(solution)/shard_map/all_to_all | solution.py:181
  314.0 4.9 %all-to-all-start.6 = ((bf16[256,16,448]{0,2,1:T(8,128)(2,1)}), bf16[256,16,448]{0,2,1:T(8,128)(2,1)}, u32[]{:S(2)}, u32[]{:S(2)}) async-start(bf16[256,16,448]{0,2,1:T(8,128)(2,1)} %bitcast.29), calls=%async_computation.6 | async-start | bytes 7340032 | tf_op jit(solution)/shard_map/all_to_all | solution.py:150
  318.9 14.5 %copy.50 = bf16[1,8,2,2,16,2,3584]{6,5,4,3,2,1,0:T(2,128)(2,1)} copy(bf16[1,8,2,2,16,2,3584]{6,4,5,3,2,1,0:T(8,128)(2,1)} %bitcast.11) | data formatting | bytes 14680064
  333.4 31.1 %all-to-all-done.6 = bf16[256,16,448]{0,2,1:T(8,128)(2,1)} async-done(((bf16[256,16,448]{0,2,1:T(8,128)(2,1)}), bf16[256,16,448]{0,2,1:T(8,128)(2,1)}, u32[]{:S(2)}, u32[]{:S(2)}) %all-to-all-start.6) | async-done | bytes 3670048 | tf_op jit(solution)/shard_map/all_to_all | solution.py:150
  364.5 5.9 %copy.49 = bf16[1,256,7168]{2,1,0:T(8,128)(2,1)} copy(bf16[1,256,7168]{1,2,0:T(8,128)(2,1)} %bitcast.19) | data formatting | bytes 7340032
  (5 shorter events, 0.0 us)
Async XLA Ops:
  6.5 54.8 %all-to-all-start = ((bf16[256,16,448]{0,2,1:T(8,128)(2,1)}), bf16[256,16,448]{0,2,1:T(8,128)(2,1)}, u32[]{:S(2)}, u32[]{:S(2)}) async-start(bf16[256,16,448]{0,2,1:T(8,128)(2,1)} %bitcast.27), calls=%async_computation | async-start | bytes 7340032 | tf_op jit(solution)/shard_map/all_to_all | solution.py:143
  25.1 87.0 %copy-start.1 = (s32[1,8,1]{1,2,0:T(1,128)S(1)}, s32[1,8,1]{1,2,0:T(1,128)}, u32[]{:S(2)}) copy-start(s32[1,8,1]{1,2,0:T(1,128)} %param.11) | copy-start | bytes 100
  61.3 50.7 %all-to-all-start.2 = ((bf16[8,2,16,2,3584]{4,3,1,0,2:T(2,128)(2,1)}), bf16[8,2,16,2,3584]{4,3,1,0,2:T(2,128)(2,1)}, u32[]{:S(2)}, u32[]{:S(2)}) async-start(bf16[8,2,16,2,3584]{4,3,1,0,2:T(2,128)(2,1)} %copy.44), calls=%async_computation.2 | async-start | bytes 7340032 | tf_op jit(solution)/shard_map/all_to_all | solution.py:159
  112.6 11.2 %all-to-all-start.1 = ((s32[16,1,8]{2,1,0:T(1,128)}), s32[16,1,8]{2,1,0:T(1,128)S(1)}, u32[]{:S(2)}, u32[]{:S(2)}) async-start(s32[16,1,8]{2,1,0:T(1,128)} %broadcast_in_dim.60), calls=%async_computation.1 | async-start | bytes 16384 | tf_op jit(solution)/shard_map/all_to_all | solution.py:192
  123.8 51.7 %all-to-all-start.4 = ((bf16[256,16,448]{0,2,1:T(8,128)(2,1)}), bf16[256,16,448]{0,2,1:T(8,128)(2,1)}, u32[]{:S(2)}, u32[]{:S(2)}) async-start(bf16[256,16,448]{0,2,1:T(8,128)(2,1)} %bitcast.26), calls=%async_computation.4 | async-start | bytes 7340032 | tf_op jit(solution)/shard_map/all_to_all | solution.py:143
  175.5 50.7 %all-to-all-start.3 = ((bf16[256,16,448]{0,2,1:T(8,128)(2,1)}), bf16[256,16,448]{0,2,1:T(8,128)(2,1)}, u32[]{:S(2)}, u32[]{:S(2)}) async-start(bf16[256,16,448]{0,2,1:T(8,128)(2,1)} %bitcast.25), calls=%async_computation.3 | async-start | bytes 7340032 | tf_op jit(solution)/shard_map/all_to_all | solution.py:143
  226.3 5.2 %copy-start.2 = (s32[1,6]{1,0:T(1,128)S(1)}, s32[1,6]{1,0:T(1,128)}, u32[]{:S(2)}) copy-start(s32[1,6]{1,0:T(1,128)} %param.9) | copy-start | bytes 76
  226.3 87.8 %all-to-all-start.5 = ((bf16[8,2,2,16,2,3584]{5,3,4,2,1,0:T(8,128)(2,1)}), bf16[8,2,2,16,2,3584]{5,3,4,2,1,0:T(8,128)(2,1)}, u32[]{:S(2)}, u32[]{:S(2)}) async-start(bf16[8,2,2,16,2,3584]{5,3,4,2,1,0:T(8,128)(2,1)} %select_reduce_fusion), calls=%async_computation.5 | async-start | bytes 14680064 | tf_op jit(solution)/shard_map/all_to_all | solution.py:181
  231.7 3.4 copy-start
  231.8 3.3 copy-start.3
  314.0 50.5 %all-to-all-start.6 = ((bf16[256,16,448]{0,2,1:T(8,128)(2,1)}), bf16[256,16,448]{0,2,1:T(8,128)(2,1)}, u32[]{:S(2)}, u32[]{:S(2)}) async-start(bf16[256,16,448]{0,2,1:T(8,128)(2,1)} %bitcast.29), calls=%async_computation.6 | async-start | bytes 7340032 | tf_op jit(solution)/shard_map/all_to_all | solution.py:150

commit v8 on v7

--- a/solution.py
+++ b/solution.py
@@ -186,13 +186,14 @@
     span_length = query_rows.shape[1] * lax.axis_size("tok")
     segments = segment_ids(lengths[0], span_length)
     tok_count = lax.axis_size("tok")
-    query_t = to_heads(query_rows)
-    query_t, destinations = lax.optimization_barrier((query_t, destinations))
     own_targets = destinations[0, :, 0]
     targets = lax.all_to_all(
         jnp.broadcast_to(own_targets[None, :], (tok_count, own_targets.shape[0])),
         "tok", split_axis=0, concat_axis=0, tiled=True,
     )
+    query_split = query_rows[0].reshape(query_rows.shape[1], tok_count, -1)
+    targets, query_split = lax.optimization_barrier((targets, query_split))
+    query_t = lax.all_to_all(query_split, "tok", split_axis=1, concat_axis=1, tiled=True).transpose(1, 2, 0)
     by_head = relocate_by_head(cache_blocks)
     by_head, key_rows, value_rows = lax.optimization_barrier((by_head, key_rows, value_rows))
     outgoing = place_slots(by_head, targets)

time: 372 us -> 371 us (level)
    all_to_all x0 -> x1, waiting for transfers between devices: none -> 39.6 us  [on_device(): lax.all_to_all(query_split, 'tok', split_axis=1, concat_axis=1, tiled=True)]
    all_to_all x3 -> x2, waiting for transfers between devices: 99.3 us -> 66.4 us  [to_heads(): lax.all_to_all(split, 'tok', split_axis=1, concat_axis=1, tiled=True)]
    all_to_all x3 -> x2, starting transfers between devices: 20.7 us -> 10.4 us  [to_heads(): lax.all_to_all(split, 'tok', split_axis=1, concat_axis=1, tiled=True)]
    all_to_all x1, waiting for transfers between devices: 45.6 us -> 39.5 us  [relocate_by_head(): return lax.all_to_all(split, 'tok', split_axis=2, concat_axis=2, tiled=True)]
    all_to_all x0 -> x1, starting transfers between devices: none -> 5.17 us  [on_device(): lax.all_to_all(query_split, 'tok', split_axis=1, concat_axis=1, tiled=True)]
    all_to_all x1, starting transfers between devices: 4.19 us -> 9.29 us  [on_device(): lax.all_to_all(jnp.broadcast_to(own_targets[None, :], (tok_count, own_tar...]
    unnamed x12 -> x10, local copies, waits for them, and re-layouts: 30.4 us -> 30.4 us
  transfers between devices with their start and end apart: 7 -> 7, of which waited for: 7 -> 6; matrix products, arithmetic and copies ran while one was open for 17% -> 17% of each run, Pallas kernels for 16% -> 16%
where the time goes in v8:
time: 371 us; the launch traced here: 369 us
  waiting for transfers between devices  196 us (53%)
  Pallas kernels  59.6 us (16%)
  local copies, waits for them, and re-layouts  55.4 us (15%)
  starting transfers between devices  42.1 us (11%)
  other arithmetic  15.7 us (4%)
    all_to_all x2, waiting for transfers between devices, to_heads(): lax.all_to_all(split, 'tok', split_axis=1, concat_axis=1, tiled=True)  66.4 us
    pallas_call x1, Pallas kernels, attend_local(): pl.pallas_call(attention_kernel, out_shape=jax.ShapeDtypeStruct(query_t.s...  59.6 us
    all_to_all x1, waiting for transfers between devices, on_device(): lax.all_to_all(query_split, 'tok', split_axis=1, concat_axis=1, tiled=True)  39.6 us
    all_to_all x1, waiting for transfers between devices, relocate_by_head(): return lax.all_to_all(split, 'tok', split_axis=2, concat_axis=2, tiled=True)  39.5 us
    all_to_all x1, waiting for transfers between devices, from_heads(): lax.all_to_all(by_source, 'tok', split_axis=1, concat_axis=1, tiled=True)  31.1 us
    unnamed x10, local copies, waits for them, and re-layouts  30.4 us
    all_to_all x1, waiting for transfers between devices, relocate_groups(): lax.all_to_all(outgoing, 'req', split_axis=0, concat_axis=0, tiled=True)  19.3 us
    optimization_barrier x3, local copies, waits for them, and re-layouts, on_device(): lax.optimization_barrier((by_head, key_rows, value_rows))  15.9 us
  transfers between devices with their start and end apart: 7, of which 6 were waited for; matrix products, arithmetic and copies ran while one was open for 17% of the time, Pallas kernels for 16%

profile of v8, /device:TPU:1, one launch (start us, length us, event | category | flops | bytes accessed | tf_op | source)
XLA Modules:
  0.0 369.5 jit_solution(10606556463724464091)
XLA Ops:
  0.6 1.3 broadcast_in_dim.60
  1.9 9.3 %all-to-all-start = ((s32[16,1,8]{2,1,0:T(1,128)}), s32[16,1,8]{2,1,0:T(1,128)S(1)}, u32[]{:S(2)}, u32[]{:S(2)}) async-start(s32[16,1,8]{2,1,0:T(1,128)} %broadcast_in_dim.60), calls=%async_computation | async-start | bytes 16384 | tf_op jit(solution)/shard_map/all_to_all | solution.py:190
  11.2 4.0 %copy.43 = bf16[1,8,2,32,3584]{4,1,3,2,0:T(8,128)(2,1)S(1)} copy(bf16[1,8,2,32,3584]{4,3,2,1,0:T(8,128)(2,1)} %param.10) | data formatting | bytes 7340032 | tf_op args[4]
  15.2 5.2 %copy.44 = bf16[8,2,16,2,3584]{4,3,1,0,2:T(2,128)(2,1)} copy(bf16[8,2,16,2,3584]{4,0,3,2,1:T(8,128)(2,1)S(1)} %bitcast.27) | data formatting | bytes 7340032 | tf_op jit(solution)/shard_map/reshape;squeeze | solution.py:158
  20.4 0.0 all-to-all-done
  20.4 7.2 %all-to-all-start.1 = ((bf16[8,2,16,2,3584]{4,3,1,0,2:T(2,128)(2,1)}), bf16[8,2,16,2,3584]{4,3,1,0,2:T(2,128)(2,1)}, u32[]{:S(2)}, u32[]{:S(2)}) async-start(bf16[8,2,16,2,3584]{4,3,1,0,2:T(2,128)(2,1)} %copy.44), calls=%async_computation.1 | async-start | bytes 7340032 | tf_op jit(solution)/shard_map/all_to_all | solution.py:159
  27.6 5.9 %copy.42 = bf16[1,256,7168]{1,2,0:T(8,128)(2,1)} copy(bf16[1,256,7168]{2,1,0:T(8,128)(2,1)} %param.6) | data formatting | bytes 7340032 | tf_op args[0]
  33.5 0.1 copy.41
  33.6 39.5 %all-to-all-done.1 = bf16[8,2,16,2,3584]{4,3,1,0,2:T(2,128)(2,1)} async-done(((bf16[8,2,16,2,3584]{4,3,1,0,2:T(2,128)(2,1)}), bf16[8,2,16,2,3584]{4,3,1,0,2:T(2,128)(2,1)}, u32[]{:S(2)}, u32[]{:S(2)}) %all-to-all-start.1) | async-done | bytes 3670048 | tf_op jit(solution)/shard_map/all_to_all | solution.py:159
  73.1 5.2 %all-to-all-start.2 = ((bf16[256,16,448]{0,2,1:T(8,128)(2,1)}), bf16[256,16,448]{0,2,1:T(8,128)(2,1)}, u32[]{:S(2)}, u32[]{:S(2)}) async-start(bf16[256,16,448]{0,2,1:T(8,128)(2,1)} %bitcast.25), calls=%async_computation.2 | async-start | bytes 7340032 | tf_op jit(solution)/shard_map/all_to_all | solution.py:196
  78.3 5.9 %copy.47 = bf16[1,256,7168]{1,2,0:T(8,128)(2,1)} copy(bf16[1,256,7168]{2,1,0:T(8,128)(2,1)} %param.8) | data formatting | bytes 7340032 | tf_op jit(solution)/shard_map/optimization_barrier | solution.py:198
  84.2 39.6 %all-to-all-done.2 = bf16[256,16,448]{0,2,1:T(8,128)(2,1)} async-done(((bf16[256,16,448]{0,2,1:T(8,128)(2,1)}), bf16[256,16,448]{0,2,1:T(8,128)(2,1)}, u32[]{:S(2)}, u32[]{:S(2)}) %all-to-all-start.2) | async-done | bytes 3670048 | tf_op jit(solution)/shard_map/all_to_all | solution.py:196
  123.8 5.2 %all-to-all-start.4 = ((bf16[256,16,448]{0,2,1:T(8,128)(2,1)}), bf16[256,16,448]{0,2,1:T(8,128)(2,1)}, u32[]{:S(2)}, u32[]{:S(2)}) async-start(bf16[256,16,448]{0,2,1:T(8,128)(2,1)} %bitcast.26), calls=%async_computation.4 | async-start | bytes 7340032 | tf_op jit(solution)/shard_map/all_to_all | solution.py:143
  129.0 5.9 %copy.46 = bf16[1,256,7168]{1,2,0:T(8,128)(2,1)} copy(bf16[1,256,7168]{2,1,0:T(8,128)(2,1)} %param.7) | data formatting | bytes 7340032 | tf_op jit(solution)/shard_map/optimization_barrier | solution.py:198
  134.9 39.6 %all-to-all-done.4 = bf16[256,16,448]{0,2,1:T(8,128)(2,1)} async-done(((bf16[256,16,448]{0,2,1:T(8,128)(2,1)}), bf16[256,16,448]{0,2,1:T(8,128)(2,1)}, u32[]{:S(2)}, u32[]{:S(2)}) %all-to-all-start.4) | async-done | bytes 3670048 | tf_op jit(solution)/shard_map/all_to_all | solution.py:143
  174.6 5.2 %all-to-all-start.3 = ((bf16[256,16,448]{0,2,1:T(8,128)(2,1)}), bf16[256,16,448]{0,2,1:T(8,128)(2,1)}, u32[]{:S(2)}, u32[]{:S(2)}) async-start(bf16[256,16,448]{0,2,1:T(8,128)(2,1)} %bitcast.24), calls=%async_computation.3 | async-start | bytes 7340032 | tf_op jit(solution)/shard_map/all_to_all | solution.py:143
  179.8 0.1 convert_reduce_fusion.1
  179.9 4.0 %copy.45 = bf16[8,2,16,2,3584]{4,2,3,1,0:T(8,128)(2,1)S(1)} copy(bf16[8,2,16,2,3584]{4,3,1,0,2:T(2,128)(2,1)} %all-to-all-done.1) | data formatting | bytes 7340032 | tf_op jit(solution)/shard_map/optimization_barrier | solution.py:198
  184.0 14.6 %select_reduce_fusion = bf16[8,2,2,16,2,3584]{5,3,4,2,1,0:T(8,128)(2,1)} fusion(pred[8,2,8,16]{3,2,1,0:T(8,128)(4,1)S(1)} %broadcast_and_fusion, bf16[8,2,16,2,3584]{4,2,3,1,0:T(8,128)(2,1)S(1)} %copy.45), kind=kLoop, calls=%fused_computation | loop fusion | flops 55050240 | bytes 11012096 | tf_op jit(solution)/shard_map/reduce_sum | solution.py:177
  198.6 26.8 %all-to-all-done.3 = bf16[256,16,448]{0,2,1:T(8,128)(2,1)} async-done(((bf16[256,16,448]{0,2,1:T(8,128)(2,1)}), bf16[256,16,448]{0,2,1:T(8,128)(2,1)}, u32[]{:S(2)}, u32[]{:S(2)}) %all-to-all-start.3) | async-done | bytes 3670048 | tf_op jit(solution)/shard_map/all_to_all | solution.py:143
  225.3 0.0 copy-start.1
  225.3 5.1 %all-to-all-start.5 = ((bf16[8,2,2,16,2,3584]{5,3,4,2,1,0:T(8,128)(2,1)}), bf16[8,2,2,16,2,3584]{5,3,4,2,1,0:T(8,128)(2,1)}, u32[]{:S(2)}, u32[]{:S(2)}) async-start(bf16[8,2,2,16,2,3584]{5,3,4,2,1,0:T(8,128)(2,1)} %select_reduce_fusion), calls=%async_computation.5 | async-start | bytes 14680064 | tf_op jit(solution)/shard_map/all_to_all | solution.py:181
  230.5 0.0 copy-done.1
  230.5 0.2 reduce-window.4
  230.7 0.1 convert_reduce_fusion
  230.8 0.0 copy-start
  230.8 0.1 slice.6.seg_first_ref
  230.9 0.0 copy-start.2
  230.9 0.6 slice.7.seg_last_ref
  231.5 2.0 copy.48.kseg_ref
  233.5 0.1 select_reduce_fusion.1
  233.6 0.6 and_select_fusion.first_ref
  234.2 0.0 copy-done
  234.2 0.0 copy-done.2
  234.2 59.6 %shard_map.77 = bf16[16,448,256]{2,1,0:T(8,128)(2,1)} custom-call(s32[16]{0:T(128)} %and_select_fusion.first_ref, s32[16]{0:T(128)} %copy-done.2, s32[16]{0:T(128)} %slice.7.seg_last_ref, bf16[16,448,256]{2,1,0:T(8,128)(2,1)} %bitcast.6.q_ref, bf16[16,448,256]{2,1,0:T(8,128)(2,1)} %bitcast.8.k_ref, bf16[16,448,256]{2,1,0:T(8,128)(2,1)} %bitcast.10.v_ref, ...), custom_call_target="tpu_custom_call" | custom-call | flops 15032385536 | bytes 14680064 | tf_op jit(solution)/shard_map/pallas_call | solution.py:113
  293.8 19.3 %all-to-all-done.5 = bf16[8,2,2,16,2,3584]{5,3,4,2,1,0:T(8,128)(2,1)} async-done(((bf16[8,2,2,16,2,3584]{5,3,4,2,1,0:T(8,128)(2,1)}), bf16[8,2,2,16,2,3584]{5,3,4,2,1,0:T(8,128)(2,1)}, u32[]{:S(2)}, u32[]{:S(2)}) %all-to-all-start.5) | async-done | bytes 7340064 | tf_op jit(solution)/shard_map/all_to_all | solution.py:181
  313.1 4.9 %all-to-all-start.6 = ((bf16[256,16,448]{0,2,1:T(8,128)(2,1)}), bf16[256,16,448]{0,2,1:T(8,128)(2,1)}, u32[]{:S(2)}, u32[]{:S(2)}) async-start(bf16[256,16,448]{0,2,1:T(8,128)(2,1)} %bitcast.28), calls=%async_computation.6 | async-start | bytes 7340032 | tf_op jit(solution)/shard_map/all_to_all | solution.py:150
  318.0 14.5 %copy.50 = bf16[1,8,2,2,16,2,3584]{6,5,4,3,2,1,0:T(2,128)(2,1)} copy(bf16[1,8,2,2,16,2,3584]{6,4,5,3,2,1,0:T(8,128)(2,1)} %bitcast.11) | data formatting | bytes 14680064
  332.5 31.1 %all-to-all-done.6 = bf16[256,16,448]{0,2,1:T(8,128)(2,1)} async-done(((bf16[256,16,448]{0,2,1:T(8,128)(2,1)}), bf16[256,16,448]{0,2,1:T(8,128)(2,1)}, u32[]{:S(2)}, u32[]{:S(2)}) %all-to-all-start.6) | async-done | bytes 3670048 | tf_op jit(solution)/shard_map/all_to_all | solution.py:150
  363.6 5.9 %copy.49 = bf16[1,256,7168]{2,1,0:T(8,128)(2,1)} copy(bf16[1,256,7168]{1,2,0:T(8,128)(2,1)} %bitcast.19) | data formatting | bytes 7340032
  (5 shorter events, 0.0 us)
Async XLA Ops:
  1.9 18.5 %all-to-all-start = ((s32[16,1,8]{2,1,0:T(1,128)}), s32[16,1,8]{2,1,0:T(1,128)S(1)}, u32[]{:S(2)}, u32[]{:S(2)}) async-start(s32[16,1,8]{2,1,0:T(1,128)} %broadcast_in_dim.60), calls=%async_computation | async-start | bytes 16384 | tf_op jit(solution)/shard_map/all_to_all | solution.py:190
  20.4 52.7 %all-to-all-start.1 = ((bf16[8,2,16,2,3584]{4,3,1,0,2:T(2,128)(2,1)}), bf16[8,2,16,2,3584]{4,3,1,0,2:T(2,128)(2,1)}, u32[]{:S(2)}, u32[]{:S(2)}) async-start(bf16[8,2,16,2,3584]{4,3,1,0,2:T(2,128)(2,1)} %copy.44), calls=%async_computation.1 | async-start | bytes 7340032 | tf_op jit(solution)/shard_map/all_to_all | solution.py:159
  73.1 50.7 %all-to-all-start.2 = ((bf16[256,16,448]{0,2,1:T(8,128)(2,1)}), bf16[256,16,448]{0,2,1:T(8,128)(2,1)}, u32[]{:S(2)}, u32[]{:S(2)}) async-start(bf16[256,16,448]{0,2,1:T(8,128)(2,1)} %bitcast.25), calls=%async_computation.2 | async-start | bytes 7340032 | tf_op jit(solution)/shard_map/all_to_all | solution.py:196
  123.8 50.7 %all-to-all-start.4 = ((bf16[256,16,448]{0,2,1:T(8,128)(2,1)}), bf16[256,16,448]{0,2,1:T(8,128)(2,1)}, u32[]{:S(2)}, u32[]{:S(2)}) async-start(bf16[256,16,448]{0,2,1:T(8,128)(2,1)} %bitcast.26), calls=%async_computation.4 | async-start | bytes 7340032 | tf_op jit(solution)/shard_map/all_to_all | solution.py:143
  174.6 50.7 %all-to-all-start.3 = ((bf16[256,16,448]{0,2,1:T(8,128)(2,1)}), bf16[256,16,448]{0,2,1:T(8,128)(2,1)}, u32[]{:S(2)}, u32[]{:S(2)}) async-start(bf16[256,16,448]{0,2,1:T(8,128)(2,1)} %bitcast.24), calls=%async_computation.3 | async-start | bytes 7340032 | tf_op jit(solution)/shard_map/all_to_all | solution.py:143
  225.3 5.2 %copy-start.1 = (s32[1,6]{1,0:T(1,128)S(1)}, s32[1,6]{1,0:T(1,128)}, u32[]{:S(2)}) copy-start(s32[1,6]{1,0:T(1,128)} %param.9) | copy-start | bytes 76
  225.3 87.8 %all-to-all-start.5 = ((bf16[8,2,2,16,2,3584]{5,3,4,2,1,0:T(8,128)(2,1)}), bf16[8,2,2,16,2,3584]{5,3,4,2,1,0:T(8,128)(2,1)}, u32[]{:S(2)}, u32[]{:S(2)}) async-start(bf16[8,2,2,16,2,3584]{5,3,4,2,1,0:T(8,128)(2,1)} %select_reduce_fusion), calls=%async_computation.5 | async-start | bytes 14680064 | tf_op jit(solution)/shard_map/all_to_all | solution.py:181
  230.8 3.4 copy-start
  230.9 3.3 copy-start.2
  313.1 50.4 %all-to-all-start.6 = ((bf16[256,16,448]{0,2,1:T(8,128)(2,1)}), bf16[256,16,448]{0,2,1:T(8,128)(2,1)}, u32[]{:S(2)}, u32[]{:S(2)}) async-start(bf16[256,16,448]{0,2,1:T(8,128)(2,1)} %bitcast.28), calls=%async_computation.6 | async-start | bytes 7340032 | tf_op jit(solution)/shard_map/all_to_all | solution.py:150

commit v9 on v8

--- a/solution.py
+++ b/solution.py
@@ -18,10 +18,10 @@
     return jnp.sum((positions[:, None] >= ends[None, :]).astype(jnp.int32), axis=1)
 
 
-def attention_kernel(first_ref, seg_first_ref, seg_last_ref, q_ref, k_ref, v_ref, qseg_ref, kseg_ref, o_ref,
+def attention_kernel(first_ref, seg_first_ref, seg_last_ref, q_ref, kv_ref, qseg_ref, kseg_ref, o_ref,
                      m_ref, l_ref, acc_ref, k_sc):
     qi = pl.program_id(0)
-    chunks, width, rows = k_ref.shape
+    chunks, _, width, rows = kv_ref.shape
     heads_here = width // HD
     nt = (((1,), (1,)), ((), ()))
 
@@ -35,7 +35,7 @@
             start = pl.multiple_of(c * rows, rows)
             for h in range(heads_here):
                 k_sc[h, pl.ds(start, rows), :] = lax.dot_general(
-                    eye, k_ref[c, h * HD:(h + 1) * HD, :], nt, preferred_element_type=jnp.float32
+                    eye, kv_ref[c, 0, h * HD:(h + 1) * HD, :], nt, preferred_element_type=jnp.float32
                 ).astype(jnp.bfloat16)
             return carry
 
@@ -67,7 +67,7 @@
                 weights = jnp.where(visible, weights, 0.0)
             l_ref[h] = alpha * l_ref[h] + jnp.sum(weights, axis=0, keepdims=True)
             m_ref[h] = m_new
-            values = v_ref[kb, h * HD:(h + 1) * HD, :]
+            values = kv_ref[kb, 1, h * HD:(h + 1) * HD, :]
             acc_ref[h] = alpha * acc_ref[h] + jnp.dot(
                 values, weights.astype(jnp.bfloat16), preferred_element_type=jnp.float32
             )
@@ -90,7 +90,7 @@
         o_ref[0, h * HD:(h + 1) * HD, :] = (acc_ref[h] / l_ref[h]).astype(o_ref.dtype)
 
 
-def attend_local(query_t, key_t, value_t, lengths_row, segments):
+def attend_local(query_t, kv_t, lengths_row, segments):
     chunks, width, rows = query_t.shape
     heads_here = width // HD
     length = chunks * rows
@@ -118,8 +118,7 @@
             grid=(chunks,),
             in_specs=[
                 pl.BlockSpec((1, width, rows), lambda i, *_: (i, 0, 0)),
-                pl.BlockSpec((chunks, width, rows), lambda i, *_: (0, 0, 0), pipeline_mode=pl.Buffered(1)),
-                pl.BlockSpec((chunks, width, rows), lambda i, *_: (0, 0, 0), pipeline_mode=pl.Buffered(1)),
+                pl.BlockSpec((chunks, 2, width, rows), lambda i, *_: (0, 0, 0, 0), pipeline_mode=pl.Buffered(1)),
                 pl.BlockSpec((None, 1, rows), lambda i, *_: (i, 0, 0)),
                 pl.BlockSpec((length, 1), lambda i, *_: (0, 0), pipeline_mode=pl.Buffered(1)),
             ],
@@ -133,7 +132,7 @@
         ),
         compiler_params=pltpu.CompilerParams(dimension_semantics=("arbitrary",)),
         cost_estimate=cost,
-    )(first_chunk, seg_first, seg_last, query_t, key_t, value_t, qseg, kseg)
+    )(first_chunk, seg_first, seg_last, query_t, kv_t, qseg, kseg)
 
 
 def to_heads(rows_in):
@@ -142,6 +141,20 @@
     split = rows_in[0].reshape(token_rows, tok_count, feature_width // tok_count)
     gathered = lax.all_to_all(split, "tok", split_axis=1, concat_axis=1, tiled=True)
     return gathered.transpose(1, 2, 0)
+
+
+def kv_to_heads(key_rows, value_rows):
+    tok_count = lax.axis_size("tok")
+    token_rows, feature_width = key_rows.shape[1], key_rows.shape[2]
+    stacked = jnp.stack(
+        [
+            key_rows[0].reshape(token_rows, tok_count, feature_width // tok_count),
+            value_rows[0].reshape(token_rows, tok_count, feature_width // tok_count),
+        ],
+        axis=2,
+    )
+    gathered = lax.all_to_all(stacked, "tok", split_axis=1, concat_axis=1, tiled=True)
+    return gathered.transpose(1, 2, 3, 0)
 
 
 def from_heads(attended_t):
@@ -197,10 +210,10 @@
     by_head = relocate_by_head(cache_blocks)
     by_head, key_rows, value_rows = lax.optimization_barrier((by_head, key_rows, value_rows))
     outgoing = place_slots(by_head, targets)
-    key_t, value_t = to_heads(key_rows), to_heads(value_rows)
-    outgoing, query_t, key_t, value_t = lax.optimization_barrier((outgoing, query_t, key_t, value_t))
+    kv_t = kv_to_heads(key_rows, value_rows)
+    outgoing, query_t, kv_t = lax.optimization_barrier((outgoing, query_t, kv_t))
     moved_cache = relocate_groups(outgoing)
-    attended_t = attend_local(query_t, key_t, value_t, lengths[0], segments)
+    attended_t = attend_local(query_t, kv_t, lengths[0], segments)
     moved_cache, attended_t = lax.optimization_barrier((moved_cache, attended_t))
     attended = from_heads(attended_t)
     return (attended, moved_cache)

time: 371 us -> 359 us (0.968)
  waiting for transfers between devices: 196 us -> 185 us
  other arithmetic: 15.7 us -> 22.4 us
  starting transfers between devices: 42.1 us -> 37 us
    all_to_all x1, waiting for transfers between devices: 39.6 us -> 26.8 us  [on_device(): lax.all_to_all(query_split, 'tok', split_axis=1, concat_axis=1, tiled=True)]
    another operation x1 -> x2, other arithmetic: 0.18 us -> 7.06 us  [the longest x1 6.88 us: kv_to_heads(): jnp.stack([key_rows[0].reshape(token_rows, tok_count, feature_width // to...]
    all_to_all x2 -> x1, starting transfers between devices: 10.4 us -> 5.37 us  [kv_to_heads(): lax.all_to_all(stacked, 'tok', split_axis=1, concat_axis=1, tiled=True)]
    all_to_all x2 -> x1, waiting for transfers between devices: 66.4 us -> 66.1 us  [kv_to_heads(): lax.all_to_all(stacked, 'tok', split_axis=1, concat_axis=1, tiled=True)]
  transfers between devices with their start and end apart: 7 -> 6, of which waited for: 6 -> 5; matrix products, arithmetic and copies ran while one was open for 17% -> 20% of each run, Pallas kernels for 16% -> 16%
where the time goes in v9:
time: 359 us; the launch traced here: 358 us
  waiting for transfers between devices  185 us (52%)
  Pallas kernels  57.9 us (16%)
  local copies, waits for them, and re-layouts  55.5 us (15%)
  starting transfers between devices  37 us (10%)
  other arithmetic  22.4 us (6%)
    all_to_all x1, waiting for transfers between devices, kv_to_heads(): lax.all_to_all(stacked, 'tok', split_axis=1, concat_axis=1, tiled=True)  66.1 us
    pallas_call x1, Pallas kernels, attend_local(): pl.pallas_call(attention_kernel, out_shape=jax.ShapeDtypeStruct(query_t.s...  57.9 us
    all_to_all x1, waiting for transfers between devices, relocate_by_head(): return lax.all_to_all(split, 'tok', split_axis=2, concat_axis=2, tiled=True)  39.5 us
    all_to_all x1, waiting for transfers between devices, from_heads(): lax.all_to_all(by_source, 'tok', split_axis=1, concat_axis=1, tiled=True)  31.1 us
    unnamed x10, local copies, waits for them, and re-layouts  30.4 us
    all_to_all x1, waiting for transfers between devices, on_device(): lax.all_to_all(query_split, 'tok', split_axis=1, concat_axis=1, tiled=True)  26.8 us
    all_to_all x1, waiting for transfers between devices, relocate_groups(): lax.all_to_all(outgoing, 'req', split_axis=0, concat_axis=0, tiled=True)  21.1 us
    optimization_barrier x3, local copies, waits for them, and re-layouts, on_device(): lax.optimization_barrier((by_head, key_rows, value_rows))  15.9 us
  transfers between devices with their start and end apart: 6, of which 5 were waited for; matrix products, arithmetic and copies ran while one was open for 20% of the time, Pallas kernels for 16%

profile of v9, /device:TPU:1, one launch (start us, length us, event | category | flops | bytes accessed | tf_op | source)
XLA Modules:
  0.0 358.1 jit_solution(10979183633815194600)
XLA Ops:
  0.6 1.3 broadcast_in_dim.60
  1.9 9.3 %all-to-all-start = ((s32[16,1,8]{2,1,0:T(1,128)}), s32[16,1,8]{2,1,0:T(1,128)S(1)}, u32[]{:S(2)}, u32[]{:S(2)}) async-start(s32[16,1,8]{2,1,0:T(1,128)} %broadcast_in_dim.60), calls=%async_computation | async-start | bytes 16384 | tf_op jit(solution)/shard_map/all_to_all | solution.py:203
  11.2 4.0 %copy.43 = bf16[1,8,2,32,3584]{4,1,3,2,0:T(8,128)(2,1)S(1)} copy(bf16[1,8,2,32,3584]{4,3,2,1,0:T(8,128)(2,1)} %param.10) | data formatting | bytes 7340032 | tf_op args[4]
  15.2 5.2 %copy.44 = bf16[8,2,16,2,3584]{4,3,1,0,2:T(2,128)(2,1)} copy(bf16[8,2,16,2,3584]{4,0,3,2,1:T(8,128)(2,1)S(1)} %bitcast.26) | data formatting | bytes 7340032 | tf_op jit(solution)/shard_map/reshape;squeeze | solution.py:171
  20.4 0.0 all-to-all-done
  20.4 7.2 %all-to-all-start.1 = ((bf16[8,2,16,2,3584]{4,3,1,0,2:T(2,128)(2,1)}), bf16[8,2,16,2,3584]{4,3,1,0,2:T(2,128)(2,1)}, u32[]{:S(2)}, u32[]{:S(2)}) async-start(bf16[8,2,16,2,3584]{4,3,1,0,2:T(2,128)(2,1)} %copy.44), calls=%async_computation.1 | async-start | bytes 7340032 | tf_op jit(solution)/shard_map/all_to_all | solution.py:172
  27.6 5.9 %copy.42 = bf16[1,256,7168]{1,2,0:T(8,128)(2,1)} copy(bf16[1,256,7168]{2,1,0:T(8,128)(2,1)} %param.6) | data formatting | bytes 7340032 | tf_op args[0]
  33.5 0.1 copy.41
  33.6 39.5 %all-to-all-done.1 = bf16[8,2,16,2,3584]{4,3,1,0,2:T(2,128)(2,1)} async-done(((bf16[8,2,16,2,3584]{4,3,1,0,2:T(2,128)(2,1)}), bf16[8,2,16,2,3584]{4,3,1,0,2:T(2,128)(2,1)}, u32[]{:S(2)}, u32[]{:S(2)}) %all-to-all-start.1) | async-done | bytes 3670048 | tf_op jit(solution)/shard_map/all_to_all | solution.py:172
  73.1 5.2 %all-to-all-start.2 = ((bf16[256,16,448]{0,2,1:T(8,128)(2,1)}), bf16[256,16,448]{0,2,1:T(8,128)(2,1)}, u32[]{:S(2)}, u32[]{:S(2)}) async-start(bf16[256,16,448]{0,2,1:T(8,128)(2,1)} %bitcast.25), calls=%async_computation.2 | async-start | bytes 7340032 | tf_op jit(solution)/shard_map/all_to_all | solution.py:209
  78.3 5.9 %copy.46 = bf16[1,256,7168]{1,2,0:T(8,128)(2,1)} copy(bf16[1,256,7168]{2,1,0:T(8,128)(2,1)} %param.7) | data formatting | bytes 7340032 | tf_op jit(solution)/shard_map/optimization_barrier | solution.py:211
  84.2 5.9 %copy.47 = bf16[1,256,7168]{1,2,0:T(8,128)(2,1)} copy(bf16[1,256,7168]{2,1,0:T(8,128)(2,1)} %param.8) | data formatting | bytes 7340032 | tf_op jit(solution)/shard_map/optimization_barrier | solution.py:211
  90.2 6.9 %pad_maximum_fusion = bf16[256,16,2,448]{0,3,2,1:T(8,128)(2,1)} fusion(bf16[256,16,1,448]{0,3,2,1:T(8,128)(2,1)} %bitcast.24, bf16[256,16,1,448]{0,3,2,1:T(8,128)(2,1)} %bitcast.23), kind=kLoop, calls=%fused_computation.1 | loop fusion | flops 3670016 | bytes 14680064 | tf_op jit(solution)/shard_map/stack | solution.py:149
  97.1 26.8 %all-to-all-done.2 = bf16[256,16,448]{0,2,1:T(8,128)(2,1)} async-done(((bf16[256,16,448]{0,2,1:T(8,128)(2,1)}), bf16[256,16,448]{0,2,1:T(8,128)(2,1)}, u32[]{:S(2)}, u32[]{:S(2)}) %all-to-all-start.2) | async-done | bytes 3670048 | tf_op jit(solution)/shard_map/all_to_all | solution.py:209
  123.9 5.4 %all-to-all-start.3 = ((bf16[256,16,2,448]{0,3,2,1:T(8,128)(2,1)}), bf16[256,16,2,448]{0,3,2,1:T(8,128)(2,1)}, u32[]{:S(2)}, u32[]{:S(2)}) async-start(bf16[256,16,2,448]{0,3,2,1:T(8,128)(2,1)} %pad_maximum_fusion), calls=%async_computation.3 | async-start | bytes 14680064 | tf_op jit(solution)/shard_map/all_to_all | solution.py:156
  129.2 0.1 convert_reduce_fusion.1
  129.4 4.0 %copy.45 = bf16[8,2,16,2,3584]{4,2,3,1,0:T(8,128)(2,1)S(1)} copy(bf16[8,2,16,2,3584]{4,3,1,0,2:T(2,128)(2,1)} %all-to-all-done.1) | data formatting | bytes 7340032 | tf_op jit(solution)/shard_map/optimization_barrier | solution.py:211
  133.4 14.6 %select_reduce_fusion = bf16[8,2,2,16,2,3584]{5,3,4,2,1,0:T(8,128)(2,1)} fusion(pred[8,2,8,16]{3,2,1,0:T(8,128)(4,1)S(1)} %broadcast_and_fusion, bf16[8,2,16,2,3584]{4,2,3,1,0:T(8,128)(2,1)S(1)} %copy.45), kind=kLoop, calls=%fused_computation | loop fusion | flops 55050240 | bytes 11012096 | tf_op jit(solution)/shard_map/reduce_sum | solution.py:190
  148.0 66.1 %all-to-all-done.3 = bf16[256,16,2,448]{0,3,2,1:T(8,128)(2,1)} async-done(((bf16[256,16,2,448]{0,3,2,1:T(8,128)(2,1)}), bf16[256,16,2,448]{0,3,2,1:T(8,128)(2,1)}, u32[]{:S(2)}, u32[]{:S(2)}) %all-to-all-start.3) | async-done | bytes 7340064 | tf_op jit(solution)/shard_map/all_to_all | solution.py:156
  214.1 0.0 copy-start.1
  214.1 5.0 %all-to-all-start.4 = ((bf16[8,2,2,16,2,3584]{5,3,4,2,1,0:T(8,128)(2,1)}), bf16[8,2,2,16,2,3584]{5,3,4,2,1,0:T(8,128)(2,1)}, u32[]{:S(2)}, u32[]{:S(2)}) async-start(bf16[8,2,2,16,2,3584]{5,3,4,2,1,0:T(8,128)(2,1)} %select_reduce_fusion), calls=%async_computation.4 | async-start | bytes 14680064 | tf_op jit(solution)/shard_map/all_to_all | solution.py:194
  219.1 0.0 copy-done.1
  219.1 0.2 reduce-window.4
  219.3 0.1 convert_reduce_fusion
  219.4 0.0 copy-start
  219.4 0.1 slice.6.seg_first_ref
  219.5 0.0 copy-start.2
  219.5 0.6 slice.7.seg_last_ref
  220.1 2.0 copy.48.kseg_ref
  222.1 0.1 select_reduce_fusion.1
  222.2 0.5 and_select_fusion.first_ref
  222.7 0.0 copy-done
  222.7 0.0 copy-done.2
  222.7 57.9 %shard_map.77 = bf16[16,448,256]{2,1,0:T(8,128)(2,1)} custom-call(s32[16]{0:T(128)} %and_select_fusion.first_ref, s32[16]{0:T(128)} %copy-done.2, s32[16]{0:T(128)} %slice.7.seg_last_ref, bf16[16,448,256]{2,1,0:T(8,128)(2,1)} %bitcast.6.q_ref, bf16[16,2,448,256]{3,2,1,0:T(8,128)(2,1)} %bitcast.9.kv_ref, s32[16,1,256]{2,1,0:T(1,128)} %bitcast.29, ...), custom_call_target="tpu_custom_call" | custom-call | flops 15032385536 | bytes 14680064 | tf_op jit(solution)/shard_map/pallas_call | solution.py:113
  280.6 21.1 %all-to-all-done.4 = bf16[8,2,2,16,2,3584]{5,3,4,2,1,0:T(8,128)(2,1)} async-done(((bf16[8,2,2,16,2,3584]{5,3,4,2,1,0:T(8,128)(2,1)}), bf16[8,2,2,16,2,3584]{5,3,4,2,1,0:T(8,128)(2,1)}, u32[]{:S(2)}, u32[]{:S(2)}) %all-to-all-start.4) | async-done | bytes 7340064 | tf_op jit(solution)/shard_map/all_to_all | solution.py:194
  301.7 4.9 %all-to-all-start.5 = ((bf16[256,16,448]{0,2,1:T(8,128)(2,1)}), bf16[256,16,448]{0,2,1:T(8,128)(2,1)}, u32[]{:S(2)}, u32[]{:S(2)}) async-start(bf16[256,16,448]{0,2,1:T(8,128)(2,1)} %bitcast.27), calls=%async_computation.5 | async-start | bytes 7340032 | tf_op jit(solution)/shard_map/all_to_all | solution.py:163
  306.6 14.5 %copy.50 = bf16[1,8,2,2,16,2,3584]{6,5,4,3,2,1,0:T(2,128)(2,1)} copy(bf16[1,8,2,2,16,2,3584]{6,4,5,3,2,1,0:T(8,128)(2,1)} %bitcast.10) | data formatting | bytes 14680064
  321.1 31.1 %all-to-all-done.5 = bf16[256,16,448]{0,2,1:T(8,128)(2,1)} async-done(((bf16[256,16,448]{0,2,1:T(8,128)(2,1)}), bf16[256,16,448]{0,2,1:T(8,128)(2,1)}, u32[]{:S(2)}, u32[]{:S(2)}) %all-to-all-start.5) | async-done | bytes 3670048 | tf_op jit(solution)/shard_map/all_to_all | solution.py:163
  352.2 5.9 %copy.49 = bf16[1,256,7168]{2,1,0:T(8,128)(2,1)} copy(bf16[1,256,7168]{1,2,0:T(8,128)(2,1)} %bitcast.18) | data formatting | bytes 7340032
  (5 shorter events, 0.0 us)
Async XLA Ops:
  1.9 18.5 %all-to-all-start = ((s32[16,1,8]{2,1,0:T(1,128)}), s32[16,1,8]{2,1,0:T(1,128)S(1)}, u32[]{:S(2)}, u32[]{:S(2)}) async-start(s32[16,1,8]{2,1,0:T(1,128)} %broadcast_in_dim.60), calls=%async_computation | async-start | bytes 16384 | tf_op jit(solution)/shard_map/all_to_all | solution.py:203
  20.4 52.7 %all-to-all-start.1 = ((bf16[8,2,16,2,3584]{4,3,1,0,2:T(2,128)(2,1)}), bf16[8,2,16,2,3584]{4,3,1,0,2:T(2,128)(2,1)}, u32[]{:S(2)}, u32[]{:S(2)}) async-start(bf16[8,2,16,2,3584]{4,3,1,0,2:T(2,128)(2,1)} %copy.44), calls=%async_computation.1 | async-start | bytes 7340032 | tf_op jit(solution)/shard_map/all_to_all | solution.py:172
  73.1 50.7 %all-to-all-start.2 = ((bf16[256,16,448]{0,2,1:T(8,128)(2,1)}), bf16[256,16,448]{0,2,1:T(8,128)(2,1)}, u32[]{:S(2)}, u32[]{:S(2)}) async-start(bf16[256,16,448]{0,2,1:T(8,128)(2,1)} %bitcast.25), calls=%async_computation.2 | async-start | bytes 7340032 | tf_op jit(solution)/shard_map/all_to_all | solution.py:209
  123.9 90.3 %all-to-all-start.3 = ((bf16[256,16,2,448]{0,3,2,1:T(8,128)(2,1)}), bf16[256,16,2,448]{0,3,2,1:T(8,128)(2,1)}, u32[]{:S(2)}, u32[]{:S(2)}) async-start(bf16[256,16,2,448]{0,3,2,1:T(8,128)(2,1)} %pad_maximum_fusion), calls=%async_computation.3 | async-start | bytes 14680064 | tf_op jit(solution)/shard_map/all_to_all | solution.py:156
  214.1 5.0 %copy-start.1 = (s32[1,6]{1,0:T(1,128)S(1)}, s32[1,6]{1,0:T(1,128)}, u32[]{:S(2)}) copy-start(s32[1,6]{1,0:T(1,128)} %param.9) | copy-start | bytes 76
  214.1 87.6 %all-to-all-start.4 = ((bf16[8,2,2,16,2,3584]{5,3,4,2,1,0:T(8,128)(2,1)}), bf16[8,2,2,16,2,3584]{5,3,4,2,1,0:T(8,128)(2,1)}, u32[]{:S(2)}, u32[]{:S(2)}) async-start(bf16[8,2,2,16,2,3584]{5,3,4,2,1,0:T(8,128)(2,1)} %select_reduce_fusion), calls=%async_computation.4 | async-start | bytes 14680064 | tf_op jit(solution)/shard_map/all_to_all | solution.py:194
  219.4 3.2 copy-start
  219.5 3.1 copy-start.2
  301.7 50.5 %all-to-all-start.5 = ((bf16[256,16,448]{0,2,1:T(8,128)(2,1)}), bf16[256,16,448]{0,2,1:T(8,128)(2,1)}, u32[]{:S(2)}, u32[]{:S(2)}) async-start(bf16[256,16,448]{0,2,1:T(8,128)(2,1)} %bitcast.27), calls=%async_computation.5 | async-start | bytes 7340032 | tf_op jit(solution)/shard_map/all_to_all | solution.py:163

commit v10 on v9

--- a/solution.py
+++ b/solution.py
@@ -90,8 +90,8 @@
         o_ref[0, h * HD:(h + 1) * HD, :] = (acc_ref[h] / l_ref[h]).astype(o_ref.dtype)
 
 
-def attend_local(query_t, kv_t, lengths_row, segments):
-    chunks, width, rows = query_t.shape
+def attend_local(qkv_t, lengths_row, segments):
+    chunks, _, width, rows = qkv_t.shape
     heads_here = width // HD
     length = chunks * rows
     ends = jnp.cumsum(lengths_row)
@@ -112,12 +112,12 @@
     )
     return pl.pallas_call(
         attention_kernel,
-        out_shape=jax.ShapeDtypeStruct(query_t.shape, query_t.dtype),
+        out_shape=jax.ShapeDtypeStruct((chunks, width, rows), qkv_t.dtype),
         grid_spec=pltpu.PrefetchScalarGridSpec(
             num_scalar_prefetch=3,
             grid=(chunks,),
             in_specs=[
-                pl.BlockSpec((1, width, rows), lambda i, *_: (i, 0, 0)),
+                pl.BlockSpec((1, None, width, rows), lambda i, *_: (i, 2, 0, 0)),
                 pl.BlockSpec((chunks, 2, width, rows), lambda i, *_: (0, 0, 0, 0), pipeline_mode=pl.Buffered(1)),
                 pl.BlockSpec((None, 1, rows), lambda i, *_: (i, 0, 0)),
                 pl.BlockSpec((length, 1), lambda i, *_: (0, 0), pipeline_mode=pl.Buffered(1)),
@@ -132,7 +132,7 @@
         ),
         compiler_params=pltpu.CompilerParams(dimension_semantics=("arbitrary",)),
         cost_estimate=cost,
-    )(first_chunk, seg_first, seg_last, query_t, kv_t, qseg, kseg)
+    )(first_chunk, seg_first, seg_last, qkv_t, qkv_t, qseg, kseg)
 
 
 def to_heads(rows_in):
@@ -143,16 +143,20 @@
     return gathered.transpose(1, 2, 0)
 
 
-def kv_to_heads(key_rows, value_rows):
+def kv_to_heads(key_rows, value_rows, query_rows):
     tok_count = lax.axis_size("tok")
     token_rows, feature_width = key_rows.shape[1], key_rows.shape[2]
     stacked = jnp.stack(
         [
-            key_rows[0].reshape(token_rows, tok_count, feature_width // tok_count),
-            value_rows[0].reshape(token_rows, tok_count, feature_width // tok_count),
+            rows_in[0].reshape(token_rows, tok_count, feature_width // tok_count)
+            for rows_in in (key_rows, value_rows, query_rows)
         ],
         axis=2,
     )
+    return stacked
+
+
+def stacked_to_heads(stacked):
     gathered = lax.all_to_all(stacked, "tok", split_axis=1, concat_axis=1, tiled=True)
     return gathered.transpose(1, 2, 3, 0)
 
@@ -204,16 +208,14 @@
         jnp.broadcast_to(own_targets[None, :], (tok_count, own_targets.shape[0])),
         "tok", split_axis=0, concat_axis=0, tiled=True,
     )
-    query_split = query_rows[0].reshape(query_rows.shape[1], tok_count, -1)
-    targets, query_split = lax.optimization_barrier((targets, query_split))
-    query_t = lax.all_to_all(query_split, "tok", split_axis=1, concat_axis=1, tiled=True).transpose(1, 2, 0)
     by_head = relocate_by_head(cache_blocks)
-    by_head, key_rows, value_rows = lax.optimization_barrier((by_head, key_rows, value_rows))
+    stacked = kv_to_heads(key_rows, value_rows, query_rows)
+    by_head, stacked = lax.optimization_barrier((by_head, stacked))
     outgoing = place_slots(by_head, targets)
-    kv_t = kv_to_heads(key_rows, value_rows)
-    outgoing, query_t, kv_t = lax.optimization_barrier((outgoing, query_t, kv_t))
+    qkv_t = stacked_to_heads(stacked)
+    outgoing, qkv_t = lax.optimization_barrier((outgoing, qkv_t))
     moved_cache = relocate_groups(outgoing)
-    attended_t = attend_local(query_t, kv_t, lengths[0], segments)
+    attended_t = attend_local(qkv_t, lengths[0], segments)
     moved_cache, attended_t = lax.optimization_barrier((moved_cache, attended_t))
     attended = from_heads(attended_t)
     return (attended, moved_cache)

time: 359 us -> 356 us (level)
  starting transfers between devices: 37 us -> 30.8 us
  Pallas kernels: 57.9 us -> 61.9 us
  waiting for transfers between devices: 185 us -> 181 us
    all_to_all x2 -> x1, waiting for transfers between devices: 92.9 us -> 105 us  [stacked_to_heads(): lax.all_to_all(stacked, 'tok', split_axis=1, concat_axis=1, tiled=True)]
    optimization_barrier x3 -> x1, local copies, waits for them, and re-layouts: 15.9 us -> 4.05 us  [on_device(): by_head, stacked = lax.optimization_barrier((by_head, stacked))]
    unnamed x10 -> x14, local copies, waits for them, and re-layouts: 30.4 us -> 42.2 us
    all_to_all x1, waiting for transfers between devices: 39.5 us -> 27.7 us  [relocate_by_head(): return lax.all_to_all(split, 'tok', split_axis=2, concat_axis=2, tiled=True)]
    all_to_all x1, starting transfers between devices: 9.29 us -> 4.13 us  [on_device(): lax.all_to_all(jnp.broadcast_to(own_targets[None, :], (tok_count, own_tar...]
    all_to_all x1, waiting for transfers between devices: 21.1 us -> 16.9 us  [relocate_groups(): lax.all_to_all(outgoing, 'req', split_axis=0, concat_axis=0, tiled=True)]
    pallas_call x1, Pallas kernels: 57.9 us -> 61.9 us  [attend_local(): pl.pallas_call(attention_kernel, out_shape=jax.ShapeDtypeStruct((chunks,...]
    all_to_all x2 -> x1, starting transfers between devices: 10.6 us -> 7.28 us  [stacked_to_heads(): lax.all_to_all(stacked, 'tok', split_axis=1, concat_axis=1, tiled=True)]
  transfers between devices with their start and end apart: 6 -> 5, of which waited for: 5 -> 4; matrix products, arithmetic and copies ran while one was open for 20% -> 18% of each run, Pallas kernels for 16% -> 17%
where the time goes in v10:
time: 356 us; the launch traced here: 355 us
  waiting for transfers between devices  181 us (51%)
  Pallas kernels  61.9 us (17%)
  local copies, waits for them, and re-layouts  54.8 us (15%)
  starting transfers between devices  30.8 us (9%)
  other arithmetic  25.3 us (7%)
    all_to_all x1, waiting for transfers between devices, stacked_to_heads(): lax.all_to_all(stacked, 'tok', split_axis=1, concat_axis=1, tiled=True)  105 us
    pallas_call x1, Pallas kernels, attend_local(): pl.pallas_call(attention_kernel, out_shape=jax.ShapeDtypeStruct((chunks,...  61.9 us
    unnamed x14, local copies, waits for them, and re-layouts  42.2 us
    all_to_all x1, waiting for transfers between devices, from_heads(): lax.all_to_all(by_source, 'tok', split_axis=1, concat_axis=1, tiled=True)  31.1 us
    all_to_all x1, waiting for transfers between devices, relocate_by_head(): return lax.all_to_all(split, 'tok', split_axis=2, concat_axis=2, tiled=True)  27.7 us
    all_to_all x1, waiting for transfers between devices, relocate_groups(): lax.all_to_all(outgoing, 'req', split_axis=0, concat_axis=0, tiled=True)  16.9 us
    reduce_sum x1, other arithmetic, place_slots(): return jnp.sum(picked, axis=2, dtype=by_head.dtype)  14.6 us
    another operation x1, other arithmetic, kv_to_heads(): jnp.stack([rows_in[0].reshape(token_rows, tok_count, feature_width // tok...  9.68 us
  transfers between devices with their start and end apart: 5, of which 4 were waited for; matrix products, arithmetic and copies ran while one was open for 18% of the time, Pallas kernels for 17%

profile of v10, /device:TPU:1, one launch (start us, length us, event | category | flops | bytes accessed | tf_op | source)
XLA Modules:
  0.0 354.6 jit_solution(8573785576148836255)
XLA Ops:
  0.6 4.0 %copy.42 = bf16[1,8,2,32,3584]{4,1,3,2,0:T(8,128)(2,1)S(1)} copy(bf16[1,8,2,32,3584]{4,3,2,1,0:T(8,128)(2,1)} %param.10) | data formatting | bytes 7340032 | tf_op args[4]
  4.7 5.2 %copy.43 = bf16[8,2,16,2,3584]{4,3,1,0,2:T(2,128)(2,1)} copy(bf16[8,2,16,2,3584]{4,0,3,2,1:T(8,128)(2,1)S(1)} %bitcast.23) | data formatting | bytes 7340032 | tf_op jit(solution)/shard_map/reshape;squeeze | solution.py:175
  9.9 9.3 %all-to-all-start.1 = ((bf16[8,2,16,2,3584]{4,3,1,0,2:T(2,128)(2,1)}), bf16[8,2,16,2,3584]{4,3,1,0,2:T(2,128)(2,1)}, u32[]{:S(2)}, u32[]{:S(2)}) async-start(bf16[8,2,16,2,3584]{4,3,1,0,2:T(2,128)(2,1)} %copy.43), calls=%async_computation.1 | async-start | bytes 7340032 | tf_op jit(solution)/shard_map/all_to_all | solution.py:176
  19.1 5.9 %copy.46 = bf16[1,256,7168]{1,2,0:T(8,128)(2,1)} copy(bf16[1,256,7168]{2,1,0:T(8,128)(2,1)} %param.6) | data formatting | bytes 7340032 | tf_op args[0]
  25.1 5.9 %copy.44 = bf16[1,256,7168]{1,2,0:T(8,128)(2,1)} copy(bf16[1,256,7168]{2,1,0:T(8,128)(2,1)} %param.7) | data formatting | bytes 7340032 | tf_op args[1]
  31.0 0.0 copy-start.1
  31.0 5.9 %copy.45 = bf16[1,256,7168]{1,2,0:T(8,128)(2,1)} copy(bf16[1,256,7168]{2,1,0:T(8,128)(2,1)} %param.8) | data formatting | bytes 7340032 | tf_op args[2]
  36.9 27.7 %all-to-all-done.1 = bf16[8,2,16,2,3584]{4,3,1,0,2:T(2,128)(2,1)} async-done(((bf16[8,2,16,2,3584]{4,3,1,0,2:T(2,128)(2,1)}), bf16[8,2,16,2,3584]{4,3,1,0,2:T(2,128)(2,1)}, u32[]{:S(2)}, u32[]{:S(2)}) %all-to-all-start.1) | async-done | bytes 3670048 | tf_op jit(solution)/shard_map/all_to_all | solution.py:176
  64.6 0.0 copy-done.1
  64.6 0.6 broadcast_in_dim.60
  65.2 4.1 %all-to-all-start = ((s32[16,1,8]{2,1,0:T(1,128)}), s32[16,1,8]{2,1,0:T(1,128)S(1)}, u32[]{:S(2)}, u32[]{:S(2)}) async-start(s32[16,1,8]{2,1,0:T(1,128)} %broadcast_in_dim.60), calls=%async_computation | async-start | bytes 16384 | tf_op jit(solution)/shard_map/all_to_all | solution.py:207
  69.4 9.7 %pad_maximum_fusion = bf16[256,16,3,448]{0,3,2,1:T(8,128)(2,1)} fusion(bf16[256,16,1,448]{0,3,2,1:T(8,128)(2,1)} %bitcast.24, bf16[256,16,1,448]{0,3,2,1:T(8,128)(2,1)} %bitcast.26, bf16[256,16,1,448]{0,3,2,1:T(8,128)(2,1)} %bitcast.25), kind=kLoop, calls=%fused_computation.1 | loop fusion | flops 11010048 | bytes 22020096 | tf_op jit(solution)/shard_map/stack | solution.py:149
  79.0 0.0 all-to-all-done
  79.0 7.3 %all-to-all-start.2 = ((bf16[256,16,3,448]{0,3,2,1:T(8,128)(2,1)}), bf16[256,16,3,448]{0,3,2,1:T(8,128)(2,1)}, u32[]{:S(2)}, u32[]{:S(2)}) async-start(bf16[256,16,3,448]{0,3,2,1:T(8,128)(2,1)} %pad_maximum_fusion), calls=%async_computation.2 | async-start | bytes 22020096 | tf_op jit(solution)/shard_map/all_to_all | solution.py:160
  86.3 0.1 copy.41
  86.4 0.1 convert_reduce_fusion.1
  86.5 4.0 %copy.47 = bf16[8,2,16,2,3584]{4,2,3,1,0:T(8,128)(2,1)S(1)} copy(bf16[8,2,16,2,3584]{4,3,1,0,2:T(2,128)(2,1)} %all-to-all-done.1) | data formatting | bytes 7340032 | tf_op jit(solution)/shard_map/optimization_barrier | solution.py:213
  90.6 14.6 %select_reduce_fusion = bf16[8,2,2,16,2,3584]{5,3,4,2,1,0:T(8,128)(2,1)} fusion(pred[8,2,8,16]{3,2,1,0:T(8,128)(4,1)S(1)} %broadcast_and_fusion, bf16[8,2,16,2,3584]{4,2,3,1,0:T(8,128)(2,1)S(1)} %copy.47), kind=kLoop, calls=%fused_computation | loop fusion | flops 55050240 | bytes 11012096 | tf_op jit(solution)/shard_map/reduce_sum | solution.py:194
  105.2 105.3 %all-to-all-done.2 = bf16[256,16,3,448]{0,3,2,1:T(8,128)(2,1)} async-done(((bf16[256,16,3,448]{0,3,2,1:T(8,128)(2,1)}), bf16[256,16,3,448]{0,3,2,1:T(8,128)(2,1)}, u32[]{:S(2)}, u32[]{:S(2)}) %all-to-all-start.2) | async-done | bytes 11010080 | tf_op jit(solution)/shard_map/all_to_all | solution.py:160
  210.5 0.0 copy-start.2
  210.5 5.2 %all-to-all-start.3 = ((bf16[8,2,2,16,2,3584]{5,3,4,2,1,0:T(8,128)(2,1)}), bf16[8,2,2,16,2,3584]{5,3,4,2,1,0:T(8,128)(2,1)}, u32[]{:S(2)}, u32[]{:S(2)}) async-start(bf16[8,2,2,16,2,3584]{5,3,4,2,1,0:T(8,128)(2,1)} %select_reduce_fusion), calls=%async_computation.3 | async-start | bytes 14680064 | tf_op jit(solution)/shard_map/all_to_all | solution.py:198
  215.6 0.0 copy-done.2
  215.6 0.2 reduce-window.4
  215.8 0.1 convert_reduce_fusion
  215.9 0.0 copy-start
  215.9 0.1 slice.6.seg_first_ref
  216.0 0.0 copy-start.3
  216.1 0.7 slice.7.seg_last_ref
  216.7 2.0 copy.48.kseg_ref
  218.7 0.1 select_reduce_fusion.1
  218.8 0.5 and_select_fusion.first_ref
  219.3 0.0 copy-done
  219.3 0.0 copy-done.3
  219.3 61.9 %shard_map.77 = bf16[16,448,256]{2,1,0:T(8,128)(2,1)} custom-call(s32[16]{0:T(128)} %and_select_fusion.first_ref, s32[16]{0:T(128)} %copy-done.3, s32[16]{0:T(128)} %slice.7.seg_last_ref, bf16[16,3,448,256]{3,2,1,0:T(8,128)(2,1)} %bitcast.8.q_ref.kv_ref, bf16[16,3,448,256]{3,2,1,0:T(8,128)(2,1)} %bitcast.8.q_ref.kv_ref, s32[16,1,256]{2,1,0:T(1,128)} %bitcast.29, ...), custom_call_target="tpu_custom_call" | custom-call | flops 15032385536 | bytes 14680064 | tf_op jit(solution)/shard_map/pallas_call | solution.py:113
  281.2 16.9 %all-to-all-done.3 = bf16[8,2,2,16,2,3584]{5,3,4,2,1,0:T(8,128)(2,1)} async-done(((bf16[8,2,2,16,2,3584]{5,3,4,2,1,0:T(8,128)(2,1)}), bf16[8,2,2,16,2,3584]{5,3,4,2,1,0:T(8,128)(2,1)}, u32[]{:S(2)}, u32[]{:S(2)}) %all-to-all-start.3) | async-done | bytes 7340064 | tf_op jit(solution)/shard_map/all_to_all | solution.py:198
  298.2 4.9 %all-to-all-start.4 = ((bf16[256,16,448]{0,2,1:T(8,128)(2,1)}), bf16[256,16,448]{0,2,1:T(8,128)(2,1)}, u32[]{:S(2)}, u32[]{:S(2)}) async-start(bf16[256,16,448]{0,2,1:T(8,128)(2,1)} %bitcast.27), calls=%async_computation.4 | async-start | bytes 7340032 | tf_op jit(solution)/shard_map/all_to_all | solution.py:167
  303.1 14.5 %copy.50 = bf16[1,8,2,2,16,2,3584]{6,5,4,3,2,1,0:T(2,128)(2,1)} copy(bf16[1,8,2,2,16,2,3584]{6,4,5,3,2,1,0:T(8,128)(2,1)} %bitcast.9) | data formatting | bytes 14680064
  317.6 31.1 %all-to-all-done.4 = bf16[256,16,448]{0,2,1:T(8,128)(2,1)} async-done(((bf16[256,16,448]{0,2,1:T(8,128)(2,1)}), bf16[256,16,448]{0,2,1:T(8,128)(2,1)}, u32[]{:S(2)}, u32[]{:S(2)}) %all-to-all-start.4) | async-done | bytes 3670048 | tf_op jit(solution)/shard_map/all_to_all | solution.py:167
  348.7 5.9 %copy.49 = bf16[1,256,7168]{2,1,0:T(8,128)(2,1)} copy(bf16[1,256,7168]{1,2,0:T(8,128)(2,1)} %bitcast.17) | data formatting | bytes 7340032
  (5 shorter events, 0.0 us)
Async XLA Ops:
  9.9 54.8 %all-to-all-start.1 = ((bf16[8,2,16,2,3584]{4,3,1,0,2:T(2,128)(2,1)}), bf16[8,2,16,2,3584]{4,3,1,0,2:T(2,128)(2,1)}, u32[]{:S(2)}, u32[]{:S(2)}) async-start(bf16[8,2,16,2,3584]{4,3,1,0,2:T(2,128)(2,1)} %copy.43), calls=%async_computation.1 | async-start | bytes 7340032 | tf_op jit(solution)/shard_map/all_to_all | solution.py:176
  31.0 33.7 %copy-start.1 = (s32[1,8,1]{1,2,0:T(1,128)S(1)}, s32[1,8,1]{1,2,0:T(1,128)}, u32[]{:S(2)}) copy-start(s32[1,8,1]{1,2,0:T(1,128)} %param.11) | copy-start | bytes 100
  65.2 13.8 %all-to-all-start = ((s32[16,1,8]{2,1,0:T(1,128)}), s32[16,1,8]{2,1,0:T(1,128)S(1)}, u32[]{:S(2)}, u32[]{:S(2)}) async-start(s32[16,1,8]{2,1,0:T(1,128)} %broadcast_in_dim.60), calls=%async_computation | async-start | bytes 16384 | tf_op jit(solution)/shard_map/all_to_all | solution.py:207
  79.0 131.4 %all-to-all-start.2 = ((bf16[256,16,3,448]{0,3,2,1:T(8,128)(2,1)}), bf16[256,16,3,448]{0,3,2,1:T(8,128)(2,1)}, u32[]{:S(2)}, u32[]{:S(2)}) async-start(bf16[256,16,3,448]{0,3,2,1:T(8,128)(2,1)} %pad_maximum_fusion), calls=%async_computation.2 | async-start | bytes 22020096 | tf_op jit(solution)/shard_map/all_to_all | solution.py:160
  210.5 5.2 %copy-start.2 = (s32[1,6]{1,0:T(1,128)S(1)}, s32[1,6]{1,0:T(1,128)}, u32[]{:S(2)}) copy-start(s32[1,6]{1,0:T(1,128)} %param.9) | copy-start | bytes 76
  210.5 87.7 %all-to-all-start.3 = ((bf16[8,2,2,16,2,3584]{5,3,4,2,1,0:T(8,128)(2,1)}), bf16[8,2,2,16,2,3584]{5,3,4,2,1,0:T(8,128)(2,1)}, u32[]{:S(2)}, u32[]{:S(2)}) async-start(bf16[8,2,2,16,2,3584]{5,3,4,2,1,0:T(8,128)(2,1)} %select_reduce_fusion), calls=%async_computation.3 | async-start | bytes 14680064 | tf_op jit(solution)/shard_map/all_to_all | solution.py:198
  215.9 3.4 copy-start
  216.0 3.3 copy-start.3
  298.2 50.5 %all-to-all-start.4 = ((bf16[256,16,448]{0,2,1:T(8,128)(2,1)}), bf16[256,16,448]{0,2,1:T(8,128)(2,1)}, u32[]{:S(2)}, u32[]{:S(2)}) async-start(bf16[256,16,448]{0,2,1:T(8,128)(2,1)} %bitcast.27), calls=%async_computation.4 | async-start | bytes 7340032 | tf_op jit(solution)/shard_map/all_to_all | solution.py:167

commit v11 on v10

--- a/solution.py
+++ b/solution.py
@@ -146,14 +146,14 @@
 def kv_to_heads(key_rows, value_rows, query_rows):
     tok_count = lax.axis_size("tok")
     token_rows, feature_width = key_rows.shape[1], key_rows.shape[2]
-    stacked = jnp.stack(
+    by_chunk = jnp.stack(
         [
-            rows_in[0].reshape(token_rows, tok_count, feature_width // tok_count)
+            rows_in[0].reshape(token_rows, tok_count, feature_width // tok_count).transpose(1, 2, 0)
             for rows_in in (key_rows, value_rows, query_rows)
         ],
-        axis=2,
-    )
-    return stacked
+        axis=1,
+    )
+    return by_chunk.transpose(3, 0, 1, 2)
 
 
 def stacked_to_heads(stacked):

time: 356 us -> 356 us (level)
    another operation x2 -> x1, other arithmetic: 9.86 us -> 0.18 us  [the longest x1 9.68 us: kv_to_heads(): jnp.stack([rows_in[0].reshape(token_rows, tok_count, feature_width // tok...]
    transpose x0 -> x1, other arithmetic: none -> 9.68 us  [kv_to_heads(): return by_chunk.transpose(3, 0, 1, 2)]
where the time goes in v11:
time: 356 us; the launch traced here: 355 us
  waiting for transfers between devices  183 us (51%)
  Pallas kernels  59.6 us (17%)
  local copies, waits for them, and re-layouts  54.8 us (15%)
  starting transfers between devices  30.8 us (9%)
  other arithmetic  25.3 us (7%)
    all_to_all x1, waiting for transfers between devices, stacked_to_heads(): lax.all_to_all(stacked, 'tok', split_axis=1, concat_axis=1, tiled=True)  105 us
    pallas_call x1, Pallas kernels, attend_local(): pl.pallas_call(attention_kernel, out_shape=jax.ShapeDtypeStruct((chunks,...  59.6 us
    unnamed x14, local copies, waits for them, and re-layouts  42.2 us
    all_to_all x1, waiting for transfers between devices, from_heads(): lax.all_to_all(by_source, 'tok', split_axis=1, concat_axis=1, tiled=True)  31.1 us
    all_to_all x1, waiting for transfers between devices, relocate_by_head(): return lax.all_to_all(split, 'tok', split_axis=2, concat_axis=2, tiled=True)  27.7 us
    all_to_all x1, waiting for transfers between devices, relocate_groups(): lax.all_to_all(outgoing, 'req', split_axis=0, concat_axis=0, tiled=True)  19.3 us
    reduce_sum x1, other arithmetic, place_slots(): return jnp.sum(picked, axis=2, dtype=by_head.dtype)  14.6 us
    transpose x1, other arithmetic, kv_to_heads(): return by_chunk.transpose(3, 0, 1, 2)  9.68 us
  transfers between devices with their start and end apart: 5, of which 4 were waited for; matrix products, arithmetic and copies ran while one was open for 18% of the time, Pallas kernels for 17%

profile of v11, /device:TPU:1, one launch (start us, length us, event | category | flops | bytes accessed | tf_op | source)
XLA Modules:
  0.0 354.6 jit_solution(8573785576148836255)
XLA Ops:
  0.6 4.0 %copy.42 = bf16[1,8,2,32,3584]{4,1,3,2,0:T(8,128)(2,1)S(1)} copy(bf16[1,8,2,32,3584]{4,3,2,1,0:T(8,128)(2,1)} %param.10) | data formatting | bytes 7340032 | tf_op args[4]
  4.7 5.2 %copy.43 = bf16[8,2,16,2,3584]{4,3,1,0,2:T(2,128)(2,1)} copy(bf16[8,2,16,2,3584]{4,0,3,2,1:T(8,128)(2,1)S(1)} %bitcast.37) | data formatting | bytes 7340032 | tf_op jit(solution)/shard_map/reshape;squeeze | solution.py:175
  9.9 9.3 %all-to-all-start.1 = ((bf16[8,2,16,2,3584]{4,3,1,0,2:T(2,128)(2,1)}), bf16[8,2,16,2,3584]{4,3,1,0,2:T(2,128)(2,1)}, u32[]{:S(2)}, u32[]{:S(2)}) async-start(bf16[8,2,16,2,3584]{4,3,1,0,2:T(2,128)(2,1)} %copy.43), calls=%async_computation.1 | async-start | bytes 7340032 | tf_op jit(solution)/shard_map/all_to_all | solution.py:176
  19.1 5.9 %copy.46 = bf16[1,256,7168]{1,2,0:T(8,128)(2,1)} copy(bf16[1,256,7168]{2,1,0:T(8,128)(2,1)} %param.6) | data formatting | bytes 7340032 | tf_op args[0]
  25.1 5.9 %copy.44 = bf16[1,256,7168]{1,2,0:T(8,128)(2,1)} copy(bf16[1,256,7168]{2,1,0:T(8,128)(2,1)} %param.7) | data formatting | bytes 7340032 | tf_op args[1]
  31.0 0.0 copy-start.1
  31.0 5.9 %copy.45 = bf16[1,256,7168]{1,2,0:T(8,128)(2,1)} copy(bf16[1,256,7168]{2,1,0:T(8,128)(2,1)} %param.8) | data formatting | bytes 7340032 | tf_op args[2]
  36.9 27.7 %all-to-all-done.1 = bf16[8,2,16,2,3584]{4,3,1,0,2:T(2,128)(2,1)} async-done(((bf16[8,2,16,2,3584]{4,3,1,0,2:T(2,128)(2,1)}), bf16[8,2,16,2,3584]{4,3,1,0,2:T(2,128)(2,1)}, u32[]{:S(2)}, u32[]{:S(2)}) %all-to-all-start.1) | async-done | bytes 3670048 | tf_op jit(solution)/shard_map/all_to_all | solution.py:176
  64.6 0.0 copy-done.1
  64.6 0.6 broadcast_in_dim.60
  65.2 4.1 %all-to-all-start = ((s32[16,1,8]{2,1,0:T(1,128)}), s32[16,1,8]{2,1,0:T(1,128)S(1)}, u32[]{:S(2)}, u32[]{:S(2)}) async-start(s32[16,1,8]{2,1,0:T(1,128)} %broadcast_in_dim.60), calls=%async_computation | async-start | bytes 16384 | tf_op jit(solution)/shard_map/all_to_all | solution.py:207
  69.4 9.7 %maximum_bitcast_fusion = bf16[256,16,3,448]{0,3,2,1:T(8,128)(2,1)} fusion(bf16[16,1,448,256]{3,2,1,0:T(8,128)(2,1)} %bitcast.38, bf16[16,1,448,256]{3,2,1,0:T(8,128)(2,1)} %bitcast.40, bf16[16,1,448,256]{3,2,1,0:T(8,128)(2,1)} %bitcast.39), kind=kLoop, calls=%fused_computation.1 | loop fusion | flops 11010048 | bytes 22020096 | tf_op jit(solution)/shard_map/transpose | solution.py:156
  79.0 0.0 all-to-all-done
  79.0 7.3 %all-to-all-start.2 = ((bf16[256,16,3,448]{0,3,2,1:T(8,128)(2,1)}), bf16[256,16,3,448]{0,3,2,1:T(8,128)(2,1)}, u32[]{:S(2)}, u32[]{:S(2)}) async-start(bf16[256,16,3,448]{0,3,2,1:T(8,128)(2,1)} %maximum_bitcast_fusion), calls=%async_computation.2 | async-start | bytes 22020096 | tf_op jit(solution)/shard_map/all_to_all | solution.py:160
  86.3 0.1 copy.41
  86.4 0.1 convert_reduce_fusion.1
  86.5 4.0 %copy.47 = bf16[8,2,16,2,3584]{4,2,3,1,0:T(8,128)(2,1)S(1)} copy(bf16[8,2,16,2,3584]{4,3,1,0,2:T(2,128)(2,1)} %all-to-all-done.1) | data formatting | bytes 7340032 | tf_op jit(solution)/shard_map/optimization_barrier | solution.py:213
  90.6 14.6 %select_reduce_fusion = bf16[8,2,2,16,2,3584]{5,3,4,2,1,0:T(8,128)(2,1)} fusion(pred[8,2,8,16]{3,2,1,0:T(8,128)(4,1)S(1)} %broadcast_and_fusion, bf16[8,2,16,2,3584]{4,2,3,1,0:T(8,128)(2,1)S(1)} %copy.47), kind=kLoop, calls=%fused_computation | loop fusion | flops 55050240 | bytes 11012096 | tf_op jit(solution)/shard_map/reduce_sum | solution.py:194
  105.2 105.3 %all-to-all-done.2 = bf16[256,16,3,448]{0,3,2,1:T(8,128)(2,1)} async-done(((bf16[256,16,3,448]{0,3,2,1:T(8,128)(2,1)}), bf16[256,16,3,448]{0,3,2,1:T(8,128)(2,1)}, u32[]{:S(2)}, u32[]{:S(2)}) %all-to-all-start.2) | async-done | bytes 11010080 | tf_op jit(solution)/shard_map/all_to_all | solution.py:160
  210.5 0.0 copy-start.2
  210.5 5.2 %all-to-all-start.3 = ((bf16[8,2,2,16,2,3584]{5,3,4,2,1,0:T(8,128)(2,1)}), bf16[8,2,2,16,2,3584]{5,3,4,2,1,0:T(8,128)(2,1)}, u32[]{:S(2)}, u32[]{:S(2)}) async-start(bf16[8,2,2,16,2,3584]{5,3,4,2,1,0:T(8,128)(2,1)} %select_reduce_fusion), calls=%async_computation.3 | async-start | bytes 14680064 | tf_op jit(solution)/shard_map/all_to_all | solution.py:198
  215.6 0.0 copy-done.2
  215.6 0.2 reduce-window.4
  215.8 0.1 convert_reduce_fusion
  215.9 0.0 copy-start
  215.9 0.1 slice.6.seg_first_ref
  216.0 0.0 copy-start.3
  216.1 0.7 slice.7.seg_last_ref
  216.7 2.0 copy.48.kseg_ref
  218.7 0.1 select_reduce_fusion.1
  218.8 0.5 and_select_fusion.first_ref
  219.3 0.0 copy-done
  219.3 0.0 copy-done.3
  219.3 59.6 %shard_map.77 = bf16[16,448,256]{2,1,0:T(8,128)(2,1)} custom-call(s32[16]{0:T(128)} %and_select_fusion.first_ref, s32[16]{0:T(128)} %copy-done.3, s32[16]{0:T(128)} %slice.7.seg_last_ref, bf16[16,3,448,256]{3,2,1,0:T(8,128)(2,1)} %bitcast.15.q_ref.kv_ref, bf16[16,3,448,256]{3,2,1,0:T(8,128)(2,1)} %bitcast.15.q_ref.kv_ref, s32[16,1,256]{2,1,0:T(1,128)} %bitcast.43, ...), custom_call_target="tpu_custom_call" | custom-call | flops 15032385536 | bytes 14680064 | tf_op jit(solution)/shard_map/pallas_call | solution.py:113
  278.9 19.3 %all-to-all-done.3 = bf16[8,2,2,16,2,3584]{5,3,4,2,1,0:T(8,128)(2,1)} async-done(((bf16[8,2,2,16,2,3584]{5,3,4,2,1,0:T(8,128)(2,1)}), bf16[8,2,2,16,2,3584]{5,3,4,2,1,0:T(8,128)(2,1)}, u32[]{:S(2)}, u32[]{:S(2)}) %all-to-all-start.3) | async-done | bytes 7340064 | tf_op jit(solution)/shard_map/all_to_all | solution.py:198
  298.2 4.9 %all-to-all-start.4 = ((bf16[256,16,448]{0,2,1:T(8,128)(2,1)}), bf16[256,16,448]{0,2,1:T(8,128)(2,1)}, u32[]{:S(2)}, u32[]{:S(2)}) async-start(bf16[256,16,448]{0,2,1:T(8,128)(2,1)} %bitcast.41), calls=%async_computation.4 | async-start | bytes 7340032 | tf_op jit(solution)/shard_map/all_to_all | solution.py:167
  303.1 14.5 %copy.50 = bf16[1,8,2,2,16,2,3584]{6,5,4,3,2,1,0:T(2,128)(2,1)} copy(bf16[1,8,2,2,16,2,3584]{6,4,5,3,2,1,0:T(8,128)(2,1)} %bitcast.16) | data formatting | bytes 14680064
  317.6 31.1 %all-to-all-done.4 = bf16[256,16,448]{0,2,1:T(8,128)(2,1)} async-done(((bf16[256,16,448]{0,2,1:T(8,128)(2,1)}), bf16[256,16,448]{0,2,1:T(8,128)(2,1)}, u32[]{:S(2)}, u32[]{:S(2)}) %all-to-all-start.4) | async-done | bytes 3670048 | tf_op jit(solution)/shard_map/all_to_all | solution.py:167
  348.7 5.9 %copy.49 = bf16[1,256,7168]{2,1,0:T(8,128)(2,1)} copy(bf16[1,256,7168]{1,2,0:T(8,128)(2,1)} %bitcast.24) | data formatting | bytes 7340032
  (5 shorter events, 0.0 us)
Async XLA Ops:
  9.9 54.8 %all-to-all-start.1 = ((bf16[8,2,16,2,3584]{4,3,1,0,2:T(2,128)(2,1)}), bf16[8,2,16,2,3584]{4,3,1,0,2:T(2,128)(2,1)}, u32[]{:S(2)}, u32[]{:S(2)}) async-start(bf16[8,2,16,2,3584]{4,3,1,0,2:T(2,128)(2,1)} %copy.43), calls=%async_computation.1 | async-start | bytes 7340032 | tf_op jit(solution)/shard_map/all_to_all | solution.py:176
  31.0 33.7 %copy-start.1 = (s32[1,8,1]{1,2,0:T(1,128)S(1)}, s32[1,8,1]{1,2,0:T(1,128)}, u32[]{:S(2)}) copy-start(s32[1,8,1]{1,2,0:T(1,128)} %param.11) | copy-start | bytes 100
  65.2 13.8 %all-to-all-start = ((s32[16,1,8]{2,1,0:T(1,128)}), s32[16,1,8]{2,1,0:T(1,128)S(1)}, u32[]{:S(2)}, u32[]{:S(2)}) async-start(s32[16,1,8]{2,1,0:T(1,128)} %broadcast_in_dim.60), calls=%async_computation | async-start | bytes 16384 | tf_op jit(solution)/shard_map/all_to_all | solution.py:207
  79.0 131.4 %all-to-all-start.2 = ((bf16[256,16,3,448]{0,3,2,1:T(8,128)(2,1)}), bf16[256,16,3,448]{0,3,2,1:T(8,128)(2,1)}, u32[]{:S(2)}, u32[]{:S(2)}) async-start(bf16[256,16,3,448]{0,3,2,1:T(8,128)(2,1)} %maximum_bitcast_fusion), calls=%async_computation.2 | async-start | bytes 22020096 | tf_op jit(solution)/shard_map/all_to_all | solution.py:160
  210.5 5.2 %copy-start.2 = (s32[1,6]{1,0:T(1,128)S(1)}, s32[1,6]{1,0:T(1,128)}, u32[]{:S(2)}) copy-start(s32[1,6]{1,0:T(1,128)} %param.9) | copy-start | bytes 76
  210.5 87.7 %all-to-all-start.3 = ((bf16[8,2,2,16,2,3584]{5,3,4,2,1,0:T(8,128)(2,1)}), bf16[8,2,2,16,2,3584]{5,3,4,2,1,0:T(8,128)(2,1)}, u32[]{:S(2)}, u32[]{:S(2)}) async-start(bf16[8,2,2,16,2,3584]{5,3,4,2,1,0:T(8,128)(2,1)} %select_reduce_fusion), calls=%async_computation.3 | async-start | bytes 14680064 | tf_op jit(solution)/shard_map/all_to_all | solution.py:198
  215.9 3.4 copy-start
  216.0 3.3 copy-start.3
  298.2 50.5 %all-to-all-start.4 = ((bf16[256,16,448]{0,2,1:T(8,128)(2,1)}), bf16[256,16,448]{0,2,1:T(8,128)(2,1)}, u32[]{:S(2)}, u32[]{:S(2)}) async-start(bf16[256,16,448]{0,2,1:T(8,128)(2,1)} %bitcast.41), calls=%async_computation.4 | async-start | bytes 7340032 | tf_op jit(solution)/shard_map/all_to_all | solution.py:167

commit v12 on v11

--- a/solution.py
+++ b/solution.py
@@ -203,13 +203,14 @@
     span_length = query_rows.shape[1] * lax.axis_size("tok")
     segments = segment_ids(lengths[0], span_length)
     tok_count = lax.axis_size("tok")
+    by_head = relocate_by_head(cache_blocks)
+    stacked = kv_to_heads(key_rows, value_rows, query_rows)
+    stacked, destinations = lax.optimization_barrier((stacked, destinations))
     own_targets = destinations[0, :, 0]
     targets = lax.all_to_all(
         jnp.broadcast_to(own_targets[None, :], (tok_count, own_targets.shape[0])),
         "tok", split_axis=0, concat_axis=0, tiled=True,
     )
-    by_head = relocate_by_head(cache_blocks)
-    stacked = kv_to_heads(key_rows, value_rows, query_rows)
     by_head, stacked = lax.optimization_barrier((by_head, stacked))
     outgoing = place_slots(by_head, targets)
     qkv_t = stacked_to_heads(stacked)

time: 356 us -> 351 us (0.986)
    all_to_all x1, waiting for transfers between devices: 27.7 us -> 18 us  [relocate_by_head(): return lax.all_to_all(split, 'tok', split_axis=2, concat_axis=2, tiled=True)]
    all_to_all x1, waiting for transfers between devices: 0.01 us -> 6.97 us  [on_device(): lax.all_to_all(jnp.broadcast_to(own_targets[None, :], (tok_count, own_tar...]
  transfers between devices with their start and end apart: 5 -> 5, of which waited for: 4 -> 5; matrix products, arithmetic and copies ran while one was open for 18% -> 18% of each run, Pallas kernels for 17% -> 17%
where the time goes in v12:
time: 351 us; the launch traced here: 350 us
  waiting for transfers between devices  180 us (51%)
  Pallas kernels  60.4 us (17%)
  local copies, waits for them, and re-layouts  54.8 us (16%)
  starting transfers between devices  28.8 us (8%)
  other arithmetic  25.3 us (7%)
    all_to_all x1, waiting for transfers between devices, stacked_to_heads(): lax.all_to_all(stacked, 'tok', split_axis=1, concat_axis=1, tiled=True)  105 us
    pallas_call x1, Pallas kernels, attend_local(): pl.pallas_call(attention_kernel, out_shape=jax.ShapeDtypeStruct((chunks,...  60.4 us
    unnamed x14, local copies, waits for them, and re-layouts  42.2 us
    all_to_all x1, waiting for transfers between devices, from_heads(): lax.all_to_all(by_source, 'tok', split_axis=1, concat_axis=1, tiled=True)  31.1 us
    all_to_all x1, waiting for transfers between devices, relocate_groups(): lax.all_to_all(outgoing, 'req', split_axis=0, concat_axis=0, tiled=True)  18.5 us
    all_to_all x1, waiting for transfers between devices, relocate_by_head(): return lax.all_to_all(split, 'tok', split_axis=2, concat_axis=2, tiled=True)  18 us
    reduce_sum x1, other arithmetic, place_slots(): return jnp.sum(picked, axis=2, dtype=by_head.dtype)  14.6 us
    transpose x1, other arithmetic, kv_to_heads(): return by_chunk.transpose(3, 0, 1, 2)  9.68 us
  transfers between devices with their start and end apart: 5, of which 5 were waited for; matrix products, arithmetic and copies ran while one was open for 18% of the time, Pallas kernels for 17%

profile of v12, /device:TPU:1, one launch (start us, length us, event | category | flops | bytes accessed | tf_op | source)
XLA Modules:
  0.0 350.0 jit_solution(11926162496204020037)
XLA Ops:
  0.6 4.0 %copy.45 = bf16[1,8,2,32,3584]{4,1,3,2,0:T(8,128)(2,1)S(1)} copy(bf16[1,8,2,32,3584]{4,3,2,1,0:T(8,128)(2,1)} %param.10) | data formatting | bytes 7340032 | tf_op args[4]
  4.7 5.1 %copy.46 = bf16[8,2,16,2,3584]{4,3,1,0,2:T(2,128)(2,1)} copy(bf16[8,2,16,2,3584]{4,0,3,2,1:T(8,128)(2,1)S(1)} %bitcast.37) | data formatting | bytes 7340032 | tf_op jit(solution)/shard_map/reshape;squeeze | solution.py:175
  9.8 9.3 %all-to-all-start.1 = ((bf16[8,2,16,2,3584]{4,3,1,0,2:T(2,128)(2,1)}), bf16[8,2,16,2,3584]{4,3,1,0,2:T(2,128)(2,1)}, u32[]{:S(2)}, u32[]{:S(2)}) async-start(bf16[8,2,16,2,3584]{4,3,1,0,2:T(2,128)(2,1)} %copy.46), calls=%async_computation.1 | async-start | bytes 7340032 | tf_op jit(solution)/shard_map/all_to_all | solution.py:176
  19.1 5.9 %copy.43 = bf16[1,256,7168]{1,2,0:T(8,128)(2,1)} copy(bf16[1,256,7168]{2,1,0:T(8,128)(2,1)} %param.6) | data formatting | bytes 7340032 | tf_op args[0]
  25.0 5.9 %copy.41 = bf16[1,256,7168]{1,2,0:T(8,128)(2,1)} copy(bf16[1,256,7168]{2,1,0:T(8,128)(2,1)} %param.7) | data formatting | bytes 7340032 | tf_op args[1]
  31.0 5.9 %copy.42 = bf16[1,256,7168]{1,2,0:T(8,128)(2,1)} copy(bf16[1,256,7168]{2,1,0:T(8,128)(2,1)} %param.8) | data formatting | bytes 7340032 | tf_op args[2]
  36.9 0.0 copy-start.1
  36.9 9.7 %maximum_bitcast_fusion = bf16[256,16,3,448]{0,3,2,1:T(8,128)(2,1)} fusion(bf16[16,1,448,256]{3,2,1,0:T(8,128)(2,1)} %bitcast.38, bf16[16,1,448,256]{3,2,1,0:T(8,128)(2,1)} %bitcast.40, bf16[16,1,448,256]{3,2,1,0:T(8,128)(2,1)} %bitcast.39), kind=kLoop, calls=%fused_computation.1 | loop fusion | flops 11010048 | bytes 22020096 | tf_op jit(solution)/shard_map/transpose | solution.py:156
  46.5 18.0 %all-to-all-done.1 = bf16[8,2,16,2,3584]{4,3,1,0,2:T(2,128)(2,1)} async-done(((bf16[8,2,16,2,3584]{4,3,1,0,2:T(2,128)(2,1)}), bf16[8,2,16,2,3584]{4,3,1,0,2:T(2,128)(2,1)}, u32[]{:S(2)}, u32[]{:S(2)}) %all-to-all-start.1) | async-done | bytes 3670048 | tf_op jit(solution)/shard_map/all_to_all | solution.py:176
  64.6 0.0 copy-done.1
  64.6 0.6 broadcast_in_dim.60
  65.2 4.2 %all-to-all-start = ((s32[16,1,8]{2,1,0:T(1,128)}), s32[16,1,8]{2,1,0:T(1,128)S(1)}, u32[]{:S(2)}, u32[]{:S(2)}) async-start(s32[16,1,8]{2,1,0:T(1,128)} %broadcast_in_dim.60), calls=%async_computation | async-start | bytes 16384 | tf_op jit(solution)/shard_map/all_to_all | solution.py:210
  69.4 7.0 %all-to-all-done = s32[16,1,8]{2,1,0:T(1,128)S(1)} async-done(((s32[16,1,8]{2,1,0:T(1,128)}), s32[16,1,8]{2,1,0:T(1,128)S(1)}, u32[]{:S(2)}, u32[]{:S(2)}) %all-to-all-start) | async-done | bytes 544 | tf_op jit(solution)/shard_map/all_to_all | solution.py:210
  76.3 5.3 %all-to-all-start.2 = ((bf16[256,16,3,448]{0,3,2,1:T(8,128)(2,1)}), bf16[256,16,3,448]{0,3,2,1:T(8,128)(2,1)}, u32[]{:S(2)}, u32[]{:S(2)}) async-start(bf16[256,16,3,448]{0,3,2,1:T(8,128)(2,1)} %maximum_bitcast_fusion), calls=%async_computation.2 | async-start | bytes 22020096 | tf_op jit(solution)/shard_map/all_to_all | solution.py:160
  81.6 0.1 copy.44
  81.7 0.1 convert_reduce_fusion.1
  81.8 4.0 %copy.47 = bf16[8,2,16,2,3584]{4,2,3,1,0:T(8,128)(2,1)S(1)} copy(bf16[8,2,16,2,3584]{4,3,1,0,2:T(2,128)(2,1)} %all-to-all-done.1) | data formatting | bytes 7340032 | tf_op jit(solution)/shard_map/optimization_barrier | solution.py:214
  85.9 14.6 %select_reduce_fusion = bf16[8,2,2,16,2,3584]{5,3,4,2,1,0:T(8,128)(2,1)} fusion(pred[8,2,8,16]{3,2,1,0:T(8,128)(4,1)S(1)} %broadcast_and_fusion, bf16[8,2,16,2,3584]{4,2,3,1,0:T(8,128)(2,1)S(1)} %copy.47), kind=kLoop, calls=%fused_computation | loop fusion | flops 55050240 | bytes 11012096 | tf_op jit(solution)/shard_map/reduce_sum | solution.py:194
  100.5 105.3 %all-to-all-done.2 = bf16[256,16,3,448]{0,3,2,1:T(8,128)(2,1)} async-done(((bf16[256,16,3,448]{0,3,2,1:T(8,128)(2,1)}), bf16[256,16,3,448]{0,3,2,1:T(8,128)(2,1)}, u32[]{:S(2)}, u32[]{:S(2)}) %all-to-all-start.2) | async-done | bytes 11010080 | tf_op jit(solution)/shard_map/all_to_all | solution.py:160
  205.8 0.0 copy-start.2
  205.8 5.2 %all-to-all-start.3 = ((bf16[8,2,2,16,2,3584]{5,3,4,2,1,0:T(8,128)(2,1)}), bf16[8,2,2,16,2,3584]{5,3,4,2,1,0:T(8,128)(2,1)}, u32[]{:S(2)}, u32[]{:S(2)}) async-start(bf16[8,2,2,16,2,3584]{5,3,4,2,1,0:T(8,128)(2,1)} %select_reduce_fusion), calls=%async_computation.3 | async-start | bytes 14680064 | tf_op jit(solution)/shard_map/all_to_all | solution.py:198
  211.0 0.0 copy-done.2
  211.0 0.2 reduce-window.4
  211.2 0.1 convert_reduce_fusion
  211.3 0.0 copy-start
  211.3 0.1 slice.6.seg_first_ref
  211.4 0.0 copy-start.3
  211.4 0.7 slice.7.seg_last_ref
  212.1 2.0 copy.48.kseg_ref
  214.1 0.1 select_reduce_fusion.1
  214.2 0.5 and_select_fusion.first_ref
  214.7 0.0 copy-done
  214.7 0.0 copy-done.3
  214.7 60.4 %shard_map.77 = bf16[16,448,256]{2,1,0:T(8,128)(2,1)} custom-call(s32[16]{0:T(128)} %and_select_fusion.first_ref, s32[16]{0:T(128)} %copy-done.3, s32[16]{0:T(128)} %slice.7.seg_last_ref, bf16[16,3,448,256]{3,2,1,0:T(8,128)(2,1)} %bitcast.15.q_ref.kv_ref, bf16[16,3,448,256]{3,2,1,0:T(8,128)(2,1)} %bitcast.15.q_ref.kv_ref, s32[16,1,256]{2,1,0:T(1,128)} %bitcast.43, ...), custom_call_target="tpu_custom_call" | custom-call | flops 15032385536 | bytes 14680064 | tf_op jit(solution)/shard_map/pallas_call | solution.py:113
  275.1 18.5 %all-to-all-done.3 = bf16[8,2,2,16,2,3584]{5,3,4,2,1,0:T(8,128)(2,1)} async-done(((bf16[8,2,2,16,2,3584]{5,3,4,2,1,0:T(8,128)(2,1)}), bf16[8,2,2,16,2,3584]{5,3,4,2,1,0:T(8,128)(2,1)}, u32[]{:S(2)}, u32[]{:S(2)}) %all-to-all-start.3) | async-done | bytes 7340064 | tf_op jit(solution)/shard_map/all_to_all | solution.py:198
  293.5 4.9 %all-to-all-start.4 = ((bf16[256,16,448]{0,2,1:T(8,128)(2,1)}), bf16[256,16,448]{0,2,1:T(8,128)(2,1)}, u32[]{:S(2)}, u32[]{:S(2)}) async-start(bf16[256,16,448]{0,2,1:T(8,128)(2,1)} %bitcast.41), calls=%async_computation.4 | async-start | bytes 7340032 | tf_op jit(solution)/shard_map/all_to_all | solution.py:167
  298.5 14.5 %copy.50 = bf16[1,8,2,2,16,2,3584]{6,5,4,3,2,1,0:T(2,128)(2,1)} copy(bf16[1,8,2,2,16,2,3584]{6,4,5,3,2,1,0:T(8,128)(2,1)} %bitcast.16) | data formatting | bytes 14680064
  313.0 31.1 %all-to-all-done.4 = bf16[256,16,448]{0,2,1:T(8,128)(2,1)} async-done(((bf16[256,16,448]{0,2,1:T(8,128)(2,1)}), bf16[256,16,448]{0,2,1:T(8,128)(2,1)}, u32[]{:S(2)}, u32[]{:S(2)}) %all-to-all-start.4) | async-done | bytes 3670048 | tf_op jit(solution)/shard_map/all_to_all | solution.py:167
  344.0 5.9 %copy.49 = bf16[1,256,7168]{2,1,0:T(8,128)(2,1)} copy(bf16[1,256,7168]{1,2,0:T(8,128)(2,1)} %bitcast.24) | data formatting | bytes 7340032
  (5 shorter events, 0.0 us)
Async XLA Ops:
  9.8 54.8 %all-to-all-start.1 = ((bf16[8,2,16,2,3584]{4,3,1,0,2:T(2,128)(2,1)}), bf16[8,2,16,2,3584]{4,3,1,0,2:T(2,128)(2,1)}, u32[]{:S(2)}, u32[]{:S(2)}) async-start(bf16[8,2,16,2,3584]{4,3,1,0,2:T(2,128)(2,1)} %copy.46), calls=%async_computation.1 | async-start | bytes 7340032 | tf_op jit(solution)/shard_map/all_to_all | solution.py:176
  36.9 27.7 %copy-start.1 = (s32[1,8,1]{1,2,0:T(1,128)S(1)}, s32[1,8,1]{1,2,0:T(1,128)}, u32[]{:S(2)}) copy-start(s32[1,8,1]{1,2,0:T(1,128)} %param.11) | copy-start | bytes 100
  65.2 11.2 %all-to-all-start = ((s32[16,1,8]{2,1,0:T(1,128)}), s32[16,1,8]{2,1,0:T(1,128)S(1)}, u32[]{:S(2)}, u32[]{:S(2)}) async-start(s32[16,1,8]{2,1,0:T(1,128)} %broadcast_in_dim.60), calls=%async_computation | async-start | bytes 16384 | tf_op jit(solution)/shard_map/all_to_all | solution.py:210
  76.3 129.5 %all-to-all-start.2 = ((bf16[256,16,3,448]{0,3,2,1:T(8,128)(2,1)}), bf16[256,16,3,448]{0,3,2,1:T(8,128)(2,1)}, u32[]{:S(2)}, u32[]{:S(2)}) async-start(bf16[256,16,3,448]{0,3,2,1:T(8,128)(2,1)} %maximum_bitcast_fusion), calls=%async_computation.2 | async-start | bytes 22020096 | tf_op jit(solution)/shard_map/all_to_all | solution.py:160
  205.8 5.2 %copy-start.2 = (s32[1,6]{1,0:T(1,128)S(1)}, s32[1,6]{1,0:T(1,128)}, u32[]{:S(2)}) copy-start(s32[1,6]{1,0:T(1,128)} %param.9) | copy-start | bytes 76
  205.8 87.7 %all-to-all-start.3 = ((bf16[8,2,2,16,2,3584]{5,3,4,2,1,0:T(8,128)(2,1)}), bf16[8,2,2,16,2,3584]{5,3,4,2,1,0:T(8,128)(2,1)}, u32[]{:S(2)}, u32[]{:S(2)}) async-start(bf16[8,2,2,16,2,3584]{5,3,4,2,1,0:T(8,128)(2,1)} %select_reduce_fusion), calls=%async_computation.3 | async-start | bytes 14680064 | tf_op jit(solution)/shard_map/all_to_all | solution.py:198
  211.3 3.4 copy-start
  211.4 3.3 copy-start.3
  293.5 50.5 %all-to-all-start.4 = ((bf16[256,16,448]{0,2,1:T(8,128)(2,1)}), bf16[256,16,448]{0,2,1:T(8,128)(2,1)}, u32[]{:S(2)}, u32[]{:S(2)}) async-start(bf16[256,16,448]{0,2,1:T(8,128)(2,1)} %bitcast.41), calls=%async_computation.4 | async-start | bytes 7340032 | tf_op jit(solution)/shard_map/all_to_all | solution.py:167

commit v13 on v11

--- a/solution.py
+++ b/solution.py
@@ -208,6 +208,7 @@
         jnp.broadcast_to(own_targets[None, :], (tok_count, own_targets.shape[0])),
         "tok", split_axis=0, concat_axis=0, tiled=True,
     )
+    targets, cache_blocks = lax.optimization_barrier((targets, cache_blocks))
     by_head = relocate_by_head(cache_blocks)
     stacked = kv_to_heads(key_rows, value_rows, query_rows)
     by_head, stacked = lax.optimization_barrier((by_head, stacked))

time: 356 us -> 352 us (0.989)
  blocking collectives: 0 us -> 16.1 us
  starting transfers between devices: 30.8 us -> 20.5 us
  Pallas kernels: 59.6 us -> 54.8 us
  waiting for transfers between devices: 183 us -> 179 us
    all_to_all x0 -> x1, blocking collectives: none -> 16.1 us  [on_device(): lax.all_to_all(jnp.broadcast_to(own_targets[None, :], (tok_count, own_tar...]
    all_to_all x1, waiting for transfers between devices: 27.7 us -> 18.1 us  [relocate_by_head(): return lax.all_to_all(split, 'tok', split_axis=2, concat_axis=2, tiled=True)]
    pallas_call x1, Pallas kernels: 59.6 us -> 54.8 us  [attend_local(): pl.pallas_call(attention_kernel, out_shape=jax.ShapeDtypeStruct((chunks,...]
    all_to_all x1, waiting for transfers between devices: 19.3 us -> 24 us  [relocate_groups(): lax.all_to_all(outgoing, 'req', split_axis=0, concat_axis=0, tiled=True)]
    all_to_all x1, starting transfers between devices: 9.29 us -> 4.91 us  [relocate_by_head(): return lax.all_to_all(split, 'tok', split_axis=2, concat_axis=2, tiled=True)]
    all_to_all x1 -> x0, starting transfers between devices: 4.13 us -> none  [on_device(): lax.all_to_all(jnp.broadcast_to(own_targets[None, :], (tok_count, own_tar...]
    optimization_barrier x0 -> x1, local copies, waits for them, and re-layouts: none -> 4.05 us  [on_device(): targets, cache_blocks = lax.optimization_barrier((targets, cache_blocks))]
    unnamed x14 -> x11, local copies, waits for them, and re-layouts: 42.2 us -> 38.2 us
  transfers between devices with their start and end apart: 5 -> 4, of which waited for: 4 -> 4; matrix products, arithmetic and copies ran while one was open for 18% -> 18% of each run, Pallas kernels for 17% -> 16%
where the time goes in v13:
time: 352 us; the launch traced here: 351 us
  waiting for transfers between devices  179 us (51%)
  local copies, waits for them, and re-layouts  54.9 us (16%)
  Pallas kernels  54.8 us (16%)
  other arithmetic  25.3 us (7%)
  starting transfers between devices  20.5 us (6%)
  blocking collectives  16.1 us (5%)
    all_to_all x1, waiting for transfers between devices, stacked_to_heads(): lax.all_to_all(stacked, 'tok', split_axis=1, concat_axis=1, tiled=True)  105 us
    pallas_call x1, Pallas kernels, attend_local(): pl.pallas_call(attention_kernel, out_shape=jax.ShapeDtypeStruct((chunks,...  54.8 us
    unnamed x11, local copies, waits for them, and re-layouts  38.2 us
    all_to_all x1, waiting for transfers between devices, from_heads(): lax.all_to_all(by_source, 'tok', split_axis=1, concat_axis=1, tiled=True)  31.1 us
    all_to_all x1, waiting for transfers between devices, relocate_groups(): lax.all_to_all(outgoing, 'req', split_axis=0, concat_axis=0, tiled=True)  24 us
    all_to_all x1, waiting for transfers between devices, relocate_by_head(): return lax.all_to_all(split, 'tok', split_axis=2, concat_axis=2, tiled=True)  18.1 us
    all_to_all x1, blocking collectives, on_device(): lax.all_to_all(jnp.broadcast_to(own_targets[None, :], (tok_count, own_tar...  16.1 us
    reduce_sum x1, other arithmetic, place_slots(): return jnp.sum(picked, axis=2, dtype=by_head.dtype)  14.6 us
  transfers between devices with their start and end apart: 4, of which 4 were waited for; matrix products, arithmetic and copies ran while one was open for 18% of the time, Pallas kernels for 16%

profile of v13, /device:TPU:1, one launch (start us, length us, event | category | flops | bytes accessed | tf_op | source)
XLA Modules:
  0.0 350.9 jit_solution(7208155835063655897)
XLA Ops:
  0.6 0.7 broadcast_in_dim.60
  1.3 16.1 %all_to_all.29 = s32[16,1,8]{2,1,0:T(1,128)S(1)} all-to-all(s32[16,1,8]{2,1,0:T(1,128)S(1)} %broadcast_in_dim.60), channel_id=1, replica_groups=mesh['tok'=16,'req'=8] {'tok'}, dimensions={0} | all-to-all | bytes 1024 | tf_op jit(solution)/shard_map/all_to_all | solution.py:207
  17.4 0.1 copy.41
  17.4 4.1 %copy.42 = bf16[1,8,2,32,3584]{4,1,3,2,0:T(8,128)(2,1)S(1)} copy(bf16[1,8,2,32,3584]{4,3,2,1,0:T(8,128)(2,1)} %param.10) | data formatting | bytes 7340032 | tf_op jit(solution)/shard_map/optimization_barrier | solution.py:211
  21.5 5.1 %copy.43 = bf16[8,2,16,2,3584]{4,3,1,0,2:T(2,128)(2,1)} copy(bf16[8,2,16,2,3584]{4,0,3,2,1:T(8,128)(2,1)S(1)} %bitcast.36) | data formatting | bytes 7340032 | tf_op jit(solution)/shard_map/reshape;squeeze | solution.py:175
  26.6 4.9 %all-to-all-start.1 = ((bf16[8,2,16,2,3584]{4,3,1,0,2:T(2,128)(2,1)}), bf16[8,2,16,2,3584]{4,3,1,0,2:T(2,128)(2,1)}, u32[]{:S(2)}, u32[]{:S(2)}) async-start(bf16[8,2,16,2,3584]{4,3,1,0,2:T(2,128)(2,1)} %copy.43), calls=%async_computation.1 | async-start | bytes 7340032 | tf_op jit(solution)/shard_map/all_to_all | solution.py:176
  31.5 5.9 %copy.46 = bf16[1,256,7168]{1,2,0:T(8,128)(2,1)} copy(bf16[1,256,7168]{2,1,0:T(8,128)(2,1)} %param.6) | data formatting | bytes 7340032 | tf_op args[0]
  37.4 5.9 %copy.44 = bf16[1,256,7168]{1,2,0:T(8,128)(2,1)} copy(bf16[1,256,7168]{2,1,0:T(8,128)(2,1)} %param.7) | data formatting | bytes 7340032 | tf_op args[1]
  43.4 5.9 %copy.45 = bf16[1,256,7168]{1,2,0:T(8,128)(2,1)} copy(bf16[1,256,7168]{2,1,0:T(8,128)(2,1)} %param.8) | data formatting | bytes 7340032 | tf_op args[2]
  49.3 9.7 %maximum_bitcast_fusion = bf16[256,16,3,448]{0,3,2,1:T(8,128)(2,1)} fusion(bf16[16,1,448,256]{3,2,1,0:T(8,128)(2,1)} %bitcast.37, bf16[16,1,448,256]{3,2,1,0:T(8,128)(2,1)} %bitcast.39, bf16[16,1,448,256]{3,2,1,0:T(8,128)(2,1)} %bitcast.38), kind=kLoop, calls=%fused_computation.1 | loop fusion | flops 11010048 | bytes 22020096 | tf_op jit(solution)/shard_map/transpose | solution.py:156
  58.9 18.1 %all-to-all-done.1 = bf16[8,2,16,2,3584]{4,3,1,0,2:T(2,128)(2,1)} async-done(((bf16[8,2,16,2,3584]{4,3,1,0,2:T(2,128)(2,1)}), bf16[8,2,16,2,3584]{4,3,1,0,2:T(2,128)(2,1)}, u32[]{:S(2)}, u32[]{:S(2)}) %all-to-all-start.1) | async-done | bytes 3670048 | tf_op jit(solution)/shard_map/all_to_all | solution.py:176
  77.1 5.5 %all-to-all-start.2 = ((bf16[256,16,3,448]{0,3,2,1:T(8,128)(2,1)}), bf16[256,16,3,448]{0,3,2,1:T(8,128)(2,1)}, u32[]{:S(2)}, u32[]{:S(2)}) async-start(bf16[256,16,3,448]{0,3,2,1:T(8,128)(2,1)} %maximum_bitcast_fusion), calls=%async_computation.2 | async-start | bytes 22020096 | tf_op jit(solution)/shard_map/all_to_all | solution.py:160
  82.6 0.1 convert_reduce_fusion.1
  82.8 4.0 %copy.47 = bf16[8,2,16,2,3584]{4,2,3,1,0:T(8,128)(2,1)S(1)} copy(bf16[8,2,16,2,3584]{4,3,1,0,2:T(2,128)(2,1)} %all-to-all-done.1) | data formatting | bytes 7340032 | tf_op jit(solution)/shard_map/optimization_barrier | solution.py:214
  86.8 14.6 %select_reduce_fusion = bf16[8,2,2,16,2,3584]{5,3,4,2,1,0:T(8,128)(2,1)} fusion(pred[8,2,8,16]{3,2,1,0:T(8,128)(4,1)S(1)} %broadcast_and_fusion, bf16[8,2,16,2,3584]{4,2,3,1,0:T(8,128)(2,1)S(1)} %copy.47), kind=kLoop, calls=%fused_computation | loop fusion | flops 55050240 | bytes 11012096 | tf_op jit(solution)/shard_map/reduce_sum | solution.py:194
  101.4 105.4 %all-to-all-done.2 = bf16[256,16,3,448]{0,3,2,1:T(8,128)(2,1)} async-done(((bf16[256,16,3,448]{0,3,2,1:T(8,128)(2,1)}), bf16[256,16,3,448]{0,3,2,1:T(8,128)(2,1)}, u32[]{:S(2)}, u32[]{:S(2)}) %all-to-all-start.2) | async-done | bytes 11010080 | tf_op jit(solution)/shard_map/all_to_all | solution.py:160
  206.8 0.0 copy-start.1
  206.8 5.2 %all-to-all-start.3 = ((bf16[8,2,2,16,2,3584]{5,3,4,2,1,0:T(8,128)(2,1)}), bf16[8,2,2,16,2,3584]{5,3,4,2,1,0:T(8,128)(2,1)}, u32[]{:S(2)}, u32[]{:S(2)}) async-start(bf16[8,2,2,16,2,3584]{5,3,4,2,1,0:T(8,128)(2,1)} %select_reduce_fusion), calls=%async_computation.3 | async-start | bytes 14680064 | tf_op jit(solution)/shard_map/all_to_all | solution.py:198
  212.0 0.0 copy-done.1
  212.0 0.2 reduce-window.4
  212.2 0.1 convert_reduce_fusion
  212.3 0.0 copy-start
  212.3 0.1 slice.6.seg_first_ref
  212.4 0.0 copy-start.2
  212.4 0.7 slice.7.seg_last_ref
  213.1 2.0 copy.48.kseg_ref
  215.1 0.1 select_reduce_fusion.1
  215.1 0.5 and_select_fusion.first_ref
  215.7 0.0 copy-done
  215.7 0.0 copy-done.2
  215.7 54.8 %shard_map.77 = bf16[16,448,256]{2,1,0:T(8,128)(2,1)} custom-call(s32[16]{0:T(128)} %and_select_fusion.first_ref, s32[16]{0:T(128)} %copy-done.2, s32[16]{0:T(128)} %slice.7.seg_last_ref, bf16[16,3,448,256]{3,2,1,0:T(8,128)(2,1)} %bitcast.15.q_ref.kv_ref, bf16[16,3,448,256]{3,2,1,0:T(8,128)(2,1)} %bitcast.15.q_ref.kv_ref, s32[16,1,256]{2,1,0:T(1,128)} %bitcast.42, ...), custom_call_target="tpu_custom_call" | custom-call | flops 15032385536 | bytes 14680064 | tf_op jit(solution)/shard_map/pallas_call | solution.py:113
  270.5 24.0 %all-to-all-done.3 = bf16[8,2,2,16,2,3584]{5,3,4,2,1,0:T(8,128)(2,1)} async-done(((bf16[8,2,2,16,2,3584]{5,3,4,2,1,0:T(8,128)(2,1)}), bf16[8,2,2,16,2,3584]{5,3,4,2,1,0:T(8,128)(2,1)}, u32[]{:S(2)}, u32[]{:S(2)}) %all-to-all-start.3) | async-done | bytes 7340064 | tf_op jit(solution)/shard_map/all_to_all | solution.py:198
  294.5 4.9 %all-to-all-start.4 = ((bf16[256,16,448]{0,2,1:T(8,128)(2,1)}), bf16[256,16,448]{0,2,1:T(8,128)(2,1)}, u32[]{:S(2)}, u32[]{:S(2)}) async-start(bf16[256,16,448]{0,2,1:T(8,128)(2,1)} %bitcast.40), calls=%async_computation.4 | async-start | bytes 7340032 | tf_op jit(solution)/shard_map/all_to_all | solution.py:167
  299.5 14.5 %copy.50 = bf16[1,8,2,2,16,2,3584]{6,5,4,3,2,1,0:T(2,128)(2,1)} copy(bf16[1,8,2,2,16,2,3584]{6,4,5,3,2,1,0:T(8,128)(2,1)} %bitcast.16) | data formatting | bytes 14680064
  314.0 31.1 %all-to-all-done.4 = bf16[256,16,448]{0,2,1:T(8,128)(2,1)} async-done(((bf16[256,16,448]{0,2,1:T(8,128)(2,1)}), bf16[256,16,448]{0,2,1:T(8,128)(2,1)}, u32[]{:S(2)}, u32[]{:S(2)}) %all-to-all-start.4) | async-done | bytes 3670048 | tf_op jit(solution)/shard_map/all_to_all | solution.py:167
  345.0 5.9 %copy.49 = bf16[1,256,7168]{2,1,0:T(8,128)(2,1)} copy(bf16[1,256,7168]{1,2,0:T(8,128)(2,1)} %bitcast.24) | data formatting | bytes 7340032
  (5 shorter events, 0.0 us)
Async XLA Ops:
  26.6 50.5 %all-to-all-start.1 = ((bf16[8,2,16,2,3584]{4,3,1,0,2:T(2,128)(2,1)}), bf16[8,2,16,2,3584]{4,3,1,0,2:T(2,128)(2,1)}, u32[]{:S(2)}, u32[]{:S(2)}) async-start(bf16[8,2,16,2,3584]{4,3,1,0,2:T(2,128)(2,1)} %copy.43), calls=%async_computation.1 | async-start | bytes 7340032 | tf_op jit(solution)/shard_map/all_to_all | solution.py:176
  77.1 129.7 %all-to-all-start.2 = ((bf16[256,16,3,448]{0,3,2,1:T(8,128)(2,1)}), bf16[256,16,3,448]{0,3,2,1:T(8,128)(2,1)}, u32[]{:S(2)}, u32[]{:S(2)}) async-start(bf16[256,16,3,448]{0,3,2,1:T(8,128)(2,1)} %maximum_bitcast_fusion), calls=%async_computation.2 | async-start | bytes 22020096 | tf_op jit(solution)/shard_map/all_to_all | solution.py:160
  206.8 5.2 %copy-start.1 = (s32[1,6]{1,0:T(1,128)S(1)}, s32[1,6]{1,0:T(1,128)}, u32[]{:S(2)}) copy-start(s32[1,6]{1,0:T(1,128)} %param.9) | copy-start | bytes 76
  206.8 87.7 %all-to-all-start.3 = ((bf16[8,2,2,16,2,3584]{5,3,4,2,1,0:T(8,128)(2,1)}), bf16[8,2,2,16,2,3584]{5,3,4,2,1,0:T(8,128)(2,1)}, u32[]{:S(2)}, u32[]{:S(2)}) async-start(bf16[8,2,2,16,2,3584]{5,3,4,2,1,0:T(8,128)(2,1)} %select_reduce_fusion), calls=%async_computation.3 | async-start | bytes 14680064 | tf_op jit(solution)/shard_map/all_to_all | solution.py:198
  212.3 3.4 copy-start
  212.4 3.3 copy-start.2
  294.5 50.5 %all-to-all-start.4 = ((bf16[256,16,448]{0,2,1:T(8,128)(2,1)}), bf16[256,16,448]{0,2,1:T(8,128)(2,1)}, u32[]{:S(2)}, u32[]{:S(2)}) async-start(bf16[256,16,448]{0,2,1:T(8,128)(2,1)} %bitcast.40), calls=%async_computation.4 | async-start | bytes 7340032 | tf_op jit(solution)/shard_map/all_to_all | solution.py:167

commit v14 on v11

--- a/solution.py
+++ b/solution.py
@@ -208,6 +208,7 @@
         jnp.broadcast_to(own_targets[None, :], (tok_count, own_targets.shape[0])),
         "tok", split_axis=0, concat_axis=0, tiled=True,
     )
+    targets, key_rows, value_rows, query_rows = lax.optimization_barrier((targets, key_rows, value_rows, query_rows))
     by_head = relocate_by_head(cache_blocks)
     stacked = kv_to_heads(key_rows, value_rows, query_rows)
     by_head, stacked = lax.optimization_barrier((by_head, stacked))

time: 356 us -> 348 us (0.978)
  waiting for transfers between devices: 183 us -> 177 us
    optimization_barrier x0 -> x3, local copies, waits for them, and re-layouts: none -> 17.7 us  [on_device(): lax.optimization_barrier((targets, key_rows, value_rows, query_rows))]
    unnamed x14 -> x9, local copies, waits for them, and re-layouts: 42.2 us -> 24.5 us
    all_to_all x1, waiting for transfers between devices: 27.7 us -> 18 us  [relocate_by_head(): return lax.all_to_all(split, 'tok', split_axis=2, concat_axis=2, tiled=True)]
    all_to_all x1, starting transfers between devices: 4.13 us -> 9.29 us  [on_device(): lax.all_to_all(jnp.broadcast_to(own_targets[None, :], (tok_count, own_tar...]
  transfers between devices with their start and end apart: 5 -> 5, of which waited for: 4 -> 4; matrix products, arithmetic and copies ran while one was open for 18% -> 21% of each run, Pallas kernels for 17% -> 16%
where the time goes in v14:
time: 348 us; the launch traced here: 347 us
  waiting for transfers between devices  177 us (51%)
  Pallas kernels  56.3 us (16%)
  local copies, waits for them, and re-layouts  55.5 us (16%)
  starting transfers between devices  32.1 us (9%)
  other arithmetic  25.3 us (7%)
    all_to_all x1, waiting for transfers between devices, stacked_to_heads(): lax.all_to_all(stacked, 'tok', split_axis=1, concat_axis=1, tiled=True)  105 us
    pallas_call x1, Pallas kernels, attend_local(): pl.pallas_call(attention_kernel, out_shape=jax.ShapeDtypeStruct((chunks,...  56.3 us
    all_to_all x1, waiting for transfers between devices, from_heads(): lax.all_to_all(by_source, 'tok', split_axis=1, concat_axis=1, tiled=True)  31.1 us
    unnamed x9, local copies, waits for them, and re-layouts  24.5 us
    all_to_all x1, waiting for transfers between devices, relocate_groups(): lax.all_to_all(outgoing, 'req', split_axis=0, concat_axis=0, tiled=True)  22.5 us
    all_to_all x1, waiting for transfers between devices, relocate_by_head(): return lax.all_to_all(split, 'tok', split_axis=2, concat_axis=2, tiled=True)  18 us
    optimization_barrier x3, local copies, waits for them, and re-layouts, on_device(): lax.optimization_barrier((targets, key_rows, value_rows, query_rows))  17.7 us
    reduce_sum x1, other arithmetic, place_slots(): return jnp.sum(picked, axis=2, dtype=by_head.dtype)  14.6 us
  transfers between devices with their start and end apart: 5, of which 4 were waited for; matrix products, arithmetic and copies ran while one was open for 21% of the time, Pallas kernels for 16%

profile of v14, /device:TPU:1, one launch (start us, length us, event | category | flops | bytes accessed | tf_op | source)
XLA Modules:
  0.0 346.9 jit_solution(1041070555270381826)
XLA Ops:
  0.6 1.3 broadcast_in_dim.60
  1.9 9.3 %all-to-all-start = ((s32[16,1,8]{2,1,0:T(1,128)}), s32[16,1,8]{2,1,0:T(1,128)S(1)}, u32[]{:S(2)}, u32[]{:S(2)}) async-start(s32[16,1,8]{2,1,0:T(1,128)} %broadcast_in_dim.60), calls=%async_computation | async-start | bytes 16384 | tf_op jit(solution)/shard_map/all_to_all | solution.py:207
  11.2 4.0 %copy.42 = bf16[1,8,2,32,3584]{4,1,3,2,0:T(8,128)(2,1)S(1)} copy(bf16[1,8,2,32,3584]{4,3,2,1,0:T(8,128)(2,1)} %param.10) | data formatting | bytes 7340032 | tf_op args[4]
  15.2 5.1 %copy.43 = bf16[8,2,16,2,3584]{4,3,1,0,2:T(2,128)(2,1)} copy(bf16[8,2,16,2,3584]{4,0,3,2,1:T(8,128)(2,1)S(1)} %bitcast.36) | data formatting | bytes 7340032 | tf_op jit(solution)/shard_map/reshape;squeeze | solution.py:175
  20.4 0.0 all-to-all-done
  20.4 7.2 %all-to-all-start.1 = ((bf16[8,2,16,2,3584]{4,3,1,0,2:T(2,128)(2,1)}), bf16[8,2,16,2,3584]{4,3,1,0,2:T(2,128)(2,1)}, u32[]{:S(2)}, u32[]{:S(2)}) async-start(bf16[8,2,16,2,3584]{4,3,1,0,2:T(2,128)(2,1)} %copy.43), calls=%async_computation.1 | async-start | bytes 7340032 | tf_op jit(solution)/shard_map/all_to_all | solution.py:176
  27.6 0.1 copy.41
  27.7 5.9 %copy.44 = bf16[1,256,7168]{1,2,0:T(8,128)(2,1)} copy(bf16[1,256,7168]{2,1,0:T(8,128)(2,1)} %param.7) | data formatting | bytes 7340032 | tf_op jit(solution)/shard_map/optimization_barrier | solution.py:211
  33.6 5.9 %copy.45 = bf16[1,256,7168]{1,2,0:T(8,128)(2,1)} copy(bf16[1,256,7168]{2,1,0:T(8,128)(2,1)} %param.8) | data formatting | bytes 7340032 | tf_op jit(solution)/shard_map/optimization_barrier | solution.py:211
  39.5 5.9 %copy.46 = bf16[1,256,7168]{1,2,0:T(8,128)(2,1)} copy(bf16[1,256,7168]{2,1,0:T(8,128)(2,1)} %param.6) | data formatting | bytes 7340032 | tf_op jit(solution)/shard_map/optimization_barrier | solution.py:211
  45.4 9.7 %maximum_bitcast_fusion = bf16[256,16,3,448]{0,3,2,1:T(8,128)(2,1)} fusion(bf16[16,1,448,256]{3,2,1,0:T(8,128)(2,1)} %bitcast.39, bf16[16,1,448,256]{3,2,1,0:T(8,128)(2,1)} %bitcast.38, bf16[16,1,448,256]{3,2,1,0:T(8,128)(2,1)} %bitcast.37), kind=kLoop, calls=%fused_computation.1 | loop fusion | flops 11010048 | bytes 22020096 | tf_op jit(solution)/shard_map/transpose | solution.py:156
  55.1 18.0 %all-to-all-done.1 = bf16[8,2,16,2,3584]{4,3,1,0,2:T(2,128)(2,1)} async-done(((bf16[8,2,16,2,3584]{4,3,1,0,2:T(2,128)(2,1)}), bf16[8,2,16,2,3584]{4,3,1,0,2:T(2,128)(2,1)}, u32[]{:S(2)}, u32[]{:S(2)}) %all-to-all-start.1) | async-done | bytes 3670048 | tf_op jit(solution)/shard_map/all_to_all | solution.py:176
  73.1 5.5 %all-to-all-start.2 = ((bf16[256,16,3,448]{0,3,2,1:T(8,128)(2,1)}), bf16[256,16,3,448]{0,3,2,1:T(8,128)(2,1)}, u32[]{:S(2)}, u32[]{:S(2)}) async-start(bf16[256,16,3,448]{0,3,2,1:T(8,128)(2,1)} %maximum_bitcast_fusion), calls=%async_computation.2 | async-start | bytes 22020096 | tf_op jit(solution)/shard_map/all_to_all | solution.py:160
  78.6 0.1 convert_reduce_fusion.1
  78.7 4.0 %copy.47 = bf16[8,2,16,2,3584]{4,2,3,1,0:T(8,128)(2,1)S(1)} copy(bf16[8,2,16,2,3584]{4,3,1,0,2:T(2,128)(2,1)} %all-to-all-done.1) | data formatting | bytes 7340032 | tf_op jit(solution)/shard_map/optimization_barrier | solution.py:214
  82.8 14.6 %select_reduce_fusion = bf16[8,2,2,16,2,3584]{5,3,4,2,1,0:T(8,128)(2,1)} fusion(pred[8,2,8,16]{3,2,1,0:T(8,128)(4,1)S(1)} %broadcast_and_fusion, bf16[8,2,16,2,3584]{4,2,3,1,0:T(8,128)(2,1)S(1)} %copy.47), kind=kLoop, calls=%fused_computation | loop fusion | flops 55050240 | bytes 11012096 | tf_op jit(solution)/shard_map/reduce_sum | solution.py:194
  97.4 105.4 %all-to-all-done.2 = bf16[256,16,3,448]{0,3,2,1:T(8,128)(2,1)} async-done(((bf16[256,16,3,448]{0,3,2,1:T(8,128)(2,1)}), bf16[256,16,3,448]{0,3,2,1:T(8,128)(2,1)}, u32[]{:S(2)}, u32[]{:S(2)}) %all-to-all-start.2) | async-done | bytes 11010080 | tf_op jit(solution)/shard_map/all_to_all | solution.py:160
  202.8 0.0 copy-start.1
  202.8 5.2 %all-to-all-start.3 = ((bf16[8,2,2,16,2,3584]{5,3,4,2,1,0:T(8,128)(2,1)}), bf16[8,2,2,16,2,3584]{5,3,4,2,1,0:T(8,128)(2,1)}, u32[]{:S(2)}, u32[]{:S(2)}) async-start(bf16[8,2,2,16,2,3584]{5,3,4,2,1,0:T(8,128)(2,1)} %select_reduce_fusion), calls=%async_computation.3 | async-start | bytes 14680064 | tf_op jit(solution)/shard_map/all_to_all | solution.py:198
  208.0 0.0 copy-done.1
  208.0 0.2 reduce-window.4
  208.2 0.1 convert_reduce_fusion
  208.3 0.0 copy-start
  208.3 0.1 slice.6.seg_first_ref
  208.4 0.0 copy-start.2
  208.4 0.7 slice.7.seg_last_ref
  209.1 2.0 copy.48.kseg_ref
  211.0 0.1 select_reduce_fusion.1
  211.1 0.5 and_select_fusion.first_ref
  211.7 0.0 copy-done
  211.7 0.0 copy-done.2
  211.7 56.3 %shard_map.77 = bf16[16,448,256]{2,1,0:T(8,128)(2,1)} custom-call(s32[16]{0:T(128)} %and_select_fusion.first_ref, s32[16]{0:T(128)} %copy-done.2, s32[16]{0:T(128)} %slice.7.seg_last_ref, bf16[16,3,448,256]{3,2,1,0:T(8,128)(2,1)} %bitcast.15.q_ref.kv_ref, bf16[16,3,448,256]{3,2,1,0:T(8,128)(2,1)} %bitcast.15.q_ref.kv_ref, s32[16,1,256]{2,1,0:T(1,128)} %bitcast.42, ...), custom_call_target="tpu_custom_call" | custom-call | flops 15032385536 | bytes 14680064 | tf_op jit(solution)/shard_map/pallas_call | solution.py:113
  268.0 22.5 %all-to-all-done.3 = bf16[8,2,2,16,2,3584]{5,3,4,2,1,0:T(8,128)(2,1)} async-done(((bf16[8,2,2,16,2,3584]{5,3,4,2,1,0:T(8,128)(2,1)}), bf16[8,2,2,16,2,3584]{5,3,4,2,1,0:T(8,128)(2,1)}, u32[]{:S(2)}, u32[]{:S(2)}) %all-to-all-start.3) | async-done | bytes 7340064 | tf_op jit(solution)/shard_map/all_to_all | solution.py:198
  290.5 4.9 %all-to-all-start.4 = ((bf16[256,16,448]{0,2,1:T(8,128)(2,1)}), bf16[256,16,448]{0,2,1:T(8,128)(2,1)}, u32[]{:S(2)}, u32[]{:S(2)}) async-start(bf16[256,16,448]{0,2,1:T(8,128)(2,1)} %bitcast.40), calls=%async_computation.4 | async-start | bytes 7340032 | tf_op jit(solution)/shard_map/all_to_all | solution.py:167
  295.5 14.5 %copy.50 = bf16[1,8,2,2,16,2,3584]{6,5,4,3,2,1,0:T(2,128)(2,1)} copy(bf16[1,8,2,2,16,2,3584]{6,4,5,3,2,1,0:T(8,128)(2,1)} %bitcast.16) | data formatting | bytes 14680064
  310.0 31.1 %all-to-all-done.4 = bf16[256,16,448]{0,2,1:T(8,128)(2,1)} async-done(((bf16[256,16,448]{0,2,1:T(8,128)(2,1)}), bf16[256,16,448]{0,2,1:T(8,128)(2,1)}, u32[]{:S(2)}, u32[]{:S(2)}) %all-to-all-start.4) | async-done | bytes 3670048 | tf_op jit(solution)/shard_map/all_to_all | solution.py:167
  341.0 5.9 %copy.49 = bf16[1,256,7168]{2,1,0:T(8,128)(2,1)} copy(bf16[1,256,7168]{1,2,0:T(8,128)(2,1)} %bitcast.24) | data formatting | bytes 7340032
  (5 shorter events, 0.0 us)
Async XLA Ops:
  1.9 18.5 %all-to-all-start = ((s32[16,1,8]{2,1,0:T(1,128)}), s32[16,1,8]{2,1,0:T(1,128)S(1)}, u32[]{:S(2)}, u32[]{:S(2)}) async-start(s32[16,1,8]{2,1,0:T(1,128)} %broadcast_in_dim.60), calls=%async_computation | async-start | bytes 16384 | tf_op jit(solution)/shard_map/all_to_all | solution.py:207
  20.4 52.7 %all-to-all-start.1 = ((bf16[8,2,16,2,3584]{4,3,1,0,2:T(2,128)(2,1)}), bf16[8,2,16,2,3584]{4,3,1,0,2:T(2,128)(2,1)}, u32[]{:S(2)}, u32[]{:S(2)}) async-start(bf16[8,2,16,2,3584]{4,3,1,0,2:T(2,128)(2,1)} %copy.43), calls=%async_computation.1 | async-start | bytes 7340032 | tf_op jit(solution)/shard_map/all_to_all | solution.py:176
  73.1 129.7 %all-to-all-start.2 = ((bf16[256,16,3,448]{0,3,2,1:T(8,128)(2,1)}), bf16[256,16,3,448]{0,3,2,1:T(8,128)(2,1)}, u32[]{:S(2)}, u32[]{:S(2)}) async-start(bf16[256,16,3,448]{0,3,2,1:T(8,128)(2,1)} %maximum_bitcast_fusion), calls=%async_computation.2 | async-start | bytes 22020096 | tf_op jit(solution)/shard_map/all_to_all | solution.py:160
  202.8 5.2 %copy-start.1 = (s32[1,6]{1,0:T(1,128)S(1)}, s32[1,6]{1,0:T(1,128)}, u32[]{:S(2)}) copy-start(s32[1,6]{1,0:T(1,128)} %param.9) | copy-start | bytes 76
  202.8 87.7 %all-to-all-start.3 = ((bf16[8,2,2,16,2,3584]{5,3,4,2,1,0:T(8,128)(2,1)}), bf16[8,2,2,16,2,3584]{5,3,4,2,1,0:T(8,128)(2,1)}, u32[]{:S(2)}, u32[]{:S(2)}) async-start(bf16[8,2,2,16,2,3584]{5,3,4,2,1,0:T(8,128)(2,1)} %select_reduce_fusion), calls=%async_computation.3 | async-start | bytes 14680064 | tf_op jit(solution)/shard_map/all_to_all | solution.py:198
  208.3 3.4 copy-start
  208.4 3.3 copy-start.2
  290.5 50.5 %all-to-all-start.4 = ((bf16[256,16,448]{0,2,1:T(8,128)(2,1)}), bf16[256,16,448]{0,2,1:T(8,128)(2,1)}, u32[]{:S(2)}, u32[]{:S(2)}) async-start(bf16[256,16,448]{0,2,1:T(8,128)(2,1)} %bitcast.40), calls=%async_computation.4 | async-start | bytes 7340032 | tf_op jit(solution)/shard_map/all_to_all | solution.py:167
